TPU v7x, 512 devices: a whole 4x4x16 slice. The times are simulated.
512 devices in a mesh: dp: 4 (over y), cam: 32 (over x, z_lo), slab: 4 (over z_hi, core).
Axes of the slice: x: 4, y: 4, z: 16 (z_hi: 2, z_lo: 8; z = z_hi * 8 + z_lo), core: 2. Of those that a mesh axis runs over, the one named last changes fastest.
Arguments:
- image: bfloat16 [128, 16, 256, 128], P(('dp', 'cam'), 'slab'), parts along dimension 0, may hold values from -6 to 6
- w_first: bfloat16 [3, 3, 128, 128], replicated, may hold values from -0.1875 to 0.1875
- w_second: bfloat16 [3, 3, 128, 128], replicated, may hold values from -0.1875 to 0.1875
- w_reduce: bfloat16 [128, 32], replicated, may hold values from -0.5 to 0.5
- cam_weight: float32 [32], P('cam'), may hold values from 0.3 to 3
- sample_pixel: int32 [512, 128, 32], P(('dp', 'cam', 'slab')), parts along dimension 0, may hold values from 0 to 1022, as said below
- sample_frac: float32 [512, 2, 128, 32], P(('dp', 'cam', 'slab')), parts along dimension 0, may hold values from 0 to 1
- voxel_slot: int32 [512, 128, 32], P(('dp', 'cam', 'slab')), parts along dimension 0, may hold values from 0 to 1024, as said below
- wv_first: bfloat16 [27, 32, 32], replicated, may hold values from -0.21875 to 0.21875
- wv_second: bfloat16 [27, 32, 32], replicated, may hold values from -0.21875 to 0.21875
Outputs:
- volume_out: bfloat16 [32, 256, 2048], P(None, ('dp', 'cam'), 'slab'), parts along dimension 1
There are 4 independent parts, one for each index of `dp`. A program takes and returns all parts, laid end to end along the dimension named above; an argument that names none is the same for every part. Nothing has to cross between parts.
Inputs may be any that keep to these rules, and one draw needn't show every extreme that they name: `sample_pixel`: row * 256 + column of a pixel within the source's 4 rows; the column is at most 254. `voxel_slot`: 1024 marks an empty slot; at most 32 filled slots from one source to one owner, and in every draw some owner receives 32 filled slots from every source.
All inputs are finite; a program needn't handle non-finite values.
Results may differ from a plain program's by a relative error of at most 0.0075.
Values may be sent and summed in bfloat16 or wider, within the bound.
No kernel may reach another device: no remote copies, remote signals or barrier semaphores. Data moves between devices by JAX's collectives and lax.ppermute only.
A program may use at most 64 MiB of HBM per device.

v0:
```python
import math

import jax
import jax.numpy as jnp
from jax import lax
from jax.sharding import PartitionSpec as P

BX = 2
BY = 8
VZ = 64


def padded_2(block, sides, width):
    for axis, dim in sides:
        count = lax.axis_size(axis)
        forward = [(i, i + 1) for i in range(count - 1)]
        backward = [(target, source) for source, target in forward]
        low = lax.ppermute(
            lax.slice_in_dim(block, block.shape[dim] - width, None, axis=dim), axis, forward
        )
        high = lax.ppermute(lax.slice_in_dim(block, 0, width, axis=dim), axis, backward)
        block = jnp.concatenate([low, block, high], axis=dim)
    return block


def from_behind(array, axis, by):
    length = lax.axis_size(axis)
    pairs = [(i, i + by) for i in range(length) if 0 <= i + by < length]
    return lax.ppermute(array, axis, pairs)


def image_conv(padded, weight, row_count, col_count):
    running = jnp.zeros((row_count * col_count, weight.shape[3]), jnp.float32)
    for row_off in range(3):
        for col_off in range(3):
            window = padded[row_off : row_off + row_count, col_off : col_off + col_count, :]
            window = window.reshape(row_count * col_count, weight.shape[2])
            running = running + jnp.dot(
                window, weight[row_off, col_off], preferred_element_type=jnp.float32
            )
    return running


def bilinear(table, pixel, frac_row, frac_col, col_count, scale):
    top_left = jnp.take(table, pixel, axis=1).astype(jnp.float32)
    top_right = jnp.take(table, pixel + 1, axis=1).astype(jnp.float32)
    low_left = jnp.take(table, pixel + col_count, axis=1).astype(jnp.float32)
    low_right = jnp.take(table, pixel + col_count + 1, axis=1).astype(jnp.float32)
    upper = (1.0 - frac_col) * top_left + frac_col * top_right
    lower = (1.0 - frac_col) * low_left + frac_col * low_right
    return ((1.0 - frac_row) * upper + frac_row * lower) * scale


def volume_conv(volume, weight):
    channels, planes, flat_len = volume.shape
    by_planes = padded_2(volume, (("cam", 1),), 1)
    extended = padded_2(by_planes, (("slab", 2),), VZ)
    depth_pos = lax.broadcasted_iota(jnp.int32, (1, 1, flat_len), 2) % VZ
    running = jnp.zeros((channels, planes * flat_len), jnp.float32)
    for plane_off in range(3):
        for row_off in range(3):
            window = extended[
                :, plane_off : plane_off + planes, row_off * VZ : row_off * VZ + flat_len
            ]
            padded = jnp.pad(window, ((0, 0), (0, 0), (1, 1)))
            for depth_off in range(3):
                moved = padded[:, :, depth_off : depth_off + flat_len]
                target = depth_pos + (depth_off - 1)
                inside = ((target >= 0) & (target < VZ)).astype(jnp.bfloat16)
                running = running + jnp.dot(
                    weight[(plane_off * 3 + row_off) * 3 + depth_off],
                    (moved * inside).reshape(channels, planes * flat_len),
                    preferred_element_type=jnp.float32,
                )
    return running


def local(
    image,
    w_first,
    w_second,
    w_reduce,
    cam_weight,
    sample_pixel,
    sample_frac,
    voxel_slot,
    wv_first,
    wv_second,
):
    frame_view = image[0]
    row_count, col_count, width = frame_view.shape
    channels = w_reduce.shape[1]
    extended = padded_2(frame_view, (("slab", 0),), 1)
    padded = jnp.pad(extended, ((0, 0), (1, 1), (0, 0)))
    hidden = jax.nn.relu(image_conv(padded, w_first, row_count, col_count)).astype(jnp.bfloat16)
    hidden = hidden.reshape(row_count, col_count, width)
    hidden_ext = padded_2(hidden, (("slab", 0),), 1)
    padded_hidden = jnp.pad(hidden_ext, ((0, 0), (1, 1), (0, 0)))
    second = jax.nn.relu(image_conv(padded_hidden, w_second, row_count, col_count)).astype(
        jnp.bfloat16
    )
    reduced = lax.dot_general(
        w_reduce, second, (((0,), (1,)), ((), ())), preferred_element_type=jnp.float32
    ).astype(jnp.bfloat16)
    below = from_behind(reduced[:, :col_count], "slab", -1)
    table = jnp.concatenate([reduced, below], axis=1)
    owners = sample_pixel.shape[1]
    capacity = sample_pixel.shape[2]
    pixel = sample_pixel[0].reshape(-1)
    fracs = sample_frac[0]
    values = bilinear(
        table, pixel, fracs[0].reshape(-1), fracs[1].reshape(-1), col_count, cam_weight[0]
    )
    outgoing = values.astype(jnp.bfloat16).reshape(channels, owners, capacity)
    arrived = lax.all_to_all(outgoing, ("cam", "slab"), split_axis=1, concat_axis=1, tiled=True)
    arrived = arrived.reshape(channels, owners * capacity)
    slot_ids = voxel_slot[0].reshape(-1)
    slot_total = slot_ids.shape[0]
    block_len = math.gcd(slot_total, 2048)
    voxel_count = BX * BY * VZ
    voxel_iota = lax.broadcasted_iota(jnp.int32, (block_len, voxel_count), 1)

    def add_block(counter, running):
        offset = counter * block_len
        block_vals = lax.dynamic_slice_in_dim(arrived, offset, block_len, 1)
        block_ids = lax.dynamic_slice_in_dim(slot_ids, offset, block_len, 0)
        one_hot = (block_ids[:, None] == voxel_iota).astype(jnp.bfloat16)
        return running + jnp.dot(block_vals, one_hot, preferred_element_type=jnp.float32)

    summed = lax.fori_loop(
        0, slot_total // block_len, add_block, jnp.zeros((channels, voxel_count), jnp.float32)
    )
    volume = summed.astype(jnp.bfloat16).reshape(channels, BX, BY * VZ)
    vfirst = (
        jax.nn.relu(volume_conv(volume, wv_first))
        .astype(jnp.bfloat16)
        .reshape(channels, BX, BY * VZ)
    )
    result = volume_conv(vfirst, wv_second) + volume.reshape(channels, voxel_count).astype(
        jnp.float32
    )
    return result.astype(jnp.bfloat16).reshape(channels, BX, BY * VZ)


def solution(mesh):
    placed = (
        P(("dp", "cam"), "slab", None, None),
        P(),
        P(),
        P(),
        P("cam"),
        P(("dp", "cam", "slab"), None, None),
        P(("dp", "cam", "slab"), None, None, None),
        P(("dp", "cam", "slab"), None, None),
        P(),
        P(),
    )
    return jax.shard_map(
        local, mesh=mesh, in_specs=placed, out_specs=P(None, ("dp", "cam"), "slab"), check_vma=False
    )
```

profile of v0, /device:TPU:3, one launch (start us, length us, event | category | flops | bytes accessed | tf_op | source)
XLA Modules:
  0.0 256.8 jit_solution(13834076076258123117)
XLA Ops:
  0.0 0.9 slice_bitcast_fusion.3
  0.9 16.0 %collective-permute-start = (bf16[1,256,128]{2,1,0:T(8,128)(2,1)S(1)}, bf16[1,256,128]{2,1,0:T(8,128)(2,1)S(1)}, u32[]{:S(2)}, u32[]{:S(2)}) collective-permute-start(bf16[1,256,128]{2,1,0:T(8,128)(2,1)S(1)} %get-tuple-element.152), channel_id=1, source_target_pairs={{0,1},{1,2},{2,3},{4,5},{5,6},{6,7},{8,9},{9,10},{10,11},{12,13},{... | collective-permute-start | bytes 196616 | tf_op jit(solution)/shard_map/ppermute | solution.py:18
  16.9 1.9 collective-permute-start.1
  18.9 0.8 copy.51
  19.8 0.7 fusion.223
  20.9 10.3 %collective-permute-done.1 = bf16[1,256,128]{2,1,0:T(8,128)(2,1)S(1)} collective-permute-done((bf16[1,256,128]{2,1,0:T(8,128)(2,1)S(1)}, bf16[1,256,128]{2,1,0:T(8,128)(2,1)S(1)}, u32[]{:S(2)}, u32[]{:S(2)}) %collective-permute-start.1) | collective-permute-done | bytes 65568 | tf_op jit(solution)/shard_map/ppermute | solution.py:21
  31.7 0.7 copy-done.2
  34.4 2.0 collective-permute-start.2
  36.4 2.3 collective-permute-start.3
  38.7 12.0 %collective-permute-done.3 = bf16[1,256,128]{2,1,0:T(8,128)(2,1)S(1)} collective-permute-done((bf16[1,256,128]{2,1,0:T(8,128)(2,1)S(1)}, bf16[1,256,128]{2,1,0:T(8,128)(2,1)S(1)}, u32[]{:S(2)}, u32[]{:S(2)}) %collective-permute-start.3) | collective-permute-done | bytes 65568 | tf_op jit(solution)/shard_map/ppermute | solution.py:21
  50.8 0.3 fusion.219
  51.1 0.7 copy-done.3
  53.5 0.4 fusion.41
  53.9 1.9 collective-permute-start.4
  56.6 11.2 %collective-permute-done.4 = bf16[32,256]{1,0:T(8,128)(2,1)S(1)} collective-permute-done((bf16[32,256]{1,0:T(8,128)(2,1)S(1)}, bf16[32,256]{1,0:T(8,128)(2,1)S(1)}, u32[]{:S(2)}, u32[]{:S(2)}) %collective-permute-start.4) | collective-permute-done | bytes 16416 | tf_op jit(solution)/shard_map/ppermute | solution.py:29
  67.9 12.1 %gather_fusion = bf16[4096,32]{1,0:T(8,128)(2,1)S(1)} fusion(bf16[32,1280]{0,1:T(8,128)(2,1)S(1)} %copy.52, s32[4096]{0:T(1024)S(1)} %get-tuple-element.236), kind=kCustom, calls=%fused_computation.clone | custom fusion | bytes 540672 | tf_op jit(solution)/shard_map/jit(_take)/gather | solution.py:45
  80.1 0.3 copy.53
  80.4 12.1 %gather_fusion.1 = bf16[4096,32]{1,0:T(8,128)(2,1)S(1)} fusion(bf16[32,1280]{0,1:T(8,128)(2,1)S(1)} %copy.52, s32[4096]{0:T(1024)S(1)} %get-tuple-element.237), kind=kCustom, calls=%fused_computation.1.clone | custom fusion | bytes 540672 | tf_op jit(solution)/shard_map/jit(_take)/gather | solution.py:46
  92.6 0.3 copy.55
  92.9 12.1 %gather_fusion.2 = bf16[4096,32]{1,0:T(8,128)(2,1)S(1)} fusion(bf16[32,1280]{0,1:T(8,128)(2,1)S(1)} %copy.52, s32[4096]{0:T(1024)S(1)} %get-tuple-element.238), kind=kCustom, calls=%fused_computation.2.clone | custom fusion | bytes 540672 | tf_op jit(solution)/shard_map/jit(_take)/gather | solution.py:47
  105.0 0.3 copy.57
  105.4 12.1 %gather_fusion.3 = bf16[4096,32]{1,0:T(8,128)(2,1)S(1)} fusion(bf16[32,1280]{0,1:T(8,128)(2,1)S(1)} %copy.52, s32[4096]{0:T(1024)S(1)} %get-tuple-element.239), kind=kCustom, calls=%fused_computation.3.clone | custom fusion | bytes 540672 | tf_op jit(solution)/shard_map/jit(_take)/gather | solution.py:48
  117.5 0.3 copy.59
  117.8 0.4 multiply_convert_fusion
  118.2 0.8 reshape.323
  119.0 0.7 copy.117
  119.7 1.5 reshape.424
  121.2 9.3 %all-to-all-start = ((bf16[128,2,512]{2,1,0:T(2,128)(2,1)}), bf16[128,2,512]{2,1,0:T(2,128)(2,1)S(1)}, u32[]{:S(2)}, u32[]{:S(2)}) async-start(bf16[128,2,512]{2,1,0:T(2,128)(2,1)} %reshape.424), calls=%async_computation | async-start | bytes 524288 | tf_op jit(solution)/shard_map/all_to_all | solution.py:115
  130.7 19.7 %all-to-all-done = bf16[128,2,512]{2,1,0:T(2,128)(2,1)S(1)} async-done(((bf16[128,2,512]{2,1,0:T(2,128)(2,1)}), bf16[128,2,512]{2,1,0:T(2,128)(2,1)S(1)}, u32[]{:S(2)}, u32[]{:S(2)}) %all-to-all-start) | async-done | bytes 262176 | tf_op jit(solution)/shard_map/all_to_all | solution.py:115
  150.5 0.5 reshape.425
  151.0 0.4 copy.61
  151.4 1.2 reshape.324
  152.6 3.4 %while.14 = (s32[]{:T(128)}, f32[32,1024]{1,0:T(8,128)S(1)}, bf16[32,4096]{1,0:T(8,128)(2,1)S(1)}, s32[4096]{0:T(1024)S(1)}, s32[]{:T(128)}, /*index=5*/s32[]{:T(128)}, s32[]{:T(128)}, s32[]{:T(128)}) while((s32[]{:T(128)}, f32[32,1024]{1,0:T(8,128)S(1)}, bf16[32,4096]{1,0:T(8,128)(2,1)S(1)}, s32[4096]{0:T(1024)S(1)}, s32[]{:T(128)}, ...), condition=%wide.region_1.3_spmd.clone, body=%wide.region_0.2_spmd.clone.sunk | while | flops 136380416 | bytes 417941 | solution.py:130
  152.6 1.7 fusion.298
  154.3 1.7 fusion.298
  156.2 5.3 %collective-permute-start.5 = (bf16[32,1,512]{2,1,0:T(2,128)(2,1)S(1)}, bf16[32,1,512]{2,1,0:T(2,128)(2,1)S(1)}, u32[]{:S(2)}, u32[]{:S(2)}) collective-permute-start(bf16[32,1,512]{2,1,0:T(2,128)(2,1)S(1)} %get-tuple-element.228), channel_id=1, source_target_pairs={{0,4},{4,8},{8,12},{12,16},{16,20},{20,24},{24,28},{28,32},{32,36}... | collective-permute-start | bytes 98312 | tf_op jit(solution)/shard_map/ppermute | solution.py:18
  161.5 7.5 %collective-permute-start.6 = (bf16[32,1,512]{2,1,0:T(2,128)(2,1)S(1)}, bf16[32,1,512]{2,1,0:T(2,128)(2,1)S(1)}, u32[]{:S(2)}, u32[]{:S(2)}) collective-permute-start(bf16[32,1,512]{2,1,0:T(2,128)(2,1)S(1)} %get-tuple-element.229), channel_id=1, source_target_pairs={{4,0},{8,4},{12,8},{16,12},{20,16},{24,20},{28,24},{32,28},{36,32}... | collective-permute-start | bytes 98312 | tf_op jit(solution)/shard_map/ppermute | solution.py:21
  169.0 1.3 collective-permute-done.6
  170.4 7.3 %collective-permute-start.7 = (bf16[32,4,64]{2,1,0:T(4,128)(2,1)S(1)}, bf16[32,4,64]{2,1,0:T(4,128)(2,1)S(1)}, u32[]{:S(2)}, u32[]{:S(2)}) collective-permute-start(bf16[32,4,64]{2,1,0:T(4,128)(2,1)S(1)} %get-tuple-element.160), channel_id=1, source_target_pairs={{0,1},{1,2},{2,3},{4,5},{5,6},{6,7},{8,9},{9,10},{10,11},{12,13},{... | collective-permute-start | bytes 49160 | tf_op jit(solution)/shard_map/ppermute | solution.py:18
  177.7 1.9 collective-permute-start.8
  179.7 12.0 %collective-permute-done.8 = bf16[32,4,64]{2,1,0:T(4,128)(2,1)S(1)} collective-permute-done((bf16[32,4,64]{2,1,0:T(4,128)(2,1)S(1)}, bf16[32,4,64]{2,1,0:T(4,128)(2,1)S(1)}, u32[]{:S(2)}, u32[]{:S(2)}) %collective-permute-start.8) | collective-permute-done | bytes 16416 | tf_op jit(solution)/shard_map/ppermute | solution.py:21
  191.7 0.8 maximum_maximum_fusion
  192.4 0.3 broadcast_multiply_fusion.12
  192.8 1.1 broadcast_multiply_fusion.14
  193.9 2.0 slice_multiply_fusion.19
  196.2 0.6 copy-done.4
  201.2 11.5 %collective-permute-start.10 = (bf16[32,1,512]{2,1,0:T(2,128)(2,1)S(1)}, bf16[32,1,512]{2,1,0:T(2,128)(2,1)S(1)}, u32[]{:S(2)}, u32[]{:S(2)}) collective-permute-start(bf16[32,1,512]{2,1,0:T(2,128)(2,1)S(1)} %get-tuple-element.209), channel_id=1, source_target_pairs={{4,0},{8,4},{12,8},{16,12},{20,16},{24,20},{28,24},{32,28},{36,32}... | collective-permute-start | bytes 98312 | tf_op jit(solution)/shard_map/ppermute | solution.py:21
  212.7 1.9 collective-permute-start.9
  214.6 10.6 %collective-permute-done.9 = bf16[32,1,512]{2,1,0:T(2,128)(2,1)S(1)} collective-permute-done((bf16[32,1,512]{2,1,0:T(2,128)(2,1)S(1)}, bf16[32,1,512]{2,1,0:T(2,128)(2,1)S(1)}, u32[]{:S(2)}, u32[]{:S(2)}) %collective-permute-start.9) | collective-permute-done | bytes 32800 | tf_op jit(solution)/shard_map/ppermute | solution.py:18
  225.3 3.3 %collective-permute-start.11 = (bf16[32,4,64]{2,1,0:T(4,128)(2,1)S(1)}, bf16[32,4,64]{2,1,0:T(4,128)(2,1)S(1)}, u32[]{:S(2)}, u32[]{:S(2)}) collective-permute-start(bf16[32,4,64]{2,1,0:T(4,128)(2,1)S(1)} %get-tuple-element.156), channel_id=1, source_target_pairs={{0,1},{1,2},{2,3},{4,5},{5,6},{6,7},{8,9},{9,10},{10,11},{12,13},{... | collective-permute-start | bytes 49160 | tf_op jit(solution)/shard_map/ppermute | solution.py:18
  228.7 2.1 collective-permute-start.12
  230.8 11.8 %collective-permute-done.12 = bf16[32,4,64]{2,1,0:T(4,128)(2,1)S(1)} collective-permute-done((bf16[32,4,64]{2,1,0:T(4,128)(2,1)S(1)}, bf16[32,4,64]{2,1,0:T(4,128)(2,1)S(1)}, u32[]{:S(2)}, u32[]{:S(2)}) %collective-permute-start.12) | collective-permute-done | bytes 16416 | tf_op jit(solution)/shard_map/ppermute | solution.py:21
  242.6 0.8 maximum_maximum_fusion.1
  243.4 0.3 broadcast_multiply_fusion.4
  243.7 1.1 broadcast_multiply_fusion.6
  244.8 2.0 slice_multiply_fusion.1
  247.1 0.7 copy-done.5
  249.9 0.8 convolution_bitcast_fusion
  250.8 0.8 convolution_bitcast_fusion.2
  251.6 0.8 convolution_bitcast_fusion.3
  252.5 0.8 convolution_bitcast_fusion.5
  253.3 0.8 convolution_bitcast_fusion.6
  254.2 0.8 convolution_bitcast_fusion.8
  256.2 0.7 reshape.379
  (166 shorter events, 13.4 us)
Async XLA Ops:
  0.0 53.5 %copy-start = (bf16[128,32]{0,1:T(8,128)(2,1)S(1)}, bf16[128,32]{0,1:T(8,128)(2,1)}, u32[]{:S(2)}) copy-start(bf16[128,32]{0,1:T(8,128)(2,1)} %param.17) | copy-start | bytes 24580
  0.0 31.2 %copy-start.1 = (bf16[1,4,256,128]{3,2,1,0:T(8,128)(2,1)S(1)}, bf16[1,4,256,128]{3,2,1,0:T(8,128)(2,1)}, u32[]{:S(2)}) copy-start(bf16[1,4,256,128]{3,2,1,0:T(8,128)(2,1)} %param.14) | copy-start | bytes 786436
  0.9 20.0 %collective-permute-start = (bf16[1,256,128]{2,1,0:T(8,128)(2,1)S(1)}, bf16[1,256,128]{2,1,0:T(8,128)(2,1)S(1)}, u32[]{:S(2)}, u32[]{:S(2)}) collective-permute-start(bf16[1,256,128]{2,1,0:T(8,128)(2,1)S(1)} %get-tuple-element.152), channel_id=1, source_target_pairs={{0,1},{1,2},{2,3},{4,5},{5,6},{6,7},{8,9},{9,10},{10,11},{12,13},{... | collective-permute-start | bytes 196616 | tf_op jit(solution)/shard_map/ppermute | solution.py:18
  16.9 14.3 %collective-permute-start.1 = (bf16[1,256,128]{2,1,0:T(8,128)(2,1)S(1)}, bf16[1,256,128]{2,1,0:T(8,128)(2,1)S(1)}, u32[]{:S(2)}, u32[]{:S(2)}) collective-permute-start(bf16[1,256,128]{2,1,0:T(8,128)(2,1)S(1)} %get-tuple-element.153), channel_id=1, source_target_pairs={{1,0},{2,1},{3,2},{5,4},{6,5},{7,6},{9,8},{10,9},{11,10},{13,12},{... | collective-permute-start | bytes 196616 | tf_op jit(solution)/shard_map/ppermute | solution.py:21
  31.4 1.0 copy-start.2
  34.4 4.4 %collective-permute-start.2 = (bf16[1,256,128]{2,1,0:T(8,128)(2,1)S(1)}, bf16[1,256,128]{2,1,0:T(8,128)(2,1)S(1)}, u32[]{:S(2)}, u32[]{:S(2)}) collective-permute-start(bf16[1,256,128]{2,1,0:T(8,128)(2,1)S(1)} %get-tuple-element.148), channel_id=1, source_target_pairs={{0,1},{1,2},{2,3},{4,5},{5,6},{6,7},{8,9},{9,10},{10,11},{12,13},{... | collective-permute-start | bytes 196616 | tf_op jit(solution)/shard_map/ppermute | solution.py:18
  36.4 14.3 %collective-permute-start.3 = (bf16[1,256,128]{2,1,0:T(8,128)(2,1)S(1)}, bf16[1,256,128]{2,1,0:T(8,128)(2,1)S(1)}, u32[]{:S(2)}, u32[]{:S(2)}) collective-permute-start(bf16[1,256,128]{2,1,0:T(8,128)(2,1)S(1)} %get-tuple-element.149), channel_id=1, source_target_pairs={{1,0},{2,1},{3,2},{5,4},{6,5},{7,6},{9,8},{10,9},{11,10},{13,12},{... | collective-permute-start | bytes 196616 | tf_op jit(solution)/shard_map/ppermute | solution.py:21
  50.8 1.0 copy-start.3
  53.9 13.8 %collective-permute-start.4 = (bf16[32,256]{1,0:T(8,128)(2,1)S(1)}, bf16[32,256]{1,0:T(8,128)(2,1)S(1)}, u32[]{:S(2)}, u32[]{:S(2)}) collective-permute-start(bf16[32,256]{1,0:T(8,128)(2,1)S(1)} %slice.706), channel_id=1, source_target_pairs={{1,0},{2,1},{3,2},{5,4},{6,5},{7,6},{9,8},{10,9},{11,10},{13,12},{... | collective-permute-start | bytes 49160 | tf_op jit(solution)/shard_map/ppermute | solution.py:29
  119.7 10.8 %copy-start.6 = (s32[1,128,32]{1,2,0:T(8,128)S(1)}, s32[1,128,32]{1,2,0:T(8,128)}, u32[]{:S(2)}) copy-start(s32[1,128,32]{1,2,0:T(8,128)} %param.21) | copy-start | bytes 49156
  121.2 29.2 %all-to-all-start = ((bf16[128,2,512]{2,1,0:T(2,128)(2,1)}), bf16[128,2,512]{2,1,0:T(2,128)(2,1)S(1)}, u32[]{:S(2)}, u32[]{:S(2)}) async-start(bf16[128,2,512]{2,1,0:T(2,128)(2,1)} %reshape.424), calls=%async_computation | async-start | bytes 524288 | tf_op jit(solution)/shard_map/all_to_all | solution.py:115
  156.2 12.8 %collective-permute-start.5 = (bf16[32,1,512]{2,1,0:T(2,128)(2,1)S(1)}, bf16[32,1,512]{2,1,0:T(2,128)(2,1)S(1)}, u32[]{:S(2)}, u32[]{:S(2)}) collective-permute-start(bf16[32,1,512]{2,1,0:T(2,128)(2,1)S(1)} %get-tuple-element.228), channel_id=1, source_target_pairs={{0,4},{4,8},{8,12},{12,16},{16,20},{20,24},{24,28},{28,32},{32,36}... | collective-permute-start | bytes 98312 | tf_op jit(solution)/shard_map/ppermute | solution.py:18
  161.5 8.8 %collective-permute-start.6 = (bf16[32,1,512]{2,1,0:T(2,128)(2,1)S(1)}, bf16[32,1,512]{2,1,0:T(2,128)(2,1)S(1)}, u32[]{:S(2)}, u32[]{:S(2)}) collective-permute-start(bf16[32,1,512]{2,1,0:T(2,128)(2,1)S(1)} %get-tuple-element.229), channel_id=1, source_target_pairs={{4,0},{8,4},{12,8},{16,12},{20,16},{24,20},{28,24},{32,28},{36,32}... | collective-permute-start | bytes 98312 | tf_op jit(solution)/shard_map/ppermute | solution.py:21
  170.4 9.3 %collective-permute-start.7 = (bf16[32,4,64]{2,1,0:T(4,128)(2,1)S(1)}, bf16[32,4,64]{2,1,0:T(4,128)(2,1)S(1)}, u32[]{:S(2)}, u32[]{:S(2)}) collective-permute-start(bf16[32,4,64]{2,1,0:T(4,128)(2,1)S(1)} %get-tuple-element.160), channel_id=1, source_target_pairs={{0,1},{1,2},{2,3},{4,5},{5,6},{6,7},{8,9},{9,10},{10,11},{12,13},{... | collective-permute-start | bytes 49160 | tf_op jit(solution)/shard_map/ppermute | solution.py:18
  177.7 13.9 %collective-permute-start.8 = (bf16[32,4,64]{2,1,0:T(4,128)(2,1)S(1)}, bf16[32,4,64]{2,1,0:T(4,128)(2,1)S(1)}, u32[]{:S(2)}, u32[]{:S(2)}) collective-permute-start(bf16[32,4,64]{2,1,0:T(4,128)(2,1)S(1)} %get-tuple-element.161), channel_id=1, source_target_pairs={{1,0},{2,1},{3,2},{5,4},{6,5},{7,6},{9,8},{10,9},{11,10},{13,12},{... | collective-permute-start | bytes 49160 | tf_op jit(solution)/shard_map/ppermute | solution.py:21
  195.9 0.9 copy-start.4
  201.2 13.4 %collective-permute-start.10 = (bf16[32,1,512]{2,1,0:T(2,128)(2,1)S(1)}, bf16[32,1,512]{2,1,0:T(2,128)(2,1)S(1)}, u32[]{:S(2)}, u32[]{:S(2)}) collective-permute-start(bf16[32,1,512]{2,1,0:T(2,128)(2,1)S(1)} %get-tuple-element.209), channel_id=1, source_target_pairs={{4,0},{8,4},{12,8},{16,12},{20,16},{24,20},{28,24},{32,28},{36,32}... | collective-permute-start | bytes 98312 | tf_op jit(solution)/shard_map/ppermute | solution.py:21
  212.7 12.5 %collective-permute-start.9 = (bf16[32,1,512]{2,1,0:T(2,128)(2,1)S(1)}, bf16[32,1,512]{2,1,0:T(2,128)(2,1)S(1)}, u32[]{:S(2)}, u32[]{:S(2)}) collective-permute-start(bf16[32,1,512]{2,1,0:T(2,128)(2,1)S(1)} %get-tuple-element.208), channel_id=1, source_target_pairs={{0,4},{4,8},{8,12},{12,16},{16,20},{20,24},{24,28},{28,32},{32,36}... | collective-permute-start | bytes 98312 | tf_op jit(solution)/shard_map/ppermute | solution.py:18
  225.3 5.5 %collective-permute-start.11 = (bf16[32,4,64]{2,1,0:T(4,128)(2,1)S(1)}, bf16[32,4,64]{2,1,0:T(4,128)(2,1)S(1)}, u32[]{:S(2)}, u32[]{:S(2)}) collective-permute-start(bf16[32,4,64]{2,1,0:T(4,128)(2,1)S(1)} %get-tuple-element.156), channel_id=1, source_target_pairs={{0,1},{1,2},{2,3},{4,5},{5,6},{6,7},{8,9},{9,10},{10,11},{12,13},{... | collective-permute-start | bytes 49160 | tf_op jit(solution)/shard_map/ppermute | solution.py:18
  228.7 13.9 %collective-permute-start.12 = (bf16[32,4,64]{2,1,0:T(4,128)(2,1)S(1)}, bf16[32,4,64]{2,1,0:T(4,128)(2,1)S(1)}, u32[]{:S(2)}, u32[]{:S(2)}) collective-permute-start(bf16[32,4,64]{2,1,0:T(4,128)(2,1)S(1)} %get-tuple-element.157), channel_id=1, source_target_pairs={{1,0},{2,1},{3,2},{5,4},{6,5},{7,6},{9,8},{10,9},{11,10},{13,12},{... | collective-permute-start | bytes 49160 | tf_op jit(solution)/shard_map/ppermute | solution.py:21
  246.8 0.9 copy-start.5
where the time goes:
time: 258 us; the launch traced here: 257 us
  waiting for transfers between devices  88.8 us (34%)
  starting transfers between devices  74.3 us (29%)
  local copies, waits for them, and re-layouts  63.1 us (24%)
  matrix products  19.4 us (8%)
  other arithmetic  9.4 us (4%)
    ppermute x6, waiting for transfers between devices, padded_2(): lax.ppermute(lax.slice_in_dim(block, 0, width, axis=dim), axis, backward)  47.3 us
    ppermute x6, starting transfers between devices, padded_2(): lax.ppermute(lax.slice_in_dim(block, block.shape[dim] - width, None, axis...  35.9 us
    ppermute x6, starting transfers between devices, padded_2(): lax.ppermute(lax.slice_in_dim(block, 0, width, axis=dim), axis, backward)  27.3 us
    all_to_all x1, waiting for transfers between devices, local(): lax.all_to_all(outgoing, ('cam', 'slab'), split_axis=1, concat_axis=1, ti...  19.7 us
    gather x2, local copies, waits for them, and re-layouts, bilinear(): top_left = jnp.take(table, pixel, axis=1).astype(jnp.float32)  12.5 us
    gather x2, local copies, waits for them, and re-layouts, bilinear(): low_left = jnp.take(table, pixel + col_count, axis=1).astype(jnp.float32)  12.5 us
    gather x2, local copies, waits for them, and re-layouts, bilinear(): top_right = jnp.take(table, pixel + 1, axis=1).astype(jnp.float32)  12.5 us
    gather x2, local copies, waits for them, and re-layouts, bilinear(): jnp.take(table, pixel + col_count + 1, axis=1).astype(jnp.float32)  12.5 us
  transfers between devices with their start and end apart: 14, of which 8 were waited for; matrix products, arithmetic and copies ran while one was open for 1% of the time, Pallas kernels for 0%

commit v1 on v0

v1 whole, which is shorter than its diff:
```python
import jax
import jax.numpy as jnp
from jax import lax
from jax.experimental import pallas as pl
from jax.experimental.pallas import tpu as pltpu
from jax.sharding import PartitionSpec as P

AXES = ("cam", "slab")
F32 = jnp.float32
BF16 = jnp.bfloat16


def dot(a, b):
    return jnp.dot(a, b, preferred_element_type=F32)


def dot_nt(a, b):
    return lax.dot_general(a, b, (((1,), (1,)), ((), ())), preferred_element_type=F32)


def whole(memory_space):
    return pl.BlockSpec(memory_space=memory_space)


def put_columns(dst, row, x):
    cols = x.shape[0]
    pos = lax.broadcasted_iota(jnp.int32, x.shape, 0)
    left = jnp.where(pos == 0, 0.0, pltpu.roll(x, 1, 0))
    right = jnp.where(pos == cols - 1, 0.0, pltpu.roll(x, cols - 1, 0))
    dst[row, :, 0:128] = left.astype(BF16)
    dst[row, :, 128:256] = x.astype(BF16)
    dst[row, :, 256:384] = right.astype(BF16)


def features_kernel(
    pos_ref,
    scale_ref,
    img_ref,
    far_ref,
    core_ref,
    w1_ref,
    w2_ref,
    wr_ref,
    pix_ref,
    frac_ref,
    out_ref,
    x1,
    x2,
    acc,
    packed,
):
    slab = pos_ref[0]
    even = (1 - slab % 2).astype(F32)
    odd = 1.0 - even
    not_first = jnp.where(slab == 0, 0.0, 1.0)
    not_last = jnp.where(slab == 3, 0.0, 1.0)
    for i in range(2):
        row = even * far_ref[1 + i].astype(F32) + odd * core_ref[1 + i].astype(F32)
        put_columns(x1, i, row)
    for i in range(4):
        put_columns(x1, 2 + i, img_ref[i].astype(F32))
    for i in range(3):
        row = even * core_ref[i].astype(F32) + odd * far_ref[i].astype(F32)
        put_columns(x1, 6 + i, row)
    acc[...] = dot(x1[0:7].reshape(1792, 384), w1_ref[0])
    acc[...] += dot(x1[1:8].reshape(1792, 384), w1_ref[1])
    acc[...] += dot(x1[2:9].reshape(1792, 384), w1_ref[2])
    for i in range(7):
        h = jnp.maximum(acc[i * 256 : (i + 1) * 256], 0.0)
        if i == 0:
            h = h * not_first
        if i >= 5:
            h = h * not_last
        put_columns(x2, i, h)
    acc[0:1280] = dot(x2[0:5].reshape(1280, 384), w2_ref[0])
    acc[0:1280] += dot(x2[1:6].reshape(1280, 384), w2_ref[1])
    acc[0:1280] += dot(x2[2:7].reshape(1280, 384), w2_ref[2])
    table = []
    for i in range(5):
        h = jnp.maximum(acc[i * 256 : (i + 1) * 256], 0.0)
        if i == 4:
            h = h * not_last
        table.append(dot_nt(wr_ref[...], h.astype(BF16)))
    table = jnp.concatenate(table, axis=0).astype(BF16)
    scale = scale_ref[0]
    col_iota = lax.broadcasted_iota(jnp.int32, (256, 512), 0)

    def lanes(x):
        return jnp.concatenate([x[i : i + 1] for i in range(4)], axis=1)

    for k in range(8):
        pix = lanes(pix_ref[4 * k : 4 * k + 4])
        fr = lanes(frac_ref[0, 4 * k : 4 * k + 4])
        fc = lanes(frac_ref[1, 4 * k : 4 * k + 4])
        col = pix & 255
        row = pix >> 8
        weights = jnp.where(
            col_iota == col, 1.0 - fc, jnp.where(col_iota == col + 1, fc, 0.0)
        ).astype(BF16)
        got = dot(table, weights)
        total = None
        for r in range(5):
            blend = jnp.where(row == r, 1.0 - fr, jnp.where(row == r - 1, fr, 0.0)) * scale
            part = got[32 * r : 32 * r + 32] * blend
            total = part if total is None else total + part
        block = jnp.concatenate([total[:, 128 * i : 128 * i + 128] for i in range(4)], axis=0)
        packed[pl.ds(k, 128, stride=8), :] = block.T
    out_ref[...] = packed[...].astype(BF16)


def features(slab, scale, img, far, core, w1, w2, wr, pix, frac):
    return pl.pallas_call(
        features_kernel,
        out_shape=jax.ShapeDtypeStruct((1024, 128), BF16),
        in_specs=[whole(pltpu.SMEM)] * 2 + [whole(pltpu.VMEM)] * 8,
        out_specs=whole(pltpu.VMEM),
        scratch_shapes=[
            pltpu.VMEM((9, 256, 384), BF16),
            pltpu.VMEM((7, 256, 384), BF16),
            pltpu.VMEM((1792, 128), F32),
            pltpu.VMEM((1024, 128), F32),
        ],
        compiler_params=pltpu.CompilerParams(vmem_limit_bytes=40 * 2**20),
        name="features",
    )(slab, scale, img, far, core, w1, w2, wr, pix, frac)


def scatter_kernel(val_ref, by_lane_ref, by_row_ref, out_ref):
    val = val_ref[...]
    lo_iota = lax.broadcasted_iota(jnp.int32, (256, 1024), 0)
    hi_iota = lax.broadcasted_iota(jnp.int32, (1024, 128), 1) // 32
    sel_row = lax.broadcasted_iota(jnp.int32, (128, 128), 0)
    sel_col = lax.broadcasted_iota(jnp.int32, (128, 128), 1) % 32
    total = jnp.zeros((256, 128), F32)
    for s in range(4):
        one_hot = jnp.where(lo_iota == (by_lane_ref[s : s + 1] >> 2), 1.0, 0.0).astype(BF16)
        select = jnp.where(sel_row == sel_col + 32 * s, 1.0, 0.0).astype(BF16)
        spread = dot(val, select)
        hi = by_row_ref[:, s : s + 1] & 3
        spread = jnp.where(hi_iota == hi, spread, 0.0).astype(BF16)
        total = total + dot(one_hot, spread)
    out_ref[...] = total.reshape(2, 128, 128).astype(BF16)


def scatter(val, by_lane, by_row):
    return pl.pallas_call(
        scatter_kernel,
        out_shape=jax.ShapeDtypeStruct((2, 128, 128), BF16),
        in_specs=[whole(pltpu.VMEM)] * 3,
        out_specs=whole(pltpu.VMEM),
        compiler_params=pltpu.CompilerParams(vmem_limit_bytes=40 * 2**20),
        name="scatter",
    )(val, by_lane, by_row)


def put_depth(dst, plane, x):
    step = lax.broadcasted_iota(jnp.int32, x.shape, 0) % 16
    lane = lax.broadcasted_iota(jnp.int32, x.shape, 1)
    rows = x.shape[0]
    before = jnp.where(step == 0, 0.0, pltpu.roll(x, 1, 0))
    after = jnp.where(step == 15, 0.0, pltpu.roll(x, rows - 1, 0))
    side = pltpu.roll(jnp.where(lane >= 96, before, after), 32, 1)
    dst[plane, :, 0:128] = x.astype(BF16)
    dst[plane, :, 128:256] = jnp.where(lane < 64, side, 0.0).astype(BF16)


def volume_kernel(pos_ref, own_ref, near_ref, next_ref, w1_ref, w2_ref, out_ref, x1, x2, acc):
    p = pos_ref[0]
    q = pos_ref[1]
    even = (1 - p % 2).astype(F32)
    odd = 1.0 - even
    for i in range(2):
        near = near_ref[i].astype(F32)
        nxt = next_ref[i].astype(F32)
        put_depth(x1, i, even * nxt + odd * near)
        put_depth(x1, 2 + i, own_ref[i].astype(F32))
        put_depth(x1, 4 + i, even * near + odd * nxt)
    for t in range(9):
        dx, dy = divmod(t, 3)
        part = dot_nt(x1[dx : dx + 4, dy * 16 : dy * 16 + 160, :].reshape(640, 256), w1_ref[t])
        if t == 0:
            acc[...] = part
        else:
            acc[...] += part
    y = lax.broadcasted_iota(jnp.int32, (160, 128), 0) // 16
    first_y = jnp.where(q == 0, 1, 0)
    last_y = jnp.where(q == 3, 8, 9)
    inside = (y >= first_y) & (y <= last_y)
    for i in range(4):
        h = jnp.where(inside, jnp.maximum(acc[i * 160 : (i + 1) * 160], 0.0), 0.0)
        if i == 0:
            h = h * jnp.where(p == 0, 0.0, 1.0)
        if i == 3:
            h = h * jnp.where(p == 31, 0.0, 1.0)
        put_depth(x2, i, h)
    for t in range(9):
        dx, dy = divmod(t, 3)
        part = dot_nt(x2[dx : dx + 2, dy * 16 : dy * 16 + 128, :].reshape(256, 256), w2_ref[t])
        if t == 0:
            acc[0:256] = part
        else:
            acc[0:256] += part
    place_row = lax.broadcasted_iota(jnp.int32, (128, 512), 0) * 4
    place_col = lax.broadcasted_iota(jnp.int32, (128, 512), 1)
    for i in range(2):
        res = acc[i * 128 : (i + 1) * 128] + own_ref[i, 32:160].astype(F32)
        res = res.T.astype(BF16)
        total = jnp.zeros((32, 512), F32)
        for z in range(4):
            place = jnp.where(place_col == place_row + z, 1.0, 0.0).astype(BF16)
            total = total + dot(res[32 * z : 32 * z + 32], place)
        out_ref[:, 512 * i : 512 * i + 512] = total.astype(BF16)


def volume_convs(pos, own, near, nxt, w1, w2):
    return pl.pallas_call(
        volume_kernel,
        out_shape=jax.ShapeDtypeStruct((32, 1024), BF16),
        in_specs=[whole(pltpu.SMEM)] + [whole(pltpu.VMEM)] * 5,
        out_specs=whole(pltpu.VMEM),
        scratch_shapes=[
            pltpu.VMEM((6, 192, 256), BF16),
            pltpu.VMEM((4, 160, 256), BF16),
            pltpu.VMEM((640, 128), F32),
        ],
        compiler_params=pltpu.CompilerParams(vmem_limit_bytes=40 * 2**20),
        name="volume",
    )(pos, own, near, nxt, w1, w2)


def banded(weight):
    taps = weight.reshape(9, 3, 32, 32)
    zero = jnp.zeros((9, 32, 32), weight.dtype)
    rows = []
    for z in range(4):
        blocks = [zero] * 8
        for dz in range(3):
            at = z + dz - 1
            blocks[4 if at < 0 else 5 if at > 3 else at] = taps[:, dz]
        rows.append(jnp.concatenate(blocks, axis=2))
    return jnp.concatenate(rows, axis=1)


def swap(x, partner, cams, slabs):
    pairs = []
    for p in range(cams):
        for s in range(slabs):
            to = partner(p, s)
            if 0 <= to[0] < cams and 0 <= to[1] < slabs:
                pairs.append((p * slabs + s, to[0] * slabs + to[1]))
    return lax.ppermute(x, AXES, pairs)


def core_partner(p, s):
    return p, s ^ 1


def far_partner(p, s):
    return p, (s + 1 if s % 2 else s - 1)


def near_partner(p, s):
    return p ^ 1, s


def next_partner(p, s):
    return (p + 1 if p % 2 else p - 1), s


def local(
    image,
    w_first,
    w_second,
    w_reduce,
    cam_weight,
    sample_pixel,
    sample_frac,
    voxel_slot,
    wv_first,
    wv_second,
):
    cams = lax.axis_size("cam")
    slabs = lax.axis_size("slab")
    p = lax.axis_index("cam")
    s = lax.axis_index("slab")
    even = s % 2 == 0
    img = image[0]
    top, bottom = img[0:3], img[1:4]
    far = swap(jnp.where(even, top, bottom), far_partner, cams, slabs)
    core = swap(jnp.where(even, bottom, top), core_partner, cams, slabs)

    pix = sample_pixel[0].T
    frac = jnp.transpose(sample_frac[0], (0, 2, 1))
    w1 = w_first.reshape(3, 384, 128)
    w2 = w_second.reshape(3, 384, 128)
    by_row = voxel_slot[0].reshape(1024, 4)
    by_lane = by_row.T
    band1 = banded(wv_first)
    band2 = banded(wv_second)
    slab_pos = s.astype(jnp.int32).reshape(1)
    pos = jnp.stack([p, s]).astype(jnp.int32)

    sent = features(slab_pos, cam_weight, img, far, core, w1, w2, w_reduce.T, pix, frac)
    got = lax.all_to_all(sent.reshape(128, 8, 128), AXES, 0, 0, tiled=True).reshape(1024, 128)
    volume = scatter(got, by_lane, by_row)

    top, bottom = volume[:, 0:32], volume[:, 96:128]
    far = swap(jnp.where(even, top, bottom), far_partner, cams, slabs)
    core = swap(jnp.where(even, bottom, top), core_partner, cams, slabs)
    above = jnp.where(even, far, core)
    below = jnp.where(even, core, far)
    own = jnp.concatenate([above, volume, below], axis=1)
    near = swap(own, near_partner, cams, slabs)
    nxt = swap(own, next_partner, cams, slabs)
    out = volume_convs(pos, own, near, nxt, band1, band2)
    return out.reshape(32, 2, 512)


def solution(mesh):
    placed = (
        P(("dp", "cam"), "slab", None, None),
        P(),
        P(),
        P(),
        P("cam"),
        P(("dp", "cam", "slab"), None, None),
        P(("dp", "cam", "slab"), None, None, None),
        P(("dp", "cam", "slab"), None, None),
        P(),
        P(),
    )
    return jax.shard_map(
        local, mesh=mesh, in_specs=placed, out_specs=P(None, ("dp", "cam"), "slab"), check_vma=False
    )
```

time: 258 us -> 104 us (0.40)
  the two profiles are of different devices: /device:TPU:3 before, /device:TPU:27 now
where the time goes in v1:
time: 104 us
  starting transfers between devices  55.4 us (53%)
  waiting for transfers between devices  33.2 us (32%)
  Pallas kernels  8.72 us (8%)
  local copies, waits for them, and re-layouts  3.69 us (4%)
  other arithmetic  1.62 us (2%)
    ppermute x6, starting transfers between devices, swap(): return lax.ppermute(x, AXES, pairs)  35.5 us
    all_to_all x1, starting transfers between devices, local(): lax.all_to_all(sent.reshape(128, 8, 128), AXES, 0, 0, tiled=True)  19.9 us
    all_to_all x1, waiting for transfers between devices, local(): lax.all_to_all(sent.reshape(128, 8, 128), AXES, 0, 0, tiled=True)  17.8 us
    ppermute x6, waiting for transfers between devices, swap(): return lax.ppermute(x, AXES, pairs)  15.4 us
    pallas_call x1, Pallas kernels, features(): pl.pallas_call(features_kernel, out_shape=jax.ShapeDtypeStruct((1024, 128...  4.21 us
    pallas_call x1, Pallas kernels, volume_convs(): pl.pallas_call(volume_kernel, out_shape=jax.ShapeDtypeStruct((32, 1024),...  3.27 us
  transfers between devices with their start and end apart: 7, of which 4 were waited for; matrix products, arithmetic and copies ran while one was open for 2% of the time, Pallas kernels for 0%

profile of v1, /device:TPU:27, one launch (start us, length us, event | category | flops | bytes accessed | tf_op | source)
XLA Modules:
  0.0 103.6 jit_solution(15568186576746146801)
XLA Ops:
  0.0 0.0 copy-start
  0.0 0.0 copy-start.3
  0.0 0.0 copy-start.1
  0.0 0.0 copy-start.5
  0.0 0.0 copy-start.4
  0.0 1.1 %select_bitcast_fusion = (bf16[3,256,128]{2,1,0:T(8,128)(2,1)S(1)}, bf16[3,256,128]{2,1,0:T(8,128)(2,1)S(1)}) fusion(pred[]{:T(512)S(6)} %eq.5, bf16[1,4,256,128]{3,2,1,0:T(8,128)(2,1)} %param.10), kind=kLoop, calls=%fused_computation.2 | loop fusion | flops 196608 | bytes 786433 | tf_op jit(solution)/shard_map/jit(_where)/select_n | solution.py:290
  1.2 16.0 %collective-permute-start = (bf16[3,256,128]{2,1,0:T(8,128)(2,1)S(1)}, bf16[3,256,128]{2,1,0:T(8,128)(2,1)S(1)}, u32[]{:S(2)}, u32[]{:S(2)}) collective-permute-start(bf16[3,256,128]{2,1,0:T(8,128)(2,1)S(1)} %get-tuple-element.6), channel_id=1, source_target_pairs={{1,2},{2,1},{5,6},{6,5},{9,10},{10,9},{13,14},{14,13},{17,18},{18,... | collective-permute-start | bytes 589832 | tf_op jit(solution)/shard_map/ppermute | solution.py:251
  17.2 1.9 %collective-permute-start.1 = (bf16[3,256,128]{2,1,0:T(8,128)(2,1)S(1)}, bf16[3,256,128]{2,1,0:T(8,128)(2,1)S(1)}, u32[]{:S(2)}, u32[]{:S(2)}) collective-permute-start(bf16[3,256,128]{2,1,0:T(8,128)(2,1)S(1)} %get-tuple-element.5), channel_id=1, source_target_pairs={{0,1},{1,0},{2,3},{3,2},{4,5},{5,4},{6,7},{7,6},{8,9},{9,8},{10,11... | collective-permute-start | bytes 589832 | tf_op jit(solution)/shard_map/ppermute | solution.py:251
  19.7 1.1 %collective-permute-done.far_ref = bf16[3,256,128]{2,1,0:T(8,128)(2,1)S(1)} collective-permute-done((bf16[3,256,128]{2,1,0:T(8,128)(2,1)S(1)}, bf16[3,256,128]{2,1,0:T(8,128)(2,1)S(1)}, u32[]{:S(2)}, u32[]{:S(2)}) %collective-permute-start) | collective-permute-done | bytes 196640 | tf_op jit(solution)/shard_map/ppermute | solution.py:251
  20.8 0.0 collective-permute-done.1.core_ref
  20.8 0.0 copy-done
  20.8 0.0 copy-done.3
  20.8 0.0 copy-done.1
  20.8 0.0 copy-done.5
  20.8 0.0 copy-done.4
  20.8 0.0 copy-start.2
  20.9 1.0 copy-done.2
  21.8 4.2 %features.1 = bf16[1024,128]{1,0:T(8,128)(2,1)} custom-call(s32[1]{0:T(128)} %bitcast.1.pos_ref, f32[1]{0:T(128)S(6)} %copy.27.scale_ref, bf16[4,256,128]{2,1,0:T(8,128)(2,1)S(1)} %bitcast.45, bf16[3,256,128]{2,1,0:T(8,128)(2,1)S(1)} %collective-permute-done.far_ref, bf16[3,256,128]{2,1,0:T(8,128)(2,1)S(1)} %collective-permute-done.1.core_ref, ...), custom_call_target="tpu_custom_call" | custom-call | tf_op jit(solution)/shard_map/features/pallas_call | solution.py:112
  26.0 0.0 copy-start.6
  26.0 0.0 copy-start.7
  26.0 19.9 %all-to-all-start = ((bf16[128,8,128]{2,1,0:T(8,128)(2,1)}), bf16[128,8,128]{2,1,0:T(8,128)(2,1)S(1)}, u32[]{:S(2)}, u32[]{:S(2)}) async-start(bf16[128,8,128]{2,1,0:T(8,128)(2,1)} %bitcast.12), calls=%async_computation | async-start | bytes 524288 | tf_op jit(solution)/shard_map/all_to_all | solution.py:304
  45.9 0.0 copy-done.6
  45.9 0.0 copy-done.7
  45.9 0.1 slice_bitcast_fusion.1
  46.0 0.2 concatenate.37
  46.2 0.2 concatenate.34
  46.4 0.2 concatenate.42
  46.6 0.2 concatenate.39
  46.8 0.0 copy-start.8
  46.8 0.2 concatenate.36
  47.0 0.2 concatenate.41
  47.1 0.3 copy-done.8
  47.5 0.1 copy.13
  47.6 0.2 reshape_squeeze.3.by_row_ref
  47.8 0.2 copy.14
  48.0 0.1 pad.11.clone
  48.1 17.8 %all-to-all-done = bf16[128,8,128]{2,1,0:T(8,128)(2,1)S(1)} async-done(((bf16[128,8,128]{2,1,0:T(8,128)(2,1)}), bf16[128,8,128]{2,1,0:T(8,128)(2,1)S(1)}, u32[]{:S(2)}, u32[]{:S(2)}) %all-to-all-start) | async-done | bytes 262176 | tf_op jit(solution)/shard_map/all_to_all | solution.py:304
  65.9 1.2 %scatter.1 = bf16[2,128,128]{2,1,0:T(8,128)(2,1)S(1)} custom-call(bf16[1024,128]{1,0:T(8,128)(2,1)S(1)} %bitcast.46, s32[4,1024]{1,0:T(4,128)S(1)} %bitcast.49, s32[1024,4]{1,0:T(8,128)S(1)} %reshape_squeeze.3.by_row_ref), custom_call_target="tpu_custom_call" | custom-call | tf_op jit(solution)/shard_map/scatter/pallas_call | solution.py:146
  67.1 6.2 %collective-permute-start.2 = (bf16[2,32,128]{2,1,0:T(8,128)(2,1)S(1)}, bf16[2,32,128]{2,1,0:T(8,128)(2,1)S(1)}, u32[]{:S(2)}, u32[]{:S(2)}) collective-permute-start(bf16[2,32,128]{2,1,0:T(8,128)(2,1)S(1)} %get-tuple-element.15), channel_id=1, source_target_pairs={{1,2},{2,1},{5,6},{6,5},{9,10},{10,9},{13,14},{14,13},{17,18},{18,... | collective-permute-start | bytes 49160 | tf_op jit(solution)/shard_map/ppermute | solution.py:251
  73.3 1.9 %collective-permute-start.3 = (bf16[2,32,128]{2,1,0:T(8,128)(2,1)S(1)}, bf16[2,32,128]{2,1,0:T(8,128)(2,1)S(1)}, u32[]{:S(2)}, u32[]{:S(2)}) collective-permute-start(bf16[2,32,128]{2,1,0:T(8,128)(2,1)S(1)} %get-tuple-element.16), channel_id=1, source_target_pairs={{0,1},{1,0},{2,3},{3,2},{4,5},{5,4},{6,7},{7,6},{8,9},{9,8},{10,11... | collective-permute-start | bytes 49160 | tf_op jit(solution)/shard_map/ppermute | solution.py:251
  75.3 0.4 pad_maximum_fusion.1
  75.7 5.2 %collective-permute-done.2 = bf16[2,32,128]{2,1,0:T(8,128)(2,1)S(1)} collective-permute-done((bf16[2,32,128]{2,1,0:T(8,128)(2,1)S(1)}, bf16[2,32,128]{2,1,0:T(8,128)(2,1)S(1)}, u32[]{:S(2)}, u32[]{:S(2)}) %collective-permute-start.2) | collective-permute-done | bytes 16416 | tf_op jit(solution)/shard_map/ppermute | solution.py:251
  80.9 0.0 collective-permute-done.3
  80.9 5.8 %collective-permute-start.4 = (bf16[2,192,128]{2,1,0:T(8,128)(2,1)S(1)}, bf16[2,192,128]{2,1,0:T(8,128)(2,1)S(1)}, u32[]{:S(2)}, u32[]{:S(2)}) collective-permute-start(bf16[2,192,128]{2,1,0:T(8,128)(2,1)S(1)} %pad_maximum_fusion.2.own_ref), channel_id=1, source_target_pairs={{0,4},{1,5},{2,6},{3,7},{4,0},{5,1},{6,2},{7,3},{8,12},{9,13},{10,... | collective-permute-start | bytes 294920 | tf_op jit(solution)/shard_map/ppermute | solution.py:251
  86.8 3.7 %collective-permute-start.5 = (bf16[2,192,128]{2,1,0:T(8,128)(2,1)S(1)}, bf16[2,192,128]{2,1,0:T(8,128)(2,1)S(1)}, u32[]{:S(2)}, u32[]{:S(2)}) collective-permute-start(bf16[2,192,128]{2,1,0:T(8,128)(2,1)S(1)} %pad_maximum_fusion.2.own_ref), channel_id=1, source_target_pairs={{4,8},{5,9},{6,10},{7,11},{8,4},{9,5},{10,6},{11,7},{12,16},{13,17... | collective-permute-start | bytes 294920 | tf_op jit(solution)/shard_map/ppermute | solution.py:251
  90.5 0.1 pad_add_fusion.pos_ref
  90.6 0.0 collective-permute-done.4.near_ref
  90.6 9.1 %collective-permute-done.5.next_ref = bf16[2,192,128]{2,1,0:T(8,128)(2,1)S(1)} collective-permute-done((bf16[2,192,128]{2,1,0:T(8,128)(2,1)S(1)}, bf16[2,192,128]{2,1,0:T(8,128)(2,1)S(1)}, u32[]{:S(2)}, u32[]{:S(2)}) %collective-permute-start.5) | collective-permute-done | bytes 98336 | tf_op jit(solution)/shard_map/ppermute | solution.py:251
  99.7 3.3 %volume.1 = bf16[32,1024]{1,0:T(8,128)(2,1)S(1)} custom-call(s32[2]{0:T(128)S(1)} %pad_add_fusion.pos_ref, bf16[2,192,128]{2,1,0:T(8,128)(2,1)S(1)} %pad_maximum_fusion.2.own_ref, bf16[2,192,128]{2,1,0:T(8,128)(2,1)S(1)} %collective-permute-done.4.near_ref, bf16[2,192,128]{2,1,0:T(8,128)(2,1)S(1)} %collective-permute-done.5.next_ref, ...), custom_call_target="tpu_custom_call" | custom-call | tf_op jit(solution)/shard_map/volume/pallas_call | solution.py:216
  102.9 0.7 reshape.34
  (8 shorter events, 0.1 us)
Async XLA Ops:
  0.0 20.8 %copy-start = (bf16[1,4,256,128]{3,2,1,0:T(8,128)(2,1)S(1)}, bf16[1,4,256,128]{3,2,1,0:T(8,128)(2,1)}, u32[]{:S(2)}) copy-start(bf16[1,4,256,128]{3,2,1,0:T(8,128)(2,1)} %param.10) | copy-start | bytes 786436
  0.0 20.8 %copy-start.3 = (f32[1,2,128,32]{2,3,1,0:T(8,128)S(1)}, f32[1,2,128,32]{2,3,1,0:T(8,128)}, u32[]{:S(2)}) copy-start(f32[1,2,128,32]{2,3,1,0:T(8,128)} %param.16) | copy-start | bytes 98308
  0.0 20.8 %copy-start.1 = (bf16[3,3,128,128]{3,2,1,0:T(8,128)(2,1)S(1)}, bf16[3,3,128,128]{3,2,1,0:T(8,128)(2,1)}, u32[]{:S(2)}) copy-start(bf16[3,3,128,128]{3,2,1,0:T(8,128)(2,1)} %param.11) | copy-start | bytes 884740
  0.0 20.8 %copy-start.5 = (bf16[128,32]{0,1:T(8,128)(2,1)S(1)}, bf16[128,32]{0,1:T(8,128)(2,1)}, u32[]{:S(2)}) copy-start(bf16[128,32]{0,1:T(8,128)(2,1)} %param.13) | copy-start | bytes 24580
  0.0 20.8 %copy-start.4 = (s32[1,128,32]{1,2,0:T(8,128)S(1)}, s32[1,128,32]{1,2,0:T(8,128)}, u32[]{:S(2)}) copy-start(s32[1,128,32]{1,2,0:T(8,128)} %param.15) | copy-start | bytes 49156
  1.2 19.6 %collective-permute-start = (bf16[3,256,128]{2,1,0:T(8,128)(2,1)S(1)}, bf16[3,256,128]{2,1,0:T(8,128)(2,1)S(1)}, u32[]{:S(2)}, u32[]{:S(2)}) collective-permute-start(bf16[3,256,128]{2,1,0:T(8,128)(2,1)S(1)} %get-tuple-element.6), channel_id=1, source_target_pairs={{1,2},{2,1},{5,6},{6,5},{9,10},{10,9},{13,14},{14,13},{17,18},{18,... | collective-permute-start | bytes 589832 | tf_op jit(solution)/shard_map/ppermute | solution.py:251
  17.2 3.6 %collective-permute-start.1 = (bf16[3,256,128]{2,1,0:T(8,128)(2,1)S(1)}, bf16[3,256,128]{2,1,0:T(8,128)(2,1)S(1)}, u32[]{:S(2)}, u32[]{:S(2)}) collective-permute-start(bf16[3,256,128]{2,1,0:T(8,128)(2,1)S(1)} %get-tuple-element.5), channel_id=1, source_target_pairs={{0,1},{1,0},{2,3},{3,2},{4,5},{5,4},{6,7},{7,6},{8,9},{9,8},{10,11... | collective-permute-start | bytes 589832 | tf_op jit(solution)/shard_map/ppermute | solution.py:251
  20.8 1.0 copy-start.2
  26.0 19.9 %copy-start.6 = (bf16[27,32,32]{2,1,0:T(8,128)(2,1)S(1)}, bf16[27,32,32]{2,1,0:T(8,128)(2,1)}, u32[]{:S(2)}) copy-start(bf16[27,32,32]{2,1,0:T(8,128)(2,1)} %param.19) | copy-start | bytes 165892
  26.0 19.9 %copy-start.7 = (bf16[27,32,32]{2,1,0:T(8,128)(2,1)S(1)}, bf16[27,32,32]{2,1,0:T(8,128)(2,1)}, u32[]{:S(2)}) copy-start(bf16[27,32,32]{2,1,0:T(8,128)(2,1)} %param.18) | copy-start | bytes 165892
  26.0 39.9 %all-to-all-start = ((bf16[128,8,128]{2,1,0:T(8,128)(2,1)}), bf16[128,8,128]{2,1,0:T(8,128)(2,1)S(1)}, u32[]{:S(2)}, u32[]{:S(2)}) async-start(bf16[128,8,128]{2,1,0:T(8,128)(2,1)} %bitcast.12), calls=%async_computation | async-start | bytes 524288 | tf_op jit(solution)/shard_map/all_to_all | solution.py:304
  46.8 0.7 copy-start.8
  67.1 13.8 %collective-permute-start.2 = (bf16[2,32,128]{2,1,0:T(8,128)(2,1)S(1)}, bf16[2,32,128]{2,1,0:T(8,128)(2,1)S(1)}, u32[]{:S(2)}, u32[]{:S(2)}) collective-permute-start(bf16[2,32,128]{2,1,0:T(8,128)(2,1)S(1)} %get-tuple-element.15), channel_id=1, source_target_pairs={{1,2},{2,1},{5,6},{6,5},{9,10},{10,9},{13,14},{14,13},{17,18},{18,... | collective-permute-start | bytes 49160 | tf_op jit(solution)/shard_map/ppermute | solution.py:251
  73.3 7.6 %collective-permute-start.3 = (bf16[2,32,128]{2,1,0:T(8,128)(2,1)S(1)}, bf16[2,32,128]{2,1,0:T(8,128)(2,1)S(1)}, u32[]{:S(2)}, u32[]{:S(2)}) collective-permute-start(bf16[2,32,128]{2,1,0:T(8,128)(2,1)S(1)} %get-tuple-element.16), channel_id=1, source_target_pairs={{0,1},{1,0},{2,3},{3,2},{4,5},{5,4},{6,7},{7,6},{8,9},{9,8},{10,11... | collective-permute-start | bytes 49160 | tf_op jit(solution)/shard_map/ppermute | solution.py:251
  80.9 9.6 %collective-permute-start.4 = (bf16[2,192,128]{2,1,0:T(8,128)(2,1)S(1)}, bf16[2,192,128]{2,1,0:T(8,128)(2,1)S(1)}, u32[]{:S(2)}, u32[]{:S(2)}) collective-permute-start(bf16[2,192,128]{2,1,0:T(8,128)(2,1)S(1)} %pad_maximum_fusion.2.own_ref), channel_id=1, source_target_pairs={{0,4},{1,5},{2,6},{3,7},{4,0},{5,1},{6,2},{7,3},{8,12},{9,13},{10,... | collective-permute-start | bytes 294920 | tf_op jit(solution)/shard_map/ppermute | solution.py:251
  86.8 12.9 %collective-permute-start.5 = (bf16[2,192,128]{2,1,0:T(8,128)(2,1)S(1)}, bf16[2,192,128]{2,1,0:T(8,128)(2,1)S(1)}, u32[]{:S(2)}, u32[]{:S(2)}) collective-permute-start(bf16[2,192,128]{2,1,0:T(8,128)(2,1)S(1)} %pad_maximum_fusion.2.own_ref), channel_id=1, source_target_pairs={{4,8},{5,9},{6,10},{7,11},{8,4},{9,5},{10,6},{11,7},{12,16},{13,17... | collective-permute-start | bytes 294920 | tf_op jit(solution)/shard_map/ppermute | solution.py:251

commit v2 on v1

--- a/solution.py
+++ b/solution.py
@@ -32,22 +32,56 @@
     dst[row, :, 256:384] = right.astype(BF16)
 
 
+def lanes(x):
+    return jnp.concatenate([x[i : i + 1] for i in range(4)], axis=1)
+
+
+def prepare_kernel(scale_ref, img_ref, w1_ref, pix_ref, frac_ref, acc, weights, blends, x1):
+    for i in range(4):
+        put_columns(x1, i, img_ref[i].astype(F32))
+    own = x1[...].reshape(1024, 384)
+    acc[0:512] = jnp.zeros((512, 128), F32)
+    acc[1536:1792] = jnp.zeros((256, 128), F32)
+    acc[512:1536] = dot(own, w1_ref[0])
+    acc[256:1280] += dot(own, w1_ref[1])
+    acc[0:1024] += dot(own, w1_ref[2])
+    scale = scale_ref[0]
+    col_iota = lax.broadcasted_iota(jnp.int32, (256, 512), 0)
+    row_iota = lax.broadcasted_iota(jnp.int32, (8, 512), 0)
+    for k in range(8):
+        pix = lanes(pix_ref[4 * k : 4 * k + 4])
+        fr = lanes(frac_ref[0, 4 * k : 4 * k + 4])
+        fc = lanes(frac_ref[1, 4 * k : 4 * k + 4])
+        col = pix & 255
+        row = pix >> 8
+        weights[k] = jnp.where(
+            col_iota == col, 1.0 - fc, jnp.where(col_iota == col + 1, fc, 0.0)
+        ).astype(BF16)
+        blends[k] = scale * jnp.where(
+            row_iota == row, 1.0 - fr, jnp.where(row_iota == row + 1, fr, 0.0)
+        )
+
+
+def prepare(scale, img, w1, pix, frac):
+    return pl.pallas_call(
+        prepare_kernel,
+        out_shape=(
+            jax.ShapeDtypeStruct((1792, 128), F32),
+            jax.ShapeDtypeStruct((8, 256, 512), BF16),
+            jax.ShapeDtypeStruct((8, 8, 512), F32),
+        ),
+        in_specs=[whole(pltpu.SMEM)] + [whole(pltpu.VMEM)] * 4,
+        out_specs=(whole(pltpu.VMEM),) * 3,
+        scratch_shapes=[pltpu.VMEM((4, 256, 384), BF16)],
+        compiler_params=pltpu.CompilerParams(vmem_limit_bytes=24 * 2**20),
+        cost_estimate=pl.CostEstimate(flops=10**9, bytes_accessed=4 * 10**6, transcendentals=0),
+        name="prepare",
+    )(scale, img, w1, pix, frac)
+
+
 def features_kernel(
-    pos_ref,
-    scale_ref,
-    img_ref,
-    far_ref,
-    core_ref,
-    w1_ref,
-    w2_ref,
-    wr_ref,
-    pix_ref,
-    frac_ref,
-    out_ref,
-    x1,
-    x2,
-    acc,
-    packed,
+    pos_ref, far_ref, core_ref, w1_ref, w2_ref, wr_ref, part_ref, weights, blends, out_ref,
+    x1, x2, acc, packed,
 ):
     slab = pos_ref[0]
     even = (1 - slab % 2).astype(F32)
@@ -57,24 +91,35 @@
     for i in range(2):
         row = even * far_ref[1 + i].astype(F32) + odd * core_ref[1 + i].astype(F32)
         put_columns(x1, i, row)
-    for i in range(4):
-        put_columns(x1, 2 + i, img_ref[i].astype(F32))
     for i in range(3):
         row = even * core_ref[i].astype(F32) + odd * far_ref[i].astype(F32)
-        put_columns(x1, 6 + i, row)
-    acc[...] = dot(x1[0:7].reshape(1792, 384), w1_ref[0])
-    acc[...] += dot(x1[1:8].reshape(1792, 384), w1_ref[1])
-    acc[...] += dot(x1[2:9].reshape(1792, 384), w1_ref[2])
+        put_columns(x1, 2 + i, row)
+    head = dot(x1[0:2].reshape(512, 384), w1_ref[0])
+    head0 = head[0:256] + dot(x1[1], w1_ref[1])
+    tail0 = dot(x1[2:3].reshape(256, 384), w1_ref[0])
+    tail1 = dot(x1[2:4].reshape(512, 384), w1_ref[1])
+    tail2 = dot(x1[2:5].reshape(768, 384), w1_ref[2])
     for i in range(7):
-        h = jnp.maximum(acc[i * 256 : (i + 1) * 256], 0.0)
+        h = part_ref[i * 256 : (i + 1) * 256]
+        if i == 0:
+            h = h + head0
+        elif i == 1:
+            h = h + head[256:512]
+        elif i == 4:
+            h = h + tail2[0:256]
+        elif i == 5:
+            h = h + tail2[256:512] + tail1[0:256]
+        elif i == 6:
+            h = h + tail2[512:768] + tail1[256:512] + tail0
+        h = jnp.maximum(h, 0.0)
         if i == 0:
             h = h * not_first
         if i >= 5:
             h = h * not_last
         put_columns(x2, i, h)
-    acc[0:1280] = dot(x2[0:5].reshape(1280, 384), w2_ref[0])
-    acc[0:1280] += dot(x2[1:6].reshape(1280, 384), w2_ref[1])
-    acc[0:1280] += dot(x2[2:7].reshape(1280, 384), w2_ref[2])
+    acc[...] = dot(x2[0:5].reshape(1280, 384), w2_ref[0])
+    acc[...] += dot(x2[1:6].reshape(1280, 384), w2_ref[1])
+    acc[...] += dot(x2[2:7].reshape(1280, 384), w2_ref[2])
     table = []
     for i in range(5):
         h = jnp.maximum(acc[i * 256 : (i + 1) * 256], 0.0)
@@ -82,47 +127,32 @@
             h = h * not_last
         table.append(dot_nt(wr_ref[...], h.astype(BF16)))
     table = jnp.concatenate(table, axis=0).astype(BF16)
-    scale = scale_ref[0]
-    col_iota = lax.broadcasted_iota(jnp.int32, (256, 512), 0)
-
-    def lanes(x):
-        return jnp.concatenate([x[i : i + 1] for i in range(4)], axis=1)
-
     for k in range(8):
-        pix = lanes(pix_ref[4 * k : 4 * k + 4])
-        fr = lanes(frac_ref[0, 4 * k : 4 * k + 4])
-        fc = lanes(frac_ref[1, 4 * k : 4 * k + 4])
-        col = pix & 255
-        row = pix >> 8
-        weights = jnp.where(
-            col_iota == col, 1.0 - fc, jnp.where(col_iota == col + 1, fc, 0.0)
-        ).astype(BF16)
-        got = dot(table, weights)
-        total = None
-        for r in range(5):
-            blend = jnp.where(row == r, 1.0 - fr, jnp.where(row == r - 1, fr, 0.0)) * scale
-            part = got[32 * r : 32 * r + 32] * blend
-            total = part if total is None else total + part
+        got = dot(table, weights[k])
+        blend = blends[k]
+        total = got[0:32] * blend[0:1]
+        for r in range(1, 5):
+            total = total + got[32 * r : 32 * r + 32] * blend[r : r + 1]
         block = jnp.concatenate([total[:, 128 * i : 128 * i + 128] for i in range(4)], axis=0)
         packed[pl.ds(k, 128, stride=8), :] = block.T
     out_ref[...] = packed[...].astype(BF16)
 
 
-def features(slab, scale, img, far, core, w1, w2, wr, pix, frac):
+def features(slab, far, core, w1, w2, wr, part, weights, blends):
     return pl.pallas_call(
         features_kernel,
         out_shape=jax.ShapeDtypeStruct((1024, 128), BF16),
-        in_specs=[whole(pltpu.SMEM)] * 2 + [whole(pltpu.VMEM)] * 8,
+        in_specs=[whole(pltpu.SMEM)] + [whole(pltpu.VMEM)] * 8,
         out_specs=whole(pltpu.VMEM),
         scratch_shapes=[
-            pltpu.VMEM((9, 256, 384), BF16),
+            pltpu.VMEM((5, 256, 384), BF16),
             pltpu.VMEM((7, 256, 384), BF16),
-            pltpu.VMEM((1792, 128), F32),
+            pltpu.VMEM((1280, 128), F32),
             pltpu.VMEM((1024, 128), F32),
         ],
-        compiler_params=pltpu.CompilerParams(vmem_limit_bytes=40 * 2**20),
+        compiler_params=pltpu.CompilerParams(vmem_limit_bytes=32 * 2**20),
         name="features",
-    )(slab, scale, img, far, core, w1, w2, wr, pix, frac)
+    )(slab, far, core, w1, w2, wr, part, weights, blends)
 
 
 def scatter_kernel(val_ref, by_lane_ref, by_row_ref, out_ref):
@@ -164,17 +194,35 @@
     dst[plane, :, 128:256] = jnp.where(lane < 64, side, 0.0).astype(BF16)
 
 
-def volume_kernel(pos_ref, own_ref, near_ref, next_ref, w1_ref, w2_ref, out_ref, x1, x2, acc):
+def volume_kernel(pos_ref, own_ref, quad_ref, near_ref, core_ref, w1_ref, w2_ref, out_ref, x1, x2, acc):
     p = pos_ref[0]
     q = pos_ref[1]
-    even = (1 - p % 2).astype(F32)
-    odd = 1.0 - even
+    me = pos_ref[2]
+    even_p = p % 2 == 0
+    even_q = q % 2 == 0
+    has_next = jnp.where((p == 0) | (p == 31), 0.0, 1.0)
+    has_far = jnp.where((q == 0) | (q == 3), 0.0, 1.0)
+    next_at = jnp.where(even_p, 0, 4)
+    near_at = 4 - next_at
+    far_from = pl.multiple_of(jnp.where(even_q, 96, 0), 32)
     for i in range(2):
-        near = near_ref[i].astype(F32)
-        nxt = next_ref[i].astype(F32)
-        put_depth(x1, i, even * nxt + odd * near)
-        put_depth(x1, 2 + i, own_ref[i].astype(F32))
-        put_depth(x1, 4 + i, even * near + odd * nxt)
+        nxt = quad_ref[me ^ 1, i].astype(F32) * has_next
+        far = quad_ref[me ^ 2, i, pl.ds(far_from, 32)].astype(F32) * has_far
+        diag = quad_ref[me ^ 3, i, pl.ds(far_from, 32)].astype(F32) * (has_far * has_next)
+        groups = (
+            (2 + i, own_ref[i].astype(F32), far, core_ref[i].astype(F32)),
+            (next_at + i, nxt, diag, core_ref[2 + i].astype(F32) * has_next),
+            (
+                near_at + i,
+                near_ref[i, 32:160].astype(F32),
+                near_ref[i, 0:32].astype(F32),
+                core_ref[4 + i].astype(F32),
+            ),
+        )
+        for plane, mid, far_rows, core_rows in groups:
+            above = jnp.where(even_q, far_rows, core_rows)
+            below = jnp.where(even_q, core_rows, far_rows)
+            put_depth(x1, plane, jnp.concatenate([above, mid, below], axis=0))
     for t in range(9):
         dx, dy = divmod(t, 3)
         part = dot_nt(x1[dx : dx + 4, dy * 16 : dy * 16 + 160, :].reshape(640, 256), w1_ref[t])
@@ -202,30 +250,32 @@
             acc[0:256] += part
     place_row = lax.broadcasted_iota(jnp.int32, (128, 512), 0) * 4
     place_col = lax.broadcasted_iota(jnp.int32, (128, 512), 1)
+    planes = []
     for i in range(2):
-        res = acc[i * 128 : (i + 1) * 128] + own_ref[i, 32:160].astype(F32)
+        res = acc[i * 128 : (i + 1) * 128] + own_ref[i].astype(F32)
         res = res.T.astype(BF16)
         total = jnp.zeros((32, 512), F32)
         for z in range(4):
             place = jnp.where(place_col == place_row + z, 1.0, 0.0).astype(BF16)
             total = total + dot(res[32 * z : 32 * z + 32], place)
-        out_ref[:, 512 * i : 512 * i + 512] = total.astype(BF16)
-
-
-def volume_convs(pos, own, near, nxt, w1, w2):
+        planes.append(total)
+    out_ref[...] = jnp.stack(planes, axis=1).astype(BF16)
+
+
+def volume_convs(pos, own, quad, near, core, w1, w2):
     return pl.pallas_call(
         volume_kernel,
-        out_shape=jax.ShapeDtypeStruct((32, 1024), BF16),
-        in_specs=[whole(pltpu.SMEM)] + [whole(pltpu.VMEM)] * 5,
+        out_shape=jax.ShapeDtypeStruct((32, 2, 512), BF16),
+        in_specs=[whole(pltpu.SMEM)] + [whole(pltpu.VMEM)] * 6,
         out_specs=whole(pltpu.VMEM),
         scratch_shapes=[
             pltpu.VMEM((6, 192, 256), BF16),
             pltpu.VMEM((4, 160, 256), BF16),
             pltpu.VMEM((640, 128), F32),
         ],
-        compiler_params=pltpu.CompilerParams(vmem_limit_bytes=40 * 2**20),
+        compiler_params=pltpu.CompilerParams(vmem_limit_bytes=32 * 2**20),
         name="volume",
-    )(pos, own, near, nxt, w1, w2)
+    )(pos, own, quad, near, core, w1, w2)
 
 
 def banded(weight):
@@ -263,8 +313,18 @@
     return p ^ 1, s
 
 
-def next_partner(p, s):
-    return (p + 1 if p % 2 else p - 1), s
+def quads(cams, slabs):
+    groups = []
+    for odd in range(1, cams, 2):
+        for low in range(slabs // 2):
+            groups.append(
+                [
+                    c % cams * slabs + t
+                    for t in (low, slabs - 1 - low)
+                    for c in (odd, odd + 1)
+                ]
+            )
+    return groups
 
 
 def local(
@@ -298,22 +358,28 @@
     band1 = banded(wv_first)
     band2 = banded(wv_second)
     slab_pos = s.astype(jnp.int32).reshape(1)
-    pos = jnp.stack([p, s]).astype(jnp.int32)
-
-    sent = features(slab_pos, cam_weight, img, far, core, w1, w2, w_reduce.T, pix, frac)
+
+    part, weights, blends = prepare(cam_weight, img, w1, pix, frac)
+    sent = features(slab_pos, far, core, w1, w2, w_reduce.T, part, weights, blends)
     got = lax.all_to_all(sent.reshape(128, 8, 128), AXES, 0, 0, tiled=True).reshape(1024, 128)
-    volume = scatter(got, by_lane, by_row)
-
-    top, bottom = volume[:, 0:32], volume[:, 96:128]
-    far = swap(jnp.where(even, top, bottom), far_partner, cams, slabs)
-    core = swap(jnp.where(even, bottom, top), core_partner, cams, slabs)
-    above = jnp.where(even, far, core)
-    below = jnp.where(even, core, far)
-    own = jnp.concatenate([above, volume, below], axis=1)
-    near = swap(own, near_partner, cams, slabs)
-    nxt = swap(own, next_partner, cams, slabs)
-    out = volume_convs(pos, own, near, nxt, band1, band2)
-    return out.reshape(32, 2, 512)
+    own = scatter(got, by_lane, by_row)
+
+    quad = lax.all_gather(own, AXES, axis_index_groups=quads(cams, slabs))
+    me = (1 - p % 2) + 2 * (s // 2)
+    pos = jnp.stack([p, s, me]).astype(jnp.int32)
+    has_far = (s == 1) | (s == 2)
+    far = lax.dynamic_index_in_dim(quad, me ^ 2, 0, keepdims=False)
+    far = jnp.where(even, far[:, 96:128], far[:, 0:32])
+    far = jnp.where(has_far, far, jnp.zeros_like(far))
+    near = swap(jnp.concatenate([far, own], axis=1), near_partner, cams, slabs)
+    nxt = lax.dynamic_index_in_dim(quad, me ^ 1, 0, keepdims=False)
+    core = jnp.where(
+        even,
+        jnp.concatenate([own[:, 96:128], nxt[:, 96:128], near[:, 128:160]], axis=0),
+        jnp.concatenate([own[:, 0:32], nxt[:, 0:32], near[:, 32:64]], axis=0),
+    )
+    core = swap(core, core_partner, cams, slabs)
+    return volume_convs(pos, own, quad, near, core, band1, band2)
 
 
 def solution(mesh):

time: 104 us -> 111 us (1.067)
  the two profiles are of different devices: /device:TPU:27 before, /device:TPU:1 now
where the time goes in v2:
time: 111 us; the launch traced here: 110 us
  starting transfers between devices  46 us (41%)
  blocking collectives  24.8 us (22%)
  waiting for transfers between devices  21.3 us (19%)
  Pallas kernels  10.9 us (10%)
  local copies, waits for them, and re-layouts  5.11 us (5%)
  other arithmetic  1.58 us (1%)
    ppermute x4, starting transfers between devices, swap(): return lax.ppermute(x, AXES, pairs)  31.4 us
    all_gather x1, blocking collectives, local(): quad = lax.all_gather(own, AXES, axis_index_groups=quads(cams, slabs))  24.8 us
    all_to_all x1, waiting for transfers between devices, local(): lax.all_to_all(sent.reshape(128, 8, 128), AXES, 0, 0, tiled=True)  18.7 us
    all_to_all x1, starting transfers between devices, local(): lax.all_to_all(sent.reshape(128, 8, 128), AXES, 0, 0, tiled=True)  14.6 us
    pallas_call x1, Pallas kernels, volume_convs(): pl.pallas_call(volume_kernel, out_shape=jax.ShapeDtypeStruct((32, 2, 512)...  4.02 us
    unnamed x21, local copies, waits for them, and re-layouts  3.51 us
    pallas_call x1, Pallas kernels, features(): pl.pallas_call(features_kernel, out_shape=jax.ShapeDtypeStruct((1024, 128...  3.06 us
    ppermute x4, waiting for transfers between devices, swap(): return lax.ppermute(x, AXES, pairs)  2.59 us
  transfers between devices with their start and end apart: 5, of which 3 were waited for; matrix products, arithmetic and copies ran while one was open for 2% of the time, Pallas kernels for 2%

profile of v2, /device:TPU:1, one launch (start us, length us, event | category | flops | bytes accessed | tf_op | source)
XLA Modules:
  0.0 110.5 jit_solution(11312999458497876870)
XLA Ops:
  0.0 1.1 select_bitcast_fusion
  1.1 16.8 %collective-permute-start = (bf16[3,256,128]{2,1,0:T(8,128)(2,1)S(1)}, bf16[3,256,128]{2,1,0:T(8,128)(2,1)S(1)}, u32[]{:S(2)}, u32[]{:S(2)}) collective-permute-start(bf16[3,256,128]{2,1,0:T(8,128)(2,1)S(1)} %get-tuple-element.14), channel_id=1, source_target_pairs={{1,2},{2,1},{5,6},{6,5},{9,10},{10,9},{13,14},{14,13},{17,18},{18,... | collective-permute-start | bytes 589832 | tf_op jit(solution)/shard_map/ppermute | solution.py:301
  17.9 1.9 %collective-permute-start.1 = (bf16[3,256,128]{2,1,0:T(8,128)(2,1)S(1)}, bf16[3,256,128]{2,1,0:T(8,128)(2,1)S(1)}, u32[]{:S(2)}, u32[]{:S(2)}) collective-permute-start(bf16[3,256,128]{2,1,0:T(8,128)(2,1)S(1)} %get-tuple-element.13), channel_id=1, source_target_pairs={{0,1},{1,0},{2,3},{3,2},{4,5},{5,4},{6,7},{7,6},{8,9},{9,8},{10,11... | collective-permute-start | bytes 589832 | tf_op jit(solution)/shard_map/ppermute | solution.py:301
  20.5 0.0 copy-start
  20.5 0.9 copy-done
  21.4 0.0 copy-start.1
  21.4 1.0 copy-done.1
  22.4 0.0 copy-start.5
  22.4 0.8 copy-done.5
  23.1 0.0 copy-start.6
  23.1 0.7 copy-done.6
  23.9 0.0 copy-start.2
  23.9 0.0 copy-start.3
  23.9 0.0 copy-start.4
  23.9 2.5 %prepare.1 = (f32[1792,128]{1,0:T(8,128)S(1)}, bf16[8,256,512]{2,1,0:T(8,128)(2,1)S(1)}, f32[8,8,512]{2,1,0:T(8,128)S(1)}) custom-call(f32[1]{0:T(128)S(6)} %copy.35.scale_ref, bf16[4,256,128]{2,1,0:T(8,128)(2,1)S(1)} %bitcast.54, bf16[3,384,128]{2,1,0:T(8,128)(2,1)S(1)} %bitcast.55, s32[32,128]{1,0:T(8,128)S(1)} %bitcast.61, f32[2,32,128]{2,1,0:T(8,128)S(1)} %bitcast.60), custom_call_target="tpu_custom_call" | custom-call | flops 1000000000 | bytes 4000000 | tf_op jit(solution)/shard_map/prepare/pallas_call | solution.py:66
  26.4 0.0 collective-permute-done.far_ref
  26.4 0.0 collective-permute-done.1.core_ref
  26.4 0.0 copy-done.2
  26.4 0.0 copy-done.3
  26.5 0.0 copy-done.4
  26.5 0.0 copy-start.7
  26.5 0.0 copy-start.8
  26.5 3.1 %features.1 = bf16[1024,128]{1,0:T(8,128)(2,1)} custom-call(s32[1]{0:T(128)} %bitcast.1.pos_ref, bf16[3,256,128]{2,1,0:T(8,128)(2,1)S(1)} %collective-permute-done.far_ref, bf16[3,256,128]{2,1,0:T(8,128)(2,1)S(1)} %collective-permute-done.1.core_ref, bf16[3,384,128]{2,1,0:T(8,128)(2,1)S(1)} %bitcast.56, bf16[3,384,128]{2,1,0:T(8,128)(2,1)S(1)} %bitcast.57, ...), custom_call_target="tpu_custom_call" | custom-call | tf_op jit(solution)/shard_map/features/pallas_call | solution.py:142
  29.5 14.6 %all-to-all-start = ((bf16[128,8,128]{2,1,0:T(8,128)(2,1)}), bf16[128,8,128]{2,1,0:T(8,128)(2,1)S(1)}, u32[]{:S(2)}, u32[]{:S(2)}) async-start(bf16[128,8,128]{2,1,0:T(8,128)(2,1)} %bitcast.13), calls=%async_computation | async-start | bytes 524288 | tf_op jit(solution)/shard_map/all_to_all | solution.py:364
  44.2 0.0 copy-done.7
  44.2 0.0 copy-done.8
  44.2 0.1 slice_bitcast_fusion.1
  44.3 0.2 concatenate.50
  44.5 0.2 concatenate.49
  44.7 0.0 copy-start.9
  44.7 0.2 concatenate.45
  44.9 0.2 concatenate.44
  45.1 0.2 concatenate.47
  45.2 0.2 concatenate.42
  45.4 0.0 copy-done.9
  45.4 0.1 copy.21
  45.5 0.2 reshape_squeeze.3.by_row_ref
  45.7 0.2 copy.22
  45.9 0.1 pad.11.clone
  46.0 0.4 pad_maximum_fusion.1
  46.4 18.7 %all-to-all-done = bf16[128,8,128]{2,1,0:T(8,128)(2,1)S(1)} async-done(((bf16[128,8,128]{2,1,0:T(8,128)(2,1)}), bf16[128,8,128]{2,1,0:T(8,128)(2,1)S(1)}, u32[]{:S(2)}, u32[]{:S(2)}) %all-to-all-start) | async-done | bytes 262176 | tf_op jit(solution)/shard_map/all_to_all | solution.py:364
  65.1 1.2 %scatter.1.own_ref = bf16[2,128,128]{2,1,0:T(8,128)(2,1)S(1)} custom-call(bf16[1024,128]{1,0:T(8,128)(2,1)S(1)} %bitcast.53, s32[4,1024]{1,0:T(4,128)S(1)} %bitcast.58, s32[1024,4]{1,0:T(8,128)S(1)} %reshape_squeeze.3.by_row_ref), custom_call_target="tpu_custom_call" | custom-call | tf_op jit(solution)/shard_map/scatter/pallas_call | solution.py:176
  66.3 24.8 %all-gather = bf16[8,128,128]{2,1,0:T(8,128)(2,1)S(1)} all-gather(bf16[2,128,128]{2,1,0:T(8,128)(2,1)S(1)} %scatter.1.own_ref), channel_id=2, replica_groups={{4,8,7,11},{5,9,6,10},{12,16,15,19},{13,17,14,18},{20,24,23,27},{21,25,..., dimensions={0}, use_global_device_ids=true | all-gather | bytes 327680 | tf_op jit(solution)/shard_map/all_gather | solution.py:367
  91.1 6.7 %collective-permute-start.2 = (bf16[2,160,128]{2,1,0:T(8,128)(2,1)S(1)}, bf16[2,160,128]{2,1,0:T(8,128)(2,1)S(1)}, u32[]{:S(2)}, u32[]{:S(2)}) collective-permute-start(bf16[2,160,128]{2,1,0:T(8,128)(2,1)S(1)} %pad_maximum_fusion.2), channel_id=1, source_target_pairs={{0,4},{1,5},{2,6},{3,7},{4,0},{5,1},{6,2},{7,3},{8,12},{9,13},{10,... | collective-permute-start | bytes 245768 | tf_op jit(solution)/shard_map/ppermute | solution.py:301
  97.8 1.8 %collective-permute-done.2.near_ref = bf16[2,160,128]{2,1,0:T(8,128)(2,1)S(1)} collective-permute-done((bf16[2,160,128]{2,1,0:T(8,128)(2,1)S(1)}, bf16[2,160,128]{2,1,0:T(8,128)(2,1)S(1)}, u32[]{:S(2)}, u32[]{:S(2)}) %collective-permute-start.2) | collective-permute-done | bytes 81952 | tf_op jit(solution)/shard_map/ppermute | solution.py:301
  99.6 6.0 %collective-permute-start.3 = (bf16[6,32,128]{2,1,0:T(8,128)(2,1)S(1)}, bf16[6,32,128]{2,1,0:T(8,128)(2,1)S(1)}, u32[]{:S(2)}, u32[]{:S(2)}) collective-permute-start(bf16[6,32,128]{2,1,0:T(8,128)(2,1)S(1)} %maximum_select_fusion), channel_id=1, source_target_pairs={{0,1},{1,0},{2,3},{3,2},{4,5},{5,4},{6,7},{7,6},{8,9},{9,8},{10,11... | collective-permute-start | bytes 147464 | tf_op jit(solution)/shard_map/ppermute | solution.py:301
  105.6 0.1 pad_add_fusion.pos_ref
  105.7 0.8 collective-permute-done.3.core_ref
  106.5 4.0 %volume.1 = bf16[32,2,512]{2,1,0:T(2,128)(2,1)} custom-call(s32[3]{0:T(128)S(1)} %pad_add_fusion.pos_ref, bf16[2,128,128]{2,1,0:T(8,128)(2,1)S(1)} %scatter.1.own_ref, bf16[4,2,128,128]{3,2,1,0:T(8,128)(2,1)S(1)} %bitcast.52, bf16[2,160,128]{2,1,0:T(8,128)(2,1)S(1)} %collective-permute-done.2.near_ref, ...), custom_call_target="tpu_custom_call" | custom-call | tf_op jit(solution)/shard_map/volume/pallas_call | solution.py:266
  (12 shorter events, 0.1 us)
Async XLA Ops:
  1.1 25.4 %collective-permute-start = (bf16[3,256,128]{2,1,0:T(8,128)(2,1)S(1)}, bf16[3,256,128]{2,1,0:T(8,128)(2,1)S(1)}, u32[]{:S(2)}, u32[]{:S(2)}) collective-permute-start(bf16[3,256,128]{2,1,0:T(8,128)(2,1)S(1)} %get-tuple-element.14), channel_id=1, source_target_pairs={{1,2},{2,1},{5,6},{6,5},{9,10},{10,9},{13,14},{14,13},{17,18},{18,... | collective-permute-start | bytes 589832 | tf_op jit(solution)/shard_map/ppermute | solution.py:301
  17.9 8.5 %collective-permute-start.1 = (bf16[3,256,128]{2,1,0:T(8,128)(2,1)S(1)}, bf16[3,256,128]{2,1,0:T(8,128)(2,1)S(1)}, u32[]{:S(2)}, u32[]{:S(2)}) collective-permute-start(bf16[3,256,128]{2,1,0:T(8,128)(2,1)S(1)} %get-tuple-element.13), channel_id=1, source_target_pairs={{0,1},{1,0},{2,3},{3,2},{4,5},{5,4},{6,7},{7,6},{8,9},{9,8},{10,11... | collective-permute-start | bytes 589832 | tf_op jit(solution)/shard_map/ppermute | solution.py:301
  20.5 1.0 copy-start
  21.4 1.0 copy-start.1
  22.4 0.8 copy-start.5
  23.1 0.7 copy-start.6
  23.9 2.6 %copy-start.2 = (bf16[3,3,128,128]{3,2,1,0:T(8,128)(2,1)S(1)}, bf16[3,3,128,128]{3,2,1,0:T(8,128)(2,1)}, u32[]{:S(2)}) copy-start(bf16[3,3,128,128]{3,2,1,0:T(8,128)(2,1)} %param.11) | copy-start | bytes 884740
  23.9 2.6 %copy-start.3 = (bf16[3,3,128,128]{3,2,1,0:T(8,128)(2,1)S(1)}, bf16[3,3,128,128]{3,2,1,0:T(8,128)(2,1)}, u32[]{:S(2)}) copy-start(bf16[3,3,128,128]{3,2,1,0:T(8,128)(2,1)} %param.12) | copy-start | bytes 884740
  23.9 2.6 %copy-start.4 = (bf16[128,32]{0,1:T(8,128)(2,1)S(1)}, bf16[128,32]{0,1:T(8,128)(2,1)}, u32[]{:S(2)}) copy-start(bf16[128,32]{0,1:T(8,128)(2,1)} %param.13) | copy-start | bytes 24580
  26.5 17.7 %copy-start.7 = (bf16[27,32,32]{2,1,0:T(8,128)(2,1)S(1)}, bf16[27,32,32]{2,1,0:T(8,128)(2,1)}, u32[]{:S(2)}) copy-start(bf16[27,32,32]{2,1,0:T(8,128)(2,1)} %param.19) | copy-start | bytes 165892
  26.5 17.7 %copy-start.8 = (bf16[27,32,32]{2,1,0:T(8,128)(2,1)S(1)}, bf16[27,32,32]{2,1,0:T(8,128)(2,1)}, u32[]{:S(2)}) copy-start(bf16[27,32,32]{2,1,0:T(8,128)(2,1)} %param.18) | copy-start | bytes 165892
  29.5 35.5 %all-to-all-start = ((bf16[128,8,128]{2,1,0:T(8,128)(2,1)}), bf16[128,8,128]{2,1,0:T(8,128)(2,1)S(1)}, u32[]{:S(2)}, u32[]{:S(2)}) async-start(bf16[128,8,128]{2,1,0:T(8,128)(2,1)} %bitcast.13), calls=%async_computation | async-start | bytes 524288 | tf_op jit(solution)/shard_map/all_to_all | solution.py:364
  44.7 0.7 copy-start.9
  91.1 8.5 %collective-permute-start.2 = (bf16[2,160,128]{2,1,0:T(8,128)(2,1)S(1)}, bf16[2,160,128]{2,1,0:T(8,128)(2,1)S(1)}, u32[]{:S(2)}, u32[]{:S(2)}) collective-permute-start(bf16[2,160,128]{2,1,0:T(8,128)(2,1)S(1)} %pad_maximum_fusion.2), channel_id=1, source_target_pairs={{0,4},{1,5},{2,6},{3,7},{4,0},{5,1},{6,2},{7,3},{8,12},{9,13},{10,... | collective-permute-start | bytes 245768 | tf_op jit(solution)/shard_map/ppermute | solution.py:301
  99.6 6.8 %collective-permute-start.3 = (bf16[6,32,128]{2,1,0:T(8,128)(2,1)S(1)}, bf16[6,32,128]{2,1,0:T(8,128)(2,1)S(1)}, u32[]{:S(2)}, u32[]{:S(2)}) collective-permute-start(bf16[6,32,128]{2,1,0:T(8,128)(2,1)S(1)} %maximum_select_fusion), channel_id=1, source_target_pairs={{0,1},{1,0},{2,3},{3,2},{4,5},{5,4},{6,7},{7,6},{8,9},{9,8},{10,11... | collective-permute-start | bytes 147464 | tf_op jit(solution)/shard_map/ppermute | solution.py:301

commit v3 on v2

--- a/solution.py
+++ b/solution.py
@@ -194,48 +194,66 @@
     dst[plane, :, 128:256] = jnp.where(lane < 64, side, 0.0).astype(BF16)
 
 
-def volume_kernel(pos_ref, own_ref, quad_ref, near_ref, core_ref, w1_ref, w2_ref, out_ref, x1, x2, acc):
+def volume_start_kernel(own_ref, w_ref, acc, x1):
+    for i in range(2):
+        put_depth(x1, i, own_ref[i].astype(F32))
+    zero = jnp.zeros((160, 128), F32)
+    acc[0:160] = zero
+    acc[480:640] = zero
+    for k, dx in enumerate((1, 0, 2)):
+        total = None
+        for dy in range(3):
+            rows = x1[:, dy * 16 : dy * 16 + 160, :].reshape(320, 256)
+            part = dot_nt(rows, w_ref[dx * 3 + dy])
+            total = part if total is None else total + part
+        at = (2 - dx) * 160
+        if k == 0:
+            acc[at : at + 320] = total
+        else:
+            acc[at : at + 320] += total
+
+
+def volume_start(own, w1):
+    return pl.pallas_call(
+        volume_start_kernel,
+        out_shape=jax.ShapeDtypeStruct((640, 128), F32),
+        in_specs=[whole(pltpu.VMEM)] * 2,
+        out_specs=whole(pltpu.VMEM),
+        scratch_shapes=[pltpu.VMEM((2, 192, 256), BF16)],
+        compiler_params=pltpu.CompilerParams(vmem_limit_bytes=16 * 2**20),
+        name="volume_start",
+    )(own, w1)
+
+
+def volume_kernel(
+    pos_ref, own_ref, next_ref, near_ref, part_ref, w1_ref, w2_ref, out_ref, x1, x2, acc
+):
     p = pos_ref[0]
     q = pos_ref[1]
-    me = pos_ref[2]
-    even_p = p % 2 == 0
-    even_q = q % 2 == 0
-    has_next = jnp.where((p == 0) | (p == 31), 0.0, 1.0)
-    has_far = jnp.where((q == 0) | (q == 3), 0.0, 1.0)
-    next_at = jnp.where(even_p, 0, 4)
-    near_at = 4 - next_at
-    far_from = pl.multiple_of(jnp.where(even_q, 96, 0), 32)
+    even = (1 - p % 2).astype(F32)
+    odd = 1.0 - even
     for i in range(2):
-        nxt = quad_ref[me ^ 1, i].astype(F32) * has_next
-        far = quad_ref[me ^ 2, i, pl.ds(far_from, 32)].astype(F32) * has_far
-        diag = quad_ref[me ^ 3, i, pl.ds(far_from, 32)].astype(F32) * (has_far * has_next)
-        groups = (
-            (2 + i, own_ref[i].astype(F32), far, core_ref[i].astype(F32)),
-            (next_at + i, nxt, diag, core_ref[2 + i].astype(F32) * has_next),
-            (
-                near_at + i,
-                near_ref[i, 32:160].astype(F32),
-                near_ref[i, 0:32].astype(F32),
-                core_ref[4 + i].astype(F32),
-            ),
-        )
-        for plane, mid, far_rows, core_rows in groups:
-            above = jnp.where(even_q, far_rows, core_rows)
-            below = jnp.where(even_q, core_rows, far_rows)
-            put_depth(x1, plane, jnp.concatenate([above, mid, below], axis=0))
-    for t in range(9):
-        dx, dy = divmod(t, 3)
-        part = dot_nt(x1[dx : dx + 4, dy * 16 : dy * 16 + 160, :].reshape(640, 256), w1_ref[t])
-        if t == 0:
-            acc[...] = part
-        else:
-            acc[...] += part
+        near = near_ref[i].astype(F32)
+        nxt = next_ref[i].astype(F32)
+        put_depth(x1, i, even * nxt + odd * near)
+        put_depth(x1, 2 + i, even * near + odd * nxt)
+    sums = [part_ref[i * 160 : (i + 1) * 160] for i in range(4)]
+    for dy in range(3):
+        rows = slice(dy * 16, dy * 16 + 160)
+        low0 = dot_nt(x1[0:2, rows, :].reshape(320, 256), w1_ref[dy])
+        low1 = dot_nt(x1[1, rows, :], w1_ref[3 + dy])
+        high1 = dot_nt(x1[2, rows, :], w1_ref[3 + dy])
+        high2 = dot_nt(x1[2:4, rows, :].reshape(320, 256), w1_ref[6 + dy])
+        sums[0] = sums[0] + low0[0:160] + low1
+        sums[1] = sums[1] + low0[160:320]
+        sums[2] = sums[2] + high2[0:160]
+        sums[3] = sums[3] + high2[160:320] + high1
     y = lax.broadcasted_iota(jnp.int32, (160, 128), 0) // 16
     first_y = jnp.where(q == 0, 1, 0)
     last_y = jnp.where(q == 3, 8, 9)
     inside = (y >= first_y) & (y <= last_y)
     for i in range(4):
-        h = jnp.where(inside, jnp.maximum(acc[i * 160 : (i + 1) * 160], 0.0), 0.0)
+        h = jnp.where(inside, jnp.maximum(sums[i], 0.0), 0.0)
         if i == 0:
             h = h * jnp.where(p == 0, 0.0, 1.0)
         if i == 3:
@@ -245,37 +263,39 @@
         dx, dy = divmod(t, 3)
         part = dot_nt(x2[dx : dx + 2, dy * 16 : dy * 16 + 128, :].reshape(256, 256), w2_ref[t])
         if t == 0:
-            acc[0:256] = part
+            acc[...] = part
         else:
-            acc[0:256] += part
+            acc[...] += part
     place_row = lax.broadcasted_iota(jnp.int32, (128, 512), 0) * 4
     place_col = lax.broadcasted_iota(jnp.int32, (128, 512), 1)
-    planes = []
+    both = []
     for i in range(2):
-        res = acc[i * 128 : (i + 1) * 128] + own_ref[i].astype(F32)
-        res = res.T.astype(BF16)
-        total = jnp.zeros((32, 512), F32)
-        for z in range(4):
-            place = jnp.where(place_col == place_row + z, 1.0, 0.0).astype(BF16)
-            total = total + dot(res[32 * z : 32 * z + 32], place)
-        planes.append(total)
-    out_ref[...] = jnp.stack(planes, axis=1).astype(BF16)
-
-
-def volume_convs(pos, own, quad, near, core, w1, w2):
+        res = acc[i * 128 : (i + 1) * 128] + own_ref[i, 32:160].astype(F32)
+        both.append(res.T.astype(BF16))
+    total = [None, None]
+    for z in range(4):
+        place = jnp.where(place_col == place_row + z, 1.0, 0.0).astype(BF16)
+        rows = jnp.concatenate([b[32 * z : 32 * z + 32] for b in both], axis=0)
+        part = dot(rows, place)
+        total = part if z == 0 else total + part
+    for i in range(2):
+        out_ref[:, 512 * i : 512 * i + 512] = total[32 * i : 32 * i + 32].astype(BF16)
+
+
+def volume_convs(pos, own, nxt, near, part, w1, w2):
     return pl.pallas_call(
         volume_kernel,
-        out_shape=jax.ShapeDtypeStruct((32, 2, 512), BF16),
+        out_shape=jax.ShapeDtypeStruct((32, 1024), BF16),
         in_specs=[whole(pltpu.SMEM)] + [whole(pltpu.VMEM)] * 6,
         out_specs=whole(pltpu.VMEM),
         scratch_shapes=[
-            pltpu.VMEM((6, 192, 256), BF16),
+            pltpu.VMEM((4, 192, 256), BF16),
             pltpu.VMEM((4, 160, 256), BF16),
-            pltpu.VMEM((640, 128), F32),
+            pltpu.VMEM((256, 128), F32),
         ],
         compiler_params=pltpu.CompilerParams(vmem_limit_bytes=32 * 2**20),
         name="volume",
-    )(pos, own, quad, near, core, w1, w2)
+    )(pos, own, nxt, near, part, w1, w2)
 
 
 def banded(weight):
@@ -313,18 +333,8 @@
     return p ^ 1, s
 
 
-def quads(cams, slabs):
-    groups = []
-    for odd in range(1, cams, 2):
-        for low in range(slabs // 2):
-            groups.append(
-                [
-                    c % cams * slabs + t
-                    for t in (low, slabs - 1 - low)
-                    for c in (odd, odd + 1)
-                ]
-            )
-    return groups
+def next_partner(p, s):
+    return (p + 1 if p % 2 else p - 1), s
 
 
 def local(
@@ -362,24 +372,20 @@
     part, weights, blends = prepare(cam_weight, img, w1, pix, frac)
     sent = features(slab_pos, far, core, w1, w2, w_reduce.T, part, weights, blends)
     got = lax.all_to_all(sent.reshape(128, 8, 128), AXES, 0, 0, tiled=True).reshape(1024, 128)
-    own = scatter(got, by_lane, by_row)
-
-    quad = lax.all_gather(own, AXES, axis_index_groups=quads(cams, slabs))
-    me = (1 - p % 2) + 2 * (s // 2)
-    pos = jnp.stack([p, s, me]).astype(jnp.int32)
-    has_far = (s == 1) | (s == 2)
-    far = lax.dynamic_index_in_dim(quad, me ^ 2, 0, keepdims=False)
-    far = jnp.where(even, far[:, 96:128], far[:, 0:32])
-    far = jnp.where(has_far, far, jnp.zeros_like(far))
-    near = swap(jnp.concatenate([far, own], axis=1), near_partner, cams, slabs)
-    nxt = lax.dynamic_index_in_dim(quad, me ^ 1, 0, keepdims=False)
-    core = jnp.where(
-        even,
-        jnp.concatenate([own[:, 96:128], nxt[:, 96:128], near[:, 128:160]], axis=0),
-        jnp.concatenate([own[:, 0:32], nxt[:, 0:32], near[:, 32:64]], axis=0),
-    )
-    core = swap(core, core_partner, cams, slabs)
-    return volume_convs(pos, own, quad, near, core, band1, band2)
+    volume = scatter(got, by_lane, by_row)
+
+    pos = jnp.stack([p, s]).astype(jnp.int32)
+    top, bottom = volume[:, 0:32], volume[:, 96:128]
+    far = swap(jnp.where(even, top, bottom), far_partner, cams, slabs)
+    core = swap(jnp.where(even, bottom, top), core_partner, cams, slabs)
+    above = jnp.where(even, far, core)
+    below = jnp.where(even, core, far)
+    own = jnp.concatenate([above, volume, below], axis=1)
+    nxt = swap(own, next_partner, cams, slabs)
+    near = swap(own, near_partner, cams, slabs)
+    part = volume_start(own, band1)
+    out = volume_convs(pos, own, nxt, near, part, band1, band2)
+    return out.reshape(32, 2, 512)
 
 
 def solution(mesh):

time: 111 us -> 95.2 us (0.86)
  the two profiles are of different devices: /device:TPU:1 before, /device:TPU:27 now
where the time goes in v3:
time: 95.2 us; the launch traced here: 94.6 us
  starting transfers between devices  48.9 us (51%)
  waiting for transfers between devices  27.8 us (29%)
  Pallas kernels  9.57 us (10%)
  local copies, waits for them, and re-layouts  5.75 us (6%)
  other arithmetic  1.57 us (2%)
    ppermute x6, starting transfers between devices, swap(): return lax.ppermute(x, AXES, pairs)  34.1 us
    all_to_all x1, waiting for transfers between devices, local(): lax.all_to_all(sent.reshape(128, 8, 128), AXES, 0, 0, tiled=True)  18.2 us
    all_to_all x1, starting transfers between devices, local(): lax.all_to_all(sent.reshape(128, 8, 128), AXES, 0, 0, tiled=True)  14.8 us
    ppermute x6, waiting for transfers between devices, swap(): return lax.ppermute(x, AXES, pairs)  9.69 us
    unnamed x21, local copies, waits for them, and re-layouts  3.51 us
    pallas_call x1, Pallas kernels, features(): pl.pallas_call(features_kernel, out_shape=jax.ShapeDtypeStruct((1024, 128...  3.06 us
    pallas_call x1, Pallas kernels, prepare(): pl.pallas_call(prepare_kernel, out_shape=(jax.ShapeDtypeStruct((1792, 128...  2.54 us
    pallas_call x1, Pallas kernels, volume_convs(): pl.pallas_call(volume_kernel, out_shape=jax.ShapeDtypeStruct((32, 1024),...  2.11 us
  transfers between devices with their start and end apart: 7, of which 4 were waited for; matrix products, arithmetic and copies ran while one was open for 2% of the time, Pallas kernels for 3%

profile of v3, /device:TPU:27, one launch (start us, length us, event | category | flops | bytes accessed | tf_op | source)
XLA Modules:
  0.0 94.6 jit_solution(6106166599145718713)
XLA Ops:
  0.0 1.1 %select_bitcast_fusion = (bf16[3,256,128]{2,1,0:T(8,128)(2,1)S(1)}, bf16[3,256,128]{2,1,0:T(8,128)(2,1)S(1)}) fusion(pred[]{:T(512)S(6)} %eq.5, bf16[1,4,256,128]{3,2,1,0:T(8,128)(2,1)} %param.10), kind=kLoop, calls=%fused_computation.2 | loop fusion | flops 196608 | bytes 786433 | tf_op jit(solution)/shard_map/jit(_where)/select_n | solution.py:360
  1.1 16.0 %collective-permute-start = (bf16[3,256,128]{2,1,0:T(8,128)(2,1)S(1)}, bf16[3,256,128]{2,1,0:T(8,128)(2,1)S(1)}, u32[]{:S(2)}, u32[]{:S(2)}) collective-permute-start(bf16[3,256,128]{2,1,0:T(8,128)(2,1)S(1)} %get-tuple-element.12), channel_id=1, source_target_pairs={{1,2},{2,1},{5,6},{6,5},{9,10},{10,9},{13,14},{14,13},{17,18},{18,... | collective-permute-start | bytes 589832 | tf_op jit(solution)/shard_map/ppermute | solution.py:321
  17.1 1.9 %collective-permute-start.1 = (bf16[3,256,128]{2,1,0:T(8,128)(2,1)S(1)}, bf16[3,256,128]{2,1,0:T(8,128)(2,1)S(1)}, u32[]{:S(2)}, u32[]{:S(2)}) collective-permute-start(bf16[3,256,128]{2,1,0:T(8,128)(2,1)S(1)} %get-tuple-element.11), channel_id=1, source_target_pairs={{0,1},{1,0},{2,3},{3,2},{4,5},{5,4},{6,7},{7,6},{8,9},{9,8},{10,11... | collective-permute-start | bytes 589832 | tf_op jit(solution)/shard_map/ppermute | solution.py:321
  19.6 0.0 copy-start
  19.7 0.9 copy-done
  20.6 0.0 copy-start.1
  20.6 1.0 %copy-done.1 = bf16[3,3,128,128]{3,2,1,0:T(8,128)(2,1)S(1)} copy-done((bf16[3,3,128,128]{3,2,1,0:T(8,128)(2,1)S(1)}, bf16[3,3,128,128]{3,2,1,0:T(8,128)(2,1)}, u32[]{:S(2)}) %copy-start.1) | copy-done | bytes 294936
  21.6 0.0 copy-start.5
  21.6 0.8 copy-done.5
  22.3 0.0 copy-start.6
  22.3 0.7 copy-done.6
  23.0 0.0 copy-start.2
  23.0 0.0 copy-start.3
  23.0 0.0 copy-start.4
  23.0 2.5 %prepare.1 = (f32[1792,128]{1,0:T(8,128)S(1)}, bf16[8,256,512]{2,1,0:T(8,128)(2,1)S(1)}, f32[8,8,512]{2,1,0:T(8,128)S(1)}) custom-call(f32[1]{0:T(128)S(6)} %copy.27.scale_ref, bf16[4,256,128]{2,1,0:T(8,128)(2,1)S(1)} %bitcast.46, bf16[3,384,128]{2,1,0:T(8,128)(2,1)S(1)} %bitcast.47, s32[32,128]{1,0:T(8,128)S(1)} %bitcast.53, f32[2,32,128]{2,1,0:T(8,128)S(1)} %bitcast.52), custom_call_target="tpu_custom_call" | custom-call | flops 1000000000 | bytes 4000000 | tf_op jit(solution)/shard_map/prepare/pallas_call | solution.py:66
  25.6 0.0 collective-permute-done.far_ref
  25.6 0.0 collective-permute-done.1.core_ref
  25.6 0.0 copy-done.2
  25.6 0.0 copy-done.3
  25.6 0.0 copy-done.4
  25.6 0.0 copy-start.7
  25.6 0.0 copy-start.8
  25.7 3.1 %features.1 = bf16[1024,128]{1,0:T(8,128)(2,1)} custom-call(s32[1]{0:T(128)} %bitcast.1.pos_ref, bf16[3,256,128]{2,1,0:T(8,128)(2,1)S(1)} %collective-permute-done.far_ref, bf16[3,256,128]{2,1,0:T(8,128)(2,1)S(1)} %collective-permute-done.1.core_ref, bf16[3,384,128]{2,1,0:T(8,128)(2,1)S(1)} %bitcast.48, bf16[3,384,128]{2,1,0:T(8,128)(2,1)S(1)} %bitcast.49, ...), custom_call_target="tpu_custom_call" | custom-call | tf_op jit(solution)/shard_map/features/pallas_call | solution.py:142
  28.7 14.8 %all-to-all-start = ((bf16[128,8,128]{2,1,0:T(8,128)(2,1)}), bf16[128,8,128]{2,1,0:T(8,128)(2,1)S(1)}, u32[]{:S(2)}, u32[]{:S(2)}) async-start(bf16[128,8,128]{2,1,0:T(8,128)(2,1)} %bitcast.12), calls=%async_computation | async-start | bytes 524288 | tf_op jit(solution)/shard_map/all_to_all | solution.py:374
  43.6 0.0 copy-done.7
  43.6 0.0 copy-done.8
  43.6 0.1 slice_bitcast_fusion.1
  43.7 0.2 concatenate.42
  43.9 0.2 concatenate.41
  44.1 0.0 copy-start.9
  44.1 0.2 concatenate.37
  44.3 0.2 concatenate.36
  44.5 0.2 concatenate.39
  44.6 0.2 concatenate.34
  44.8 0.0 copy-done.9
  44.8 0.1 copy.13
  44.9 0.2 reshape_squeeze.3.by_row_ref
  45.1 0.2 copy.14
  45.3 0.1 pad.11.clone
  45.4 18.2 %all-to-all-done = bf16[128,8,128]{2,1,0:T(8,128)(2,1)S(1)} async-done(((bf16[128,8,128]{2,1,0:T(8,128)(2,1)}), bf16[128,8,128]{2,1,0:T(8,128)(2,1)S(1)}, u32[]{:S(2)}, u32[]{:S(2)}) %all-to-all-start) | async-done | bytes 262176 | tf_op jit(solution)/shard_map/all_to_all | solution.py:374
  63.5 1.2 %scatter.1 = bf16[2,128,128]{2,1,0:T(8,128)(2,1)S(1)} custom-call(bf16[1024,128]{1,0:T(8,128)(2,1)S(1)} %bitcast.45, s32[4,1024]{1,0:T(4,128)S(1)} %bitcast.50, s32[1024,4]{1,0:T(8,128)S(1)} %reshape_squeeze.3.by_row_ref), custom_call_target="tpu_custom_call" | custom-call | tf_op jit(solution)/shard_map/scatter/pallas_call | solution.py:176
  64.8 6.2 %collective-permute-start.2 = (bf16[2,32,128]{2,1,0:T(8,128)(2,1)S(1)}, bf16[2,32,128]{2,1,0:T(8,128)(2,1)S(1)}, u32[]{:S(2)}, u32[]{:S(2)}) collective-permute-start(bf16[2,32,128]{2,1,0:T(8,128)(2,1)S(1)} %get-tuple-element.21), channel_id=1, source_target_pairs={{1,2},{2,1},{5,6},{6,5},{9,10},{10,9},{13,14},{14,13},{17,18},{18,... | collective-permute-start | bytes 49160 | tf_op jit(solution)/shard_map/ppermute | solution.py:321
  71.0 1.9 %collective-permute-start.3 = (bf16[2,32,128]{2,1,0:T(8,128)(2,1)S(1)}, bf16[2,32,128]{2,1,0:T(8,128)(2,1)S(1)}, u32[]{:S(2)}, u32[]{:S(2)}) collective-permute-start(bf16[2,32,128]{2,1,0:T(8,128)(2,1)S(1)} %get-tuple-element.22), channel_id=1, source_target_pairs={{0,1},{1,0},{2,3},{3,2},{4,5},{5,4},{6,7},{7,6},{8,9},{9,8},{10,11... | collective-permute-start | bytes 49160 | tf_op jit(solution)/shard_map/ppermute | solution.py:321
  72.9 0.4 pad_maximum_fusion.1
  73.3 5.2 %collective-permute-done.2 = bf16[2,32,128]{2,1,0:T(8,128)(2,1)S(1)} collective-permute-done((bf16[2,32,128]{2,1,0:T(8,128)(2,1)S(1)}, bf16[2,32,128]{2,1,0:T(8,128)(2,1)S(1)}, u32[]{:S(2)}, u32[]{:S(2)}) %collective-permute-start.2) | collective-permute-done | bytes 16416 | tf_op jit(solution)/shard_map/ppermute | solution.py:321
  78.6 0.0 collective-permute-done.3
  78.6 6.2 %collective-permute-start.4 = (bf16[2,192,128]{2,1,0:T(8,128)(2,1)S(1)}, bf16[2,192,128]{2,1,0:T(8,128)(2,1)S(1)}, u32[]{:S(2)}, u32[]{:S(2)}) collective-permute-start(bf16[2,192,128]{2,1,0:T(8,128)(2,1)S(1)} %pad_maximum_fusion.2.own_ref), channel_id=1, source_target_pairs={{4,8},{5,9},{6,10},{7,11},{8,4},{9,5},{10,6},{11,7},{12,16},{13,17... | collective-permute-start | bytes 294920 | tf_op jit(solution)/shard_map/ppermute | solution.py:321
  84.8 1.9 %collective-permute-start.5 = (bf16[2,192,128]{2,1,0:T(8,128)(2,1)S(1)}, bf16[2,192,128]{2,1,0:T(8,128)(2,1)S(1)}, u32[]{:S(2)}, u32[]{:S(2)}) collective-permute-start(bf16[2,192,128]{2,1,0:T(8,128)(2,1)S(1)} %pad_maximum_fusion.2.own_ref), channel_id=1, source_target_pairs={{0,4},{1,5},{2,6},{3,7},{4,0},{5,1},{6,2},{7,3},{8,12},{9,13},{10,... | collective-permute-start | bytes 294920 | tf_op jit(solution)/shard_map/ppermute | solution.py:321
  86.7 0.1 pad_add_fusion.pos_ref
  86.8 0.6 volume_start.1.part_ref
  87.4 4.2 %collective-permute-done.4.next_ref = bf16[2,192,128]{2,1,0:T(8,128)(2,1)S(1)} collective-permute-done((bf16[2,192,128]{2,1,0:T(8,128)(2,1)S(1)}, bf16[2,192,128]{2,1,0:T(8,128)(2,1)S(1)}, u32[]{:S(2)}, u32[]{:S(2)}) %collective-permute-start.4) | collective-permute-done | bytes 98336 | tf_op jit(solution)/shard_map/ppermute | solution.py:321
  91.6 0.3 collective-permute-done.5.near_ref
  91.9 2.1 %volume.1 = bf16[32,1024]{1,0:T(8,128)(2,1)S(1)} custom-call(s32[2]{0:T(128)S(1)} %pad_add_fusion.pos_ref, bf16[2,192,128]{2,1,0:T(8,128)(2,1)S(1)} %pad_maximum_fusion.2.own_ref, bf16[2,192,128]{2,1,0:T(8,128)(2,1)S(1)} %collective-permute-done.4.next_ref, bf16[2,192,128]{2,1,0:T(8,128)(2,1)S(1)} %collective-permute-done.5.near_ref, ...), custom_call_target="tpu_custom_call" | custom-call | tf_op jit(solution)/shard_map/volume/pallas_call | solution.py:286
  94.0 0.7 reshape.34
  (8 shorter events, 0.1 us)
Async XLA Ops:
  1.1 24.5 %collective-permute-start = (bf16[3,256,128]{2,1,0:T(8,128)(2,1)S(1)}, bf16[3,256,128]{2,1,0:T(8,128)(2,1)S(1)}, u32[]{:S(2)}, u32[]{:S(2)}) collective-permute-start(bf16[3,256,128]{2,1,0:T(8,128)(2,1)S(1)} %get-tuple-element.12), channel_id=1, source_target_pairs={{1,2},{2,1},{5,6},{6,5},{9,10},{10,9},{13,14},{14,13},{17,18},{18,... | collective-permute-start | bytes 589832 | tf_op jit(solution)/shard_map/ppermute | solution.py:321
  17.1 8.5 %collective-permute-start.1 = (bf16[3,256,128]{2,1,0:T(8,128)(2,1)S(1)}, bf16[3,256,128]{2,1,0:T(8,128)(2,1)S(1)}, u32[]{:S(2)}, u32[]{:S(2)}) collective-permute-start(bf16[3,256,128]{2,1,0:T(8,128)(2,1)S(1)} %get-tuple-element.11), channel_id=1, source_target_pairs={{0,1},{1,0},{2,3},{3,2},{4,5},{5,4},{6,7},{7,6},{8,9},{9,8},{10,11... | collective-permute-start | bytes 589832 | tf_op jit(solution)/shard_map/ppermute | solution.py:321
  19.6 1.0 %copy-start = (bf16[1,4,256,128]{3,2,1,0:T(8,128)(2,1)S(1)}, bf16[1,4,256,128]{3,2,1,0:T(8,128)(2,1)}, u32[]{:S(2)}) copy-start(bf16[1,4,256,128]{3,2,1,0:T(8,128)(2,1)} %param.10) | copy-start | bytes 786436
  20.6 1.0 %copy-start.1 = (bf16[3,3,128,128]{3,2,1,0:T(8,128)(2,1)S(1)}, bf16[3,3,128,128]{3,2,1,0:T(8,128)(2,1)}, u32[]{:S(2)}) copy-start(bf16[3,3,128,128]{3,2,1,0:T(8,128)(2,1)} %param.11) | copy-start | bytes 884740
  21.6 0.8 copy-start.5
  22.3 0.7 copy-start.6
  23.0 2.6 %copy-start.2 = (bf16[3,3,128,128]{3,2,1,0:T(8,128)(2,1)S(1)}, bf16[3,3,128,128]{3,2,1,0:T(8,128)(2,1)}, u32[]{:S(2)}) copy-start(bf16[3,3,128,128]{3,2,1,0:T(8,128)(2,1)} %param.11) | copy-start | bytes 884740
  23.0 2.6 %copy-start.3 = (bf16[3,3,128,128]{3,2,1,0:T(8,128)(2,1)S(1)}, bf16[3,3,128,128]{3,2,1,0:T(8,128)(2,1)}, u32[]{:S(2)}) copy-start(bf16[3,3,128,128]{3,2,1,0:T(8,128)(2,1)} %param.12) | copy-start | bytes 884740
  23.0 2.6 %copy-start.4 = (bf16[128,32]{0,1:T(8,128)(2,1)S(1)}, bf16[128,32]{0,1:T(8,128)(2,1)}, u32[]{:S(2)}) copy-start(bf16[128,32]{0,1:T(8,128)(2,1)} %param.13) | copy-start | bytes 24580
  25.6 17.9 %copy-start.7 = (bf16[27,32,32]{2,1,0:T(8,128)(2,1)S(1)}, bf16[27,32,32]{2,1,0:T(8,128)(2,1)}, u32[]{:S(2)}) copy-start(bf16[27,32,32]{2,1,0:T(8,128)(2,1)} %param.19) | copy-start | bytes 165892
  25.6 17.9 %copy-start.8 = (bf16[27,32,32]{2,1,0:T(8,128)(2,1)S(1)}, bf16[27,32,32]{2,1,0:T(8,128)(2,1)}, u32[]{:S(2)}) copy-start(bf16[27,32,32]{2,1,0:T(8,128)(2,1)} %param.18) | copy-start | bytes 165892
  28.7 34.8 %all-to-all-start = ((bf16[128,8,128]{2,1,0:T(8,128)(2,1)}), bf16[128,8,128]{2,1,0:T(8,128)(2,1)S(1)}, u32[]{:S(2)}, u32[]{:S(2)}) async-start(bf16[128,8,128]{2,1,0:T(8,128)(2,1)} %bitcast.12), calls=%async_computation | async-start | bytes 524288 | tf_op jit(solution)/shard_map/all_to_all | solution.py:374
  44.1 0.7 copy-start.9
  64.8 13.8 %collective-permute-start.2 = (bf16[2,32,128]{2,1,0:T(8,128)(2,1)S(1)}, bf16[2,32,128]{2,1,0:T(8,128)(2,1)S(1)}, u32[]{:S(2)}, u32[]{:S(2)}) collective-permute-start(bf16[2,32,128]{2,1,0:T(8,128)(2,1)S(1)} %get-tuple-element.21), channel_id=1, source_target_pairs={{1,2},{2,1},{5,6},{6,5},{9,10},{10,9},{13,14},{14,13},{17,18},{18,... | collective-permute-start | bytes 49160 | tf_op jit(solution)/shard_map/ppermute | solution.py:321
  71.0 7.6 %collective-permute-start.3 = (bf16[2,32,128]{2,1,0:T(8,128)(2,1)S(1)}, bf16[2,32,128]{2,1,0:T(8,128)(2,1)S(1)}, u32[]{:S(2)}, u32[]{:S(2)}) collective-permute-start(bf16[2,32,128]{2,1,0:T(8,128)(2,1)S(1)} %get-tuple-element.22), channel_id=1, source_target_pairs={{0,1},{1,0},{2,3},{3,2},{4,5},{5,4},{6,7},{7,6},{8,9},{9,8},{10,11... | collective-permute-start | bytes 49160 | tf_op jit(solution)/shard_map/ppermute | solution.py:321
  78.6 13.0 %collective-permute-start.4 = (bf16[2,192,128]{2,1,0:T(8,128)(2,1)S(1)}, bf16[2,192,128]{2,1,0:T(8,128)(2,1)S(1)}, u32[]{:S(2)}, u32[]{:S(2)}) collective-permute-start(bf16[2,192,128]{2,1,0:T(8,128)(2,1)S(1)} %pad_maximum_fusion.2.own_ref), channel_id=1, source_target_pairs={{4,8},{5,9},{6,10},{7,11},{8,4},{9,5},{10,6},{11,7},{12,16},{13,17... | collective-permute-start | bytes 294920 | tf_op jit(solution)/shard_map/ppermute | solution.py:321
  84.8 7.1 %collective-permute-start.5 = (bf16[2,192,128]{2,1,0:T(8,128)(2,1)S(1)}, bf16[2,192,128]{2,1,0:T(8,128)(2,1)S(1)}, u32[]{:S(2)}, u32[]{:S(2)}) collective-permute-start(bf16[2,192,128]{2,1,0:T(8,128)(2,1)S(1)} %pad_maximum_fusion.2.own_ref), channel_id=1, source_target_pairs={{0,4},{1,5},{2,6},{3,7},{4,0},{5,1},{6,2},{7,3},{8,12},{9,13},{10,... | collective-permute-start | bytes 294920 | tf_op jit(solution)/shard_map/ppermute | solution.py:321

commit v4 on v3

--- a/solution.py
+++ b/solution.py
@@ -36,15 +36,7 @@
     return jnp.concatenate([x[i : i + 1] for i in range(4)], axis=1)
 
 
-def prepare_kernel(scale_ref, img_ref, w1_ref, pix_ref, frac_ref, acc, weights, blends, x1):
-    for i in range(4):
-        put_columns(x1, i, img_ref[i].astype(F32))
-    own = x1[...].reshape(1024, 384)
-    acc[0:512] = jnp.zeros((512, 128), F32)
-    acc[1536:1792] = jnp.zeros((256, 128), F32)
-    acc[512:1536] = dot(own, w1_ref[0])
-    acc[256:1280] += dot(own, w1_ref[1])
-    acc[0:1024] += dot(own, w1_ref[2])
+def sample_weights(scale_ref, pix_ref, frac_ref, weights, blends):
     scale = scale_ref[0]
     col_iota = lax.broadcasted_iota(jnp.int32, (256, 512), 0)
     row_iota = lax.broadcasted_iota(jnp.int32, (8, 512), 0)
@@ -62,6 +54,29 @@
         )
 
 
+def prepare_kernel(
+    scale_ref, img_hbm, w1_hbm, pix_hbm, frac_hbm, acc, weights, blends,
+    x1, img_ref, w1_ref, pix_ref, frac_ref, sems,
+):
+    pairs = ((pix_hbm, pix_ref), (frac_hbm, frac_ref), (img_hbm, img_ref), (w1_hbm, w1_ref))
+    copies = [pltpu.make_async_copy(src, dst, sems.at[i]) for i, (src, dst) in enumerate(pairs)]
+    for copy in copies:
+        copy.start()
+    copies[0].wait()
+    copies[1].wait()
+    sample_weights(scale_ref, pix_ref, frac_ref, weights, blends)
+    copies[2].wait()
+    copies[3].wait()
+    for i in range(4):
+        put_columns(x1, i, img_ref[i].astype(F32))
+    own = x1[...].reshape(1024, 384)
+    acc[0:512] = jnp.zeros((512, 128), F32)
+    acc[1536:1792] = jnp.zeros((256, 128), F32)
+    acc[512:1536] = dot(own, w1_ref[0])
+    acc[256:1280] += dot(own, w1_ref[1])
+    acc[0:1024] += dot(own, w1_ref[2])
+
+
 def prepare(scale, img, w1, pix, frac):
     return pl.pallas_call(
         prepare_kernel,
@@ -70,13 +85,20 @@
             jax.ShapeDtypeStruct((8, 256, 512), BF16),
             jax.ShapeDtypeStruct((8, 8, 512), F32),
         ),
-        in_specs=[whole(pltpu.SMEM)] + [whole(pltpu.VMEM)] * 4,
+        in_specs=[whole(pltpu.SMEM)] + [whole(pltpu.HBM)] * 4,
         out_specs=(whole(pltpu.VMEM),) * 3,
-        scratch_shapes=[pltpu.VMEM((4, 256, 384), BF16)],
+        scratch_shapes=[
+            pltpu.VMEM((4, 256, 384), BF16),
+            pltpu.VMEM((4, 256, 128), BF16),
+            pltpu.VMEM((3, 384, 128), BF16),
+            pltpu.VMEM((32, 128), jnp.int32),
+            pltpu.VMEM((2, 32, 128), F32),
+            pltpu.SemaphoreType.DMA((4,)),
+        ],
         compiler_params=pltpu.CompilerParams(vmem_limit_bytes=24 * 2**20),
         cost_estimate=pl.CostEstimate(flops=10**9, bytes_accessed=4 * 10**6, transcendentals=0),
         name="prepare",
-    )(scale, img, w1, pix, frac)
+    )(scale, *(pltpu.with_memory_space_constraint(x, pltpu.HBM) for x in (img, w1, pix, frac)))
 
 
 def features_kernel(
@@ -155,32 +177,68 @@
     )(slab, far, core, w1, w2, wr, part, weights, blends)
 
 
-def scatter_kernel(val_ref, by_lane_ref, by_row_ref, out_ref):
+def slots_kernel(by_lane_ref, one_hot):
+    lo_iota = lax.broadcasted_iota(jnp.int32, (256, 1024), 0)
+    for s in range(4):
+        hit = lo_iota == (by_lane_ref[s : s + 1] >> 2)
+        one_hot[:, 1024 * s : 1024 * s + 1024] = jnp.where(hit, 1.0, 0.0).astype(BF16)
+
+
+def slots(by_lane):
+    return pl.pallas_call(
+        slots_kernel,
+        out_shape=jax.ShapeDtypeStruct((256, 4096), BF16),
+        in_specs=[whole(pltpu.VMEM)],
+        out_specs=whole(pltpu.VMEM),
+        compiler_params=pltpu.CompilerParams(vmem_limit_bytes=16 * 2**20),
+        cost_estimate=pl.CostEstimate(flops=10**7, bytes_accessed=2 * 10**6, transcendentals=0),
+        name="slots",
+    )(by_lane)
+
+
+def spread_kernel(pos_ref, val_ref, one_hot, by_row_ref, spread, facing):
+    start = pl.multiple_of((pos_ref[0] % 2) * 96, 32)
     val = val_ref[...]
-    lo_iota = lax.broadcasted_iota(jnp.int32, (256, 1024), 0)
     hi_iota = lax.broadcasted_iota(jnp.int32, (1024, 128), 1) // 32
     sel_row = lax.broadcasted_iota(jnp.int32, (128, 128), 0)
     sel_col = lax.broadcasted_iota(jnp.int32, (128, 128), 1) % 32
-    total = jnp.zeros((256, 128), F32)
     for s in range(4):
-        one_hot = jnp.where(lo_iota == (by_lane_ref[s : s + 1] >> 2), 1.0, 0.0).astype(BF16)
         select = jnp.where(sel_row == sel_col + 32 * s, 1.0, 0.0).astype(BF16)
-        spread = dot(val, select)
-        hi = by_row_ref[:, s : s + 1] & 3
-        spread = jnp.where(hi_iota == hi, spread, 0.0).astype(BF16)
-        total = total + dot(one_hot, spread)
-    out_ref[...] = total.reshape(2, 128, 128).astype(BF16)
-
-
-def scatter(val, by_lane, by_row):
+        block = hi_iota == (by_row_ref[:, s : s + 1] & 3)
+        spread[1024 * s : 1024 * s + 1024] = jnp.where(block, dot(val, select), 0.0).astype(BF16)
+    for i in range(2):
+        rows = one_hot[pl.ds(128 * i + start, 32), :]
+        facing[i] = dot(rows, spread[...]).astype(BF16)
+
+
+def spread_values(slab, val, one_hot, by_row):
+    return pl.pallas_call(
+        spread_kernel,
+        out_shape=(
+            jax.ShapeDtypeStruct((4096, 128), BF16),
+            jax.ShapeDtypeStruct((2, 32, 128), BF16),
+        ),
+        in_specs=[whole(pltpu.SMEM)] + [whole(pltpu.VMEM)] * 3,
+        out_specs=(whole(pltpu.VMEM),) * 2,
+        compiler_params=pltpu.CompilerParams(vmem_limit_bytes=16 * 2**20),
+        name="spread",
+    )(slab, val, one_hot, by_row)
+
+
+def scatter_kernel(one_hot, spread, out_ref):
+    out_ref[...] = dot(one_hot[...], spread[...]).reshape(2, 128, 128).astype(BF16)
+
+
+def scatter(one_hot, spread):
     return pl.pallas_call(
         scatter_kernel,
         out_shape=jax.ShapeDtypeStruct((2, 128, 128), BF16),
-        in_specs=[whole(pltpu.VMEM)] * 3,
+        in_specs=[whole(pltpu.VMEM)] * 2,
         out_specs=whole(pltpu.VMEM),
-        compiler_params=pltpu.CompilerParams(vmem_limit_bytes=40 * 2**20),
+        compiler_params=pltpu.CompilerParams(vmem_limit_bytes=16 * 2**20),
+        cost_estimate=pl.CostEstimate(flops=3 * 10**8, bytes_accessed=3 * 10**6, transcendentals=0),
         name="scatter",
-    )(val, by_lane, by_row)
+    )(one_hot, spread)
 
 
 def put_depth(dst, plane, x):
@@ -226,7 +284,7 @@
 
 
 def volume_kernel(
-    pos_ref, own_ref, next_ref, near_ref, part_ref, w1_ref, w2_ref, out_ref, x1, x2, acc
+    pos_ref, own_ref, next_ref, near_ref, part_ref, w1_ref, w2_ref, out_ref, x1, x2, acc, packed
 ):
     p = pos_ref[0]
     q = pos_ref[1]
@@ -266,31 +324,28 @@
             acc[...] = part
         else:
             acc[...] += part
-    place_row = lax.broadcasted_iota(jnp.int32, (128, 512), 0) * 4
-    place_col = lax.broadcasted_iota(jnp.int32, (128, 512), 1)
-    both = []
     for i in range(2):
         res = acc[i * 128 : (i + 1) * 128] + own_ref[i, 32:160].astype(F32)
-        both.append(res.T.astype(BF16))
-    total = [None, None]
-    for z in range(4):
-        place = jnp.where(place_col == place_row + z, 1.0, 0.0).astype(BF16)
-        rows = jnp.concatenate([b[32 * z : 32 * z + 32] for b in both], axis=0)
-        part = dot(rows, place)
-        total = part if z == 0 else total + part
-    for i in range(2):
-        out_ref[:, 512 * i : 512 * i + 512] = total[32 * i : 32 * i + 32].astype(BF16)
+        res = res.T
+        for k in range(4):
+            block = [res[32 * z : 32 * z + 32, 32 * k : 32 * k + 32] for z in range(4)]
+            packed[pl.ds(2 * k + i, 32, stride=8), :] = jnp.concatenate(block, axis=1)
+    source = lax.broadcasted_iota(jnp.int32, (128, 128), 0)
+    target = lax.broadcasted_iota(jnp.int32, (128, 128), 1)
+    place = jnp.where(target == (source % 32) * 4 + source // 32, 1.0, 0.0).astype(BF16)
+    out_ref[...] = dot(packed[...].astype(BF16), place).astype(BF16)
 
 
 def volume_convs(pos, own, nxt, near, part, w1, w2):
     return pl.pallas_call(
         volume_kernel,
-        out_shape=jax.ShapeDtypeStruct((32, 1024), BF16),
+        out_shape=jax.ShapeDtypeStruct((256, 128), BF16),
         in_specs=[whole(pltpu.SMEM)] + [whole(pltpu.VMEM)] * 6,
         out_specs=whole(pltpu.VMEM),
         scratch_shapes=[
             pltpu.VMEM((4, 192, 256), BF16),
             pltpu.VMEM((4, 160, 256), BF16),
+            pltpu.VMEM((256, 128), F32),
             pltpu.VMEM((256, 128), F32),
         ],
         compiler_params=pltpu.CompilerParams(vmem_limit_bytes=32 * 2**20),
@@ -372,11 +427,13 @@
     part, weights, blends = prepare(cam_weight, img, w1, pix, frac)
     sent = features(slab_pos, far, core, w1, w2, w_reduce.T, part, weights, blends)
     got = lax.all_to_all(sent.reshape(128, 8, 128), AXES, 0, 0, tiled=True).reshape(1024, 128)
-    volume = scatter(got, by_lane, by_row)
+    one_hot = slots(by_lane)
+    spread, facing = spread_values(slab_pos, got, one_hot, by_row)
+    far = swap(facing, far_partner, cams, slabs)
+    volume = scatter(one_hot, spread)
 
     pos = jnp.stack([p, s]).astype(jnp.int32)
     top, bottom = volume[:, 0:32], volume[:, 96:128]
-    far = swap(jnp.where(even, top, bottom), far_partner, cams, slabs)
     core = swap(jnp.where(even, bottom, top), core_partner, cams, slabs)
     above = jnp.where(even, far, core)
     below = jnp.where(even, core, far)
@@ -385,7 +442,7 @@
     near = swap(own, near_partner, cams, slabs)
     part = volume_start(own, band1)
     out = volume_convs(pos, own, nxt, near, part, band1, band2)
-    return out.reshape(32, 2, 512)
+    return out.reshape(32, 4, 2, 128).transpose(0, 2, 1, 3).reshape(32, 2, 512)
 
 
 def solution(mesh):

time: 95.2 us -> 95.2 us (level)
  waiting for transfers between devices: 27.8 us -> 23.9 us
  starting transfers between devices: 48.9 us -> 52.5 us
  Pallas kernels: 9.57 us -> 10.9 us
    all_to_all x1, waiting for transfers between devices: 18.2 us -> 14.5 us  [local(): lax.all_to_all(sent.reshape(128, 8, 128), AXES, 0, 0, tiled=True)]
    all_to_all x1, starting transfers between devices: 14.8 us -> 18.4 us  [local(): lax.all_to_all(sent.reshape(128, 8, 128), AXES, 0, 0, tiled=True)]
    unnamed x21 -> x23, local copies, waits for them, and re-layouts: 3.51 us -> 0.15 us
    concatenate x7, local copies, waits for them, and re-layouts: 1.11 us -> 4.42 us  [banded(): rows.append(jnp.concatenate(blocks, axis=2))]
    pallas_call x1 -> x3, Pallas kernels: 2.11 us -> 4.11 us  [the longest x1 2.72 us: volume_convs(): pl.pallas_call(volume_kernel, out_shape=jax.ShapeDtypeStruct((256, 128),...]
  transfers between devices with their start and end apart: 7 -> 7, of which waited for: 4 -> 4; matrix products, arithmetic and copies ran while one was open for 2% -> 6% of each run, Pallas kernels for 3% -> 4%
where the time goes in v4:
time: 95.2 us; the launch traced here: 94.8 us
  starting transfers between devices  52.5 us (55%)
  waiting for transfers between devices  23.9 us (25%)
  Pallas kernels  10.9 us (11%)
  local copies, waits for them, and re-layouts  5.05 us (5%)
  other arithmetic  1.57 us (2%)
  between operations  0.99 us (1%)
    ppermute x6, starting transfers between devices, swap(): return lax.ppermute(x, AXES, pairs)  34.1 us
    all_to_all x1, starting transfers between devices, local(): lax.all_to_all(sent.reshape(128, 8, 128), AXES, 0, 0, tiled=True)  18.4 us
    all_to_all x1, waiting for transfers between devices, local(): lax.all_to_all(sent.reshape(128, 8, 128), AXES, 0, 0, tiled=True)  14.5 us
    ppermute x6, waiting for transfers between devices, swap(): return lax.ppermute(x, AXES, pairs)  9.33 us
    concatenate x7, local copies, waits for them, and re-layouts, banded(): rows.append(jnp.concatenate(blocks, axis=2))  4.42 us
    pallas_call x1, Pallas kernels, features(): pl.pallas_call(features_kernel, out_shape=jax.ShapeDtypeStruct((1024, 128...  3.07 us
    pallas_call x1, Pallas kernels, volume_convs(): pl.pallas_call(volume_kernel, out_shape=jax.ShapeDtypeStruct((256, 128),...  2.72 us
    pallas_call x1, Pallas kernels, prepare(): pl.pallas_call(prepare_kernel, out_shape=(jax.ShapeDtypeStruct((1792, 128...  2.35 us
  transfers between devices with their start and end apart: 7, of which 4 were waited for; matrix products, arithmetic and copies ran while one was open for 6% of the time, Pallas kernels for 4%

profile of v4, /device:TPU:27, one launch (start us, length us, event | category | flops | bytes accessed | tf_op | source)
XLA Modules:
  0.0 94.8 jit_solution(12496771019619556221)
XLA Ops:
  0.0 1.1 %select_bitcast_fusion = (bf16[3,256,128]{2,1,0:T(8,128)(2,1)S(1)}, bf16[3,256,128]{2,1,0:T(8,128)(2,1)S(1)}) fusion(pred[]{:T(512)S(6)} %eq.5, bf16[1,4,256,128]{3,2,1,0:T(8,128)(2,1)} %param.10), kind=kLoop, calls=%fused_computation.2 | loop fusion | flops 196608 | bytes 786433 | tf_op jit(solution)/shard_map/jit(_where)/select_n | solution.py:415
  1.1 16.0 %collective-permute-start = (bf16[3,256,128]{2,1,0:T(8,128)(2,1)S(1)}, bf16[3,256,128]{2,1,0:T(8,128)(2,1)S(1)}, u32[]{:S(2)}, u32[]{:S(2)}) collective-permute-start(bf16[3,256,128]{2,1,0:T(8,128)(2,1)S(1)} %get-tuple-element.16), channel_id=1, source_target_pairs={{1,2},{2,1},{5,6},{6,5},{9,10},{10,9},{13,14},{14,13},{17,18},{18,... | collective-permute-start | bytes 589832 | tf_op jit(solution)/shard_map/ppermute | solution.py:376
  17.1 1.9 %collective-permute-start.1 = (bf16[3,256,128]{2,1,0:T(8,128)(2,1)S(1)}, bf16[3,256,128]{2,1,0:T(8,128)(2,1)S(1)}, u32[]{:S(2)}, u32[]{:S(2)}) collective-permute-start(bf16[3,256,128]{2,1,0:T(8,128)(2,1)S(1)} %get-tuple-element.15), channel_id=1, source_target_pairs={{0,1},{1,0},{2,3},{3,2},{4,5},{5,4},{6,7},{7,6},{8,9},{9,8},{10,11... | collective-permute-start | bytes 589832 | tf_op jit(solution)/shard_map/ppermute | solution.py:376
  19.6 0.0 copy-start
  19.7 0.0 copy-start.1
  19.7 0.0 copy-start.2
  19.7 2.4 %prepare.1 = (f32[1792,128]{1,0:T(8,128)S(1)}, bf16[8,256,512]{2,1,0:T(8,128)(2,1)S(1)}, f32[8,8,512]{2,1,0:T(8,128)S(1)}) custom-call(f32[1]{0:T(128)S(6)} %copy.29.scale_ref, bf16[4,256,128]{2,1,0:T(8,128)(2,1)} %bitcast.56, bf16[3,384,128]{2,1,0:T(8,128)(2,1)} %bitcast.51, s32[32,128]{1,0:T(8,128)} %bitcast.60, f32[2,32,128]{2,1,0:T(8,128)} %bitcast.59), custom_call_target="tpu_custom_call" | custom-call | flops 1000000000 | bytes 4000000 | tf_op jit(solution)/shard_map/prepare/pallas_call | solution.py:81
  22.0 0.0 collective-permute-done.far_ref
  22.0 0.0 collective-permute-done.1.core_ref
  22.1 0.0 copy-done
  22.1 0.0 copy-done.1
  22.1 0.0 copy-done.2
  22.1 0.0 copy-start.8
  22.1 0.0 copy-start.9
  22.1 3.1 %features.1 = bf16[1024,128]{1,0:T(8,128)(2,1)} custom-call(s32[1]{0:T(128)} %bitcast.1.pos_ref, bf16[3,256,128]{2,1,0:T(8,128)(2,1)S(1)} %collective-permute-done.far_ref, bf16[3,256,128]{2,1,0:T(8,128)(2,1)S(1)} %collective-permute-done.1.core_ref, bf16[3,384,128]{2,1,0:T(8,128)(2,1)S(1)} %bitcast.52, bf16[3,384,128]{2,1,0:T(8,128)(2,1)S(1)} %bitcast.53, ...), custom_call_target="tpu_custom_call" | custom-call | tf_op jit(solution)/shard_map/features/pallas_call | solution.py:164
  25.2 18.4 %all-to-all-start = ((bf16[128,8,128]{2,1,0:T(8,128)(2,1)}), bf16[128,8,128]{2,1,0:T(8,128)(2,1)S(1)}, u32[]{:S(2)}, u32[]{:S(2)}) async-start(bf16[128,8,128]{2,1,0:T(8,128)(2,1)} %bitcast.12), calls=%async_computation | async-start | bytes 524288 | tf_op jit(solution)/shard_map/all_to_all | solution.py:429
  43.6 0.0 copy-done.8
  43.6 0.0 copy-done.9
  43.6 0.1 slice_bitcast_fusion.1
  43.7 0.2 concatenate.42
  43.9 0.8 concatenate.41
  44.7 0.0 copy-start.10
  44.7 0.9 concatenate.37
  45.6 0.8 concatenate.36
  46.4 0.8 concatenate.39
  47.3 0.8 concatenate.34
  48.1 0.0 copy-done.10
  48.1 0.1 copy.14
  48.2 0.2 reshape_squeeze.3.by_row_ref
  48.4 0.2 copy.15
  48.6 0.1 pad.11.clone
  48.6 0.4 slots.1.one_hot
  49.0 14.5 %all-to-all-done = bf16[128,8,128]{2,1,0:T(8,128)(2,1)S(1)} async-done(((bf16[128,8,128]{2,1,0:T(8,128)(2,1)}), bf16[128,8,128]{2,1,0:T(8,128)(2,1)S(1)}, u32[]{:S(2)}, u32[]{:S(2)}) %all-to-all-start) | async-done | bytes 262176 | tf_op jit(solution)/shard_map/all_to_all | solution.py:429
  63.6 1.0 %spread.1 = (bf16[4096,128]{1,0:T(8,128)(2,1)S(1)}, bf16[2,32,128]{2,1,0:T(8,128)(2,1)S(1)}) custom-call(s32[1]{0:T(128)} %bitcast.1.pos_ref, bf16[1024,128]{1,0:T(8,128)(2,1)S(1)} %bitcast.50, bf16[256,4096]{1,0:T(8,128)(2,1)S(1)} %slots.1.one_hot, s32[1024,4]{1,0:T(8,128)S(1)} %reshape_squeeze.3.by_row_ref), custom_call_target="tpu_custom_call" | custom-call | tf_op jit(solution)/shard_map/spread/pallas_call | solution.py:215
  64.6 6.2 %collective-permute-start.2 = (bf16[2,32,128]{2,1,0:T(8,128)(2,1)S(1)}, bf16[2,32,128]{2,1,0:T(8,128)(2,1)S(1)}, u32[]{:S(2)}, u32[]{:S(2)}) collective-permute-start(bf16[2,32,128]{2,1,0:T(8,128)(2,1)S(1)} %get-tuple-element.13), channel_id=1, source_target_pairs={{1,2},{2,1},{5,6},{6,5},{9,10},{10,9},{13,14},{14,13},{17,18},{18,... | collective-permute-start | bytes 49160 | tf_op jit(solution)/shard_map/ppermute | solution.py:376
  70.8 0.0 copy-start.3
  70.8 0.0 copy-start.4
  70.8 0.0 copy-start.5
  70.8 0.0 copy-start.6
  70.8 0.0 copy-start.7
  70.8 0.7 scatter.1
  71.6 1.9 %collective-permute-start.3 = (bf16[2,32,128]{2,1,0:T(8,128)(2,1)S(1)}, bf16[2,32,128]{2,1,0:T(8,128)(2,1)S(1)}, u32[]{:S(2)}, u32[]{:S(2)}) collective-permute-start(bf16[2,32,128]{2,1,0:T(8,128)(2,1)S(1)} %slice_select_fusion), channel_id=1, source_target_pairs={{0,1},{1,0},{2,3},{3,2},{4,5},{5,4},{6,7},{7,6},{8,9},{9,8},{10,11... | collective-permute-start | bytes 49160 | tf_op jit(solution)/shard_map/ppermute | solution.py:376
  73.5 0.0 copy-done.3
  73.5 0.0 copy-done.4
  73.5 0.0 copy-done.5
  73.5 0.0 copy-done.6
  73.5 0.0 copy-done.7
  73.5 0.4 pad_maximum_fusion.1
  74.0 4.4 %collective-permute-done.2 = bf16[2,32,128]{2,1,0:T(8,128)(2,1)S(1)} collective-permute-done((bf16[2,32,128]{2,1,0:T(8,128)(2,1)S(1)}, bf16[2,32,128]{2,1,0:T(8,128)(2,1)S(1)}, u32[]{:S(2)}, u32[]{:S(2)}) %collective-permute-start.2) | collective-permute-done | bytes 16416 | tf_op jit(solution)/shard_map/ppermute | solution.py:376
  78.4 0.0 collective-permute-done.3
  78.4 6.2 %collective-permute-start.4 = (bf16[2,192,128]{2,1,0:T(8,128)(2,1)S(1)}, bf16[2,192,128]{2,1,0:T(8,128)(2,1)S(1)}, u32[]{:S(2)}, u32[]{:S(2)}) collective-permute-start(bf16[2,192,128]{2,1,0:T(8,128)(2,1)S(1)} %pad_maximum_fusion.2.own_ref), channel_id=1, source_target_pairs={{4,8},{5,9},{6,10},{7,11},{8,4},{9,5},{10,6},{11,7},{12,16},{13,17... | collective-permute-start | bytes 294920 | tf_op jit(solution)/shard_map/ppermute | solution.py:376
  84.6 1.9 %collective-permute-start.5 = (bf16[2,192,128]{2,1,0:T(8,128)(2,1)S(1)}, bf16[2,192,128]{2,1,0:T(8,128)(2,1)S(1)}, u32[]{:S(2)}, u32[]{:S(2)}) collective-permute-start(bf16[2,192,128]{2,1,0:T(8,128)(2,1)S(1)} %pad_maximum_fusion.2.own_ref), channel_id=1, source_target_pairs={{0,4},{1,5},{2,6},{3,7},{4,0},{5,1},{6,2},{7,3},{8,12},{9,13},{10,... | collective-permute-start | bytes 294920 | tf_op jit(solution)/shard_map/ppermute | solution.py:376
  86.5 0.1 pad_add_fusion.pos_ref
  86.6 0.6 volume_start.1.part_ref
  87.2 4.2 %collective-permute-done.4.next_ref = bf16[2,192,128]{2,1,0:T(8,128)(2,1)S(1)} collective-permute-done((bf16[2,192,128]{2,1,0:T(8,128)(2,1)S(1)}, bf16[2,192,128]{2,1,0:T(8,128)(2,1)S(1)}, u32[]{:S(2)}, u32[]{:S(2)}) %collective-permute-start.4) | collective-permute-done | bytes 98336 | tf_op jit(solution)/shard_map/ppermute | solution.py:376
  91.4 0.7 collective-permute-done.5.near_ref
  92.1 2.7 %volume.1 = bf16[256,128]{1,0:T(8,128)(2,1)} custom-call(s32[2]{0:T(128)S(1)} %pad_add_fusion.pos_ref, bf16[2,192,128]{2,1,0:T(8,128)(2,1)S(1)} %pad_maximum_fusion.2.own_ref, bf16[2,192,128]{2,1,0:T(8,128)(2,1)S(1)} %collective-permute-done.4.next_ref, bf16[2,192,128]{2,1,0:T(8,128)(2,1)S(1)} %collective-permute-done.5.near_ref, ...), custom_call_target="tpu_custom_call" | custom-call | tf_op jit(solution)/shard_map/volume/pallas_call | solution.py:340
  (8 shorter events, 0.1 us)
Async XLA Ops:
  1.1 21.0 %collective-permute-start = (bf16[3,256,128]{2,1,0:T(8,128)(2,1)S(1)}, bf16[3,256,128]{2,1,0:T(8,128)(2,1)S(1)}, u32[]{:S(2)}, u32[]{:S(2)}) collective-permute-start(bf16[3,256,128]{2,1,0:T(8,128)(2,1)S(1)} %get-tuple-element.16), channel_id=1, source_target_pairs={{1,2},{2,1},{5,6},{6,5},{9,10},{10,9},{13,14},{14,13},{17,18},{18,... | collective-permute-start | bytes 589832 | tf_op jit(solution)/shard_map/ppermute | solution.py:376
  17.1 5.0 %collective-permute-start.1 = (bf16[3,256,128]{2,1,0:T(8,128)(2,1)S(1)}, bf16[3,256,128]{2,1,0:T(8,128)(2,1)S(1)}, u32[]{:S(2)}, u32[]{:S(2)}) collective-permute-start(bf16[3,256,128]{2,1,0:T(8,128)(2,1)S(1)} %get-tuple-element.15), channel_id=1, source_target_pairs={{0,1},{1,0},{2,3},{3,2},{4,5},{5,4},{6,7},{7,6},{8,9},{9,8},{10,11... | collective-permute-start | bytes 589832 | tf_op jit(solution)/shard_map/ppermute | solution.py:376
  19.6 2.4 %copy-start = (bf16[3,3,128,128]{3,2,1,0:T(8,128)(2,1)S(1)}, bf16[3,3,128,128]{3,2,1,0:T(8,128)(2,1)}, u32[]{:S(2)}) copy-start(bf16[3,3,128,128]{3,2,1,0:T(8,128)(2,1)} %param.11) | copy-start | bytes 884740
  19.7 2.4 %copy-start.1 = (bf16[3,3,128,128]{3,2,1,0:T(8,128)(2,1)S(1)}, bf16[3,3,128,128]{3,2,1,0:T(8,128)(2,1)}, u32[]{:S(2)}) copy-start(bf16[3,3,128,128]{3,2,1,0:T(8,128)(2,1)} %param.12) | copy-start | bytes 884740
  19.7 2.4 %copy-start.2 = (bf16[128,32]{0,1:T(8,128)(2,1)S(1)}, bf16[128,32]{0,1:T(8,128)(2,1)}, u32[]{:S(2)}) copy-start(bf16[128,32]{0,1:T(8,128)(2,1)} %param.13) | copy-start | bytes 24580
  22.1 21.5 %copy-start.8 = (bf16[27,32,32]{2,1,0:T(8,128)(2,1)S(1)}, bf16[27,32,32]{2,1,0:T(8,128)(2,1)}, u32[]{:S(2)}) copy-start(bf16[27,32,32]{2,1,0:T(8,128)(2,1)} %param.19) | copy-start | bytes 165892
  22.1 21.5 %copy-start.9 = (bf16[27,32,32]{2,1,0:T(8,128)(2,1)S(1)}, bf16[27,32,32]{2,1,0:T(8,128)(2,1)}, u32[]{:S(2)}) copy-start(bf16[27,32,32]{2,1,0:T(8,128)(2,1)} %param.18) | copy-start | bytes 165892
  25.2 38.4 %all-to-all-start = ((bf16[128,8,128]{2,1,0:T(8,128)(2,1)}), bf16[128,8,128]{2,1,0:T(8,128)(2,1)S(1)}, u32[]{:S(2)}, u32[]{:S(2)}) async-start(bf16[128,8,128]{2,1,0:T(8,128)(2,1)} %bitcast.12), calls=%async_computation | async-start | bytes 524288 | tf_op jit(solution)/shard_map/all_to_all | solution.py:429
  44.7 3.3 %copy-start.10 = (s32[1,128,32]{1,2,0:T(8,128)S(1)}, s32[1,128,32]{1,2,0:T(8,128)}, u32[]{:S(2)}) copy-start(s32[1,128,32]{1,2,0:T(8,128)} %param.17) | copy-start | bytes 49156
  64.6 13.8 %collective-permute-start.2 = (bf16[2,32,128]{2,1,0:T(8,128)(2,1)S(1)}, bf16[2,32,128]{2,1,0:T(8,128)(2,1)S(1)}, u32[]{:S(2)}, u32[]{:S(2)}) collective-permute-start(bf16[2,32,128]{2,1,0:T(8,128)(2,1)S(1)} %get-tuple-element.13), channel_id=1, source_target_pairs={{1,2},{2,1},{5,6},{6,5},{9,10},{10,9},{13,14},{14,13},{17,18},{18,... | collective-permute-start | bytes 49160 | tf_op jit(solution)/shard_map/ppermute | solution.py:376
  70.8 2.7 %copy-start.3 = (bf16[9,32,256]{2,1,0:T(8,128)(2,1)S(1)}, bf16[9,32,256]{2,1,0:T(8,128)(2,1)}, u32[]{:S(2)}) copy-start(bf16[9,32,256]{2,1,0:T(8,128)(2,1)} %concatenate.41) | copy-start | bytes 442372
  70.8 2.7 %copy-start.4 = (bf16[9,32,256]{2,1,0:T(8,128)(2,1)S(1)}, bf16[9,32,256]{2,1,0:T(8,128)(2,1)}, u32[]{:S(2)}) copy-start(bf16[9,32,256]{2,1,0:T(8,128)(2,1)} %concatenate.37) | copy-start | bytes 442372
  70.8 2.7 %copy-start.5 = (bf16[9,32,256]{2,1,0:T(8,128)(2,1)S(1)}, bf16[9,32,256]{2,1,0:T(8,128)(2,1)}, u32[]{:S(2)}) copy-start(bf16[9,32,256]{2,1,0:T(8,128)(2,1)} %concatenate.36) | copy-start | bytes 442372
  70.8 2.7 %copy-start.6 = (bf16[9,32,256]{2,1,0:T(8,128)(2,1)S(1)}, bf16[9,32,256]{2,1,0:T(8,128)(2,1)}, u32[]{:S(2)}) copy-start(bf16[9,32,256]{2,1,0:T(8,128)(2,1)} %concatenate.39) | copy-start | bytes 442372
  70.8 2.7 %copy-start.7 = (bf16[9,32,256]{2,1,0:T(8,128)(2,1)S(1)}, bf16[9,32,256]{2,1,0:T(8,128)(2,1)}, u32[]{:S(2)}) copy-start(bf16[9,32,256]{2,1,0:T(8,128)(2,1)} %concatenate.34) | copy-start | bytes 442372
  71.6 6.8 %collective-permute-start.3 = (bf16[2,32,128]{2,1,0:T(8,128)(2,1)S(1)}, bf16[2,32,128]{2,1,0:T(8,128)(2,1)S(1)}, u32[]{:S(2)}, u32[]{:S(2)}) collective-permute-start(bf16[2,32,128]{2,1,0:T(8,128)(2,1)S(1)} %slice_select_fusion), channel_id=1, source_target_pairs={{0,1},{1,0},{2,3},{3,2},{4,5},{5,4},{6,7},{7,6},{8,9},{9,8},{10,11... | collective-permute-start | bytes 49160 | tf_op jit(solution)/shard_map/ppermute | solution.py:376
  78.4 13.0 %collective-permute-start.4 = (bf16[2,192,128]{2,1,0:T(8,128)(2,1)S(1)}, bf16[2,192,128]{2,1,0:T(8,128)(2,1)S(1)}, u32[]{:S(2)}, u32[]{:S(2)}) collective-permute-start(bf16[2,192,128]{2,1,0:T(8,128)(2,1)S(1)} %pad_maximum_fusion.2.own_ref), channel_id=1, source_target_pairs={{4,8},{5,9},{6,10},{7,11},{8,4},{9,5},{10,6},{11,7},{12,16},{13,17... | collective-permute-start | bytes 294920 | tf_op jit(solution)/shard_map/ppermute | solution.py:376
  84.6 7.6 %collective-permute-start.5 = (bf16[2,192,128]{2,1,0:T(8,128)(2,1)S(1)}, bf16[2,192,128]{2,1,0:T(8,128)(2,1)S(1)}, u32[]{:S(2)}, u32[]{:S(2)}) collective-permute-start(bf16[2,192,128]{2,1,0:T(8,128)(2,1)S(1)} %pad_maximum_fusion.2.own_ref), channel_id=1, source_target_pairs={{0,4},{1,5},{2,6},{3,7},{4,0},{5,1},{6,2},{7,3},{8,12},{9,13},{10,... | collective-permute-start | bytes 294920 | tf_op jit(solution)/shard_map/ppermute | solution.py:376

commit v5 on v4

--- a/solution.py
+++ b/solution.py
@@ -96,61 +96,122 @@
             pltpu.SemaphoreType.DMA((4,)),
         ],
         compiler_params=pltpu.CompilerParams(vmem_limit_bytes=24 * 2**20),
-        cost_estimate=pl.CostEstimate(flops=10**9, bytes_accessed=4 * 10**6, transcendentals=0),
+        cost_estimate=pl.CostEstimate(flops=10000000000, bytes_accessed=4 * 10**6, transcendentals=0),
         name="prepare",
     )(scale, *(pltpu.with_memory_space_constraint(x, pltpu.HBM) for x in (img, w1, pix, frac)))
 
 
+def table_rows(acc, at, count, wr):
+    rows = []
+    for i in range(at, at + count):
+        h = jnp.maximum(acc[i * 256 : (i + 1) * 256], 0.0)
+        rows.append(dot_nt(wr, h.astype(BF16)))
+    return rows
+
+
+def middle_kernel(pos_ref, core_ref, w1_ref, w2_ref, wr_ref, part_ref, inner, table, x1, x2, acc):
+    @pl.when(pos_ref[0] % 2 == 0)
+    def _():
+        for i in range(3):
+            put_columns(x1, i, core_ref[i].astype(F32))
+        tail0 = dot(x1[0], w1_ref[0])
+        tail1 = dot(x1[0:2].reshape(512, 384), w1_ref[1])
+        tail2 = dot(x1[0:3].reshape(768, 384), w1_ref[2])
+        for i in range(2, 7):
+            h = part_ref[i * 256 : (i + 1) * 256]
+            if i == 4:
+                h = h + tail2[0:256]
+            elif i == 5:
+                h = h + tail2[256:512] + tail1[0:256]
+            elif i == 6:
+                h = h + tail2[512:768] + tail1[256:512] + tail0
+            put_columns(x2, i - 2, jnp.maximum(h, 0.0))
+        inner[...] = x2[0:2]
+        acc[...] = dot(x2[0:3].reshape(768, 384), w2_ref[0])
+        acc[...] += dot(x2[1:4].reshape(768, 384), w2_ref[1])
+        acc[...] += dot(x2[2:5].reshape(768, 384), w2_ref[2])
+        table[...] = jnp.concatenate(table_rows(acc, 0, 3, wr_ref[...]), axis=0).astype(BF16)
+
+
+def middle(slab, core, w1, w2, wr, part):
+    return pl.pallas_call(
+        middle_kernel,
+        out_shape=(
+            jax.ShapeDtypeStruct((2, 256, 384), BF16),
+            jax.ShapeDtypeStruct((96, 256), BF16),
+        ),
+        in_specs=[whole(pltpu.SMEM)] + [whole(pltpu.VMEM)] * 5,
+        out_specs=(whole(pltpu.VMEM),) * 2,
+        scratch_shapes=[
+            pltpu.VMEM((3, 256, 384), BF16),
+            pltpu.VMEM((5, 256, 384), BF16),
+            pltpu.VMEM((768, 128), F32),
+        ],
+        compiler_params=pltpu.CompilerParams(vmem_limit_bytes=24 * 2**20),
+        cost_estimate=pl.CostEstimate(flops=1000000, bytes_accessed=10**3, transcendentals=0),
+        name="middle",
+    )(slab, core, w1, w2, wr, part)
+
+
 def features_kernel(
-    pos_ref, far_ref, core_ref, w1_ref, w2_ref, wr_ref, part_ref, weights, blends, out_ref,
-    x1, x2, acc, packed,
+    pos_ref, far_ref, core_ref, w1_ref, w2_ref, wr_ref, part_ref, weights, blends,
+    inner, ready, out_ref, x1, x2, acc, table, packed,
 ):
     slab = pos_ref[0]
-    even = (1 - slab % 2).astype(F32)
-    odd = 1.0 - even
     not_first = jnp.where(slab == 0, 0.0, 1.0)
     not_last = jnp.where(slab == 3, 0.0, 1.0)
-    for i in range(2):
-        row = even * far_ref[1 + i].astype(F32) + odd * core_ref[1 + i].astype(F32)
-        put_columns(x1, i, row)
-    for i in range(3):
-        row = even * core_ref[i].astype(F32) + odd * far_ref[i].astype(F32)
-        put_columns(x1, 2 + i, row)
-    head = dot(x1[0:2].reshape(512, 384), w1_ref[0])
-    head0 = head[0:256] + dot(x1[1], w1_ref[1])
-    tail0 = dot(x1[2:3].reshape(256, 384), w1_ref[0])
-    tail1 = dot(x1[2:4].reshape(512, 384), w1_ref[1])
-    tail2 = dot(x1[2:5].reshape(768, 384), w1_ref[2])
-    for i in range(7):
-        h = part_ref[i * 256 : (i + 1) * 256]
-        if i == 0:
-            h = h + head0
-        elif i == 1:
-            h = h + head[256:512]
-        elif i == 4:
-            h = h + tail2[0:256]
-        elif i == 5:
-            h = h + tail2[256:512] + tail1[0:256]
-        elif i == 6:
-            h = h + tail2[512:768] + tail1[256:512] + tail0
-        h = jnp.maximum(h, 0.0)
-        if i == 0:
-            h = h * not_first
-        if i >= 5:
-            h = h * not_last
-        put_columns(x2, i, h)
-    acc[...] = dot(x2[0:5].reshape(1280, 384), w2_ref[0])
-    acc[...] += dot(x2[1:6].reshape(1280, 384), w2_ref[1])
-    acc[...] += dot(x2[2:7].reshape(1280, 384), w2_ref[2])
-    table = []
-    for i in range(5):
-        h = jnp.maximum(acc[i * 256 : (i + 1) * 256], 0.0)
-        if i == 4:
-            h = h * not_last
-        table.append(dot_nt(wr_ref[...], h.astype(BF16)))
-    table = jnp.concatenate(table, axis=0).astype(BF16)
+
+    def first_rows(above):
+        for i in range(2):
+            put_columns(x1, i, above[1 + i].astype(F32))
+        head = dot(x1[0:2].reshape(512, 384), w1_ref[0])
+        return head[0:256] + dot(x1[1], w1_ref[1]), head[256:512]
+
+    @pl.when(slab % 2 == 0)
+    def _():
+        head0, head1 = first_rows(far_ref)
+        put_columns(x2, 0, jnp.maximum(part_ref[0:256] + head0, 0.0) * not_first)
+        put_columns(x2, 1, jnp.maximum(part_ref[256:512] + head1, 0.0))
+        x2[2:4] = inner[...]
+        acc[0:512] = dot(x2[0:2].reshape(512, 384), w2_ref[0])
+        acc[0:512] += dot(x2[1:3].reshape(512, 384), w2_ref[1])
+        acc[0:512] += dot(x2[2:4].reshape(512, 384), w2_ref[2])
+        table[0:64] = jnp.concatenate(table_rows(acc, 0, 2, wr_ref[...]), axis=0).astype(BF16)
+        table[64:160] = ready[...]
+
+    @pl.when(slab % 2 == 1)
+    def _():
+        head0, head1 = first_rows(core_ref)
+        for i in range(3):
+            put_columns(x1, 2 + i, far_ref[i].astype(F32))
+        tail0 = dot(x1[2], w1_ref[0])
+        tail1 = dot(x1[2:4].reshape(512, 384), w1_ref[1])
+        tail2 = dot(x1[2:5].reshape(768, 384), w1_ref[2])
+        for i in range(7):
+            h = part_ref[i * 256 : (i + 1) * 256]
+            if i == 0:
+                h = h + head0
+            elif i == 1:
+                h = h + head1
+            elif i == 4:
+                h = h + tail2[0:256]
+            elif i == 5:
+                h = h + tail2[256:512] + tail1[0:256]
+            elif i == 6:
+                h = h + tail2[512:768] + tail1[256:512] + tail0
+            h = jnp.maximum(h, 0.0)
+            if i >= 5:
+                h = h * not_last
+            put_columns(x2, i, h)
+        acc[...] = dot(x2[0:5].reshape(1280, 384), w2_ref[0])
+        acc[...] += dot(x2[1:6].reshape(1280, 384), w2_ref[1])
+        acc[...] += dot(x2[2:7].reshape(1280, 384), w2_ref[2])
+        rows = table_rows(acc, 0, 5, wr_ref[...])
+        rows[4] = rows[4] * not_last
+        table[...] = jnp.concatenate(rows, axis=0).astype(BF16)
+
     for k in range(8):
-        got = dot(table, weights[k])
+        got = dot(table[...], weights[k])
         blend = blends[k]
         total = got[0:32] * blend[0:1]
         for r in range(1, 5):
@@ -160,21 +221,22 @@
     out_ref[...] = packed[...].astype(BF16)
 
 
-def features(slab, far, core, w1, w2, wr, part, weights, blends):
+def features(slab, far, core, w1, w2, wr, part, weights, blends, inner, ready):
     return pl.pallas_call(
         features_kernel,
         out_shape=jax.ShapeDtypeStruct((1024, 128), BF16),
-        in_specs=[whole(pltpu.SMEM)] + [whole(pltpu.VMEM)] * 8,
+        in_specs=[whole(pltpu.SMEM)] + [whole(pltpu.VMEM)] * 10,
         out_specs=whole(pltpu.VMEM),
         scratch_shapes=[
             pltpu.VMEM((5, 256, 384), BF16),
             pltpu.VMEM((7, 256, 384), BF16),
             pltpu.VMEM((1280, 128), F32),
+            pltpu.VMEM((160, 256), BF16),
             pltpu.VMEM((1024, 128), F32),
         ],
         compiler_params=pltpu.CompilerParams(vmem_limit_bytes=32 * 2**20),
         name="features",
-    )(slab, far, core, w1, w2, wr, part, weights, blends)
+    )(slab, far, core, w1, w2, wr, part, weights, blends, inner, ready)
 
 
 def slots_kernel(by_lane_ref, one_hot):
@@ -425,7 +487,10 @@
     slab_pos = s.astype(jnp.int32).reshape(1)
 
     part, weights, blends = prepare(cam_weight, img, w1, pix, frac)
-    sent = features(slab_pos, far, core, w1, w2, w_reduce.T, part, weights, blends)
+    inner, ready = middle(slab_pos, core, w1, w2, w_reduce.T, part)
+    sent = features(
+        slab_pos, far, core, w1, w2, w_reduce.T, part, weights, blends, inner, ready
+    )
     got = lax.all_to_all(sent.reshape(128, 8, 128), AXES, 0, 0, tiled=True).reshape(1024, 128)
     one_hot = slots(by_lane)
     spread, facing = spread_values(slab_pos, got, one_hot, by_row)

time: 95.2 us -> 94.4 us (level)
  the two profiles are of different devices: /device:TPU:27 before, /device:TPU:3 now
where the time goes in v5:
time: 94.4 us; the launch traced here: 94.1 us
  starting transfers between devices  51.6 us (55%)
  waiting for transfers between devices  23.9 us (25%)
  Pallas kernels  10.9 us (12%)
  local copies, waits for them, and re-layouts  5.06 us (5%)
  other arithmetic  1.57 us (2%)
  between operations  1 us (1%)
    ppermute x6, starting transfers between devices, swap(): return lax.ppermute(x, AXES, pairs)  34.1 us
    all_to_all x1, starting transfers between devices, local(): lax.all_to_all(sent.reshape(128, 8, 128), AXES, 0, 0, tiled=True)  17.5 us
    all_to_all x1, waiting for transfers between devices, local(): lax.all_to_all(sent.reshape(128, 8, 128), AXES, 0, 0, tiled=True)  14.5 us
    ppermute x6, waiting for transfers between devices, swap(): return lax.ppermute(x, AXES, pairs)  9.33 us
    concatenate x7, local copies, waits for them, and re-layouts, banded(): rows.append(jnp.concatenate(blocks, axis=2))  4.43 us
    pallas_call x1, Pallas kernels, features(): pl.pallas_call(features_kernel, out_shape=jax.ShapeDtypeStruct((1024, 128...  3.11 us
    pallas_call x1, Pallas kernels, volume_convs(): pl.pallas_call(volume_kernel, out_shape=jax.ShapeDtypeStruct((256, 128),...  2.72 us
    pallas_call x1, Pallas kernels, prepare(): pl.pallas_call(prepare_kernel, out_shape=(jax.ShapeDtypeStruct((1792, 128...  2.36 us
  transfers between devices with their start and end apart: 7, of which 4 were waited for; matrix products, arithmetic and copies ran while one was open for 6% of the time, Pallas kernels for 4%

profile of v5, /device:TPU:3, one launch (start us, length us, event | category | flops | bytes accessed | tf_op | source)
XLA Modules:
  0.0 94.1 jit_solution(15154603779938691489)
XLA Ops:
  0.0 1.1 %select_bitcast_fusion = (bf16[3,256,128]{2,1,0:T(8,128)(2,1)S(1)}, bf16[3,256,128]{2,1,0:T(8,128)(2,1)S(1)}) fusion(pred[]{:T(512)S(6)} %eq.5, bf16[1,4,256,128]{3,2,1,0:T(8,128)(2,1)} %param.10), kind=kLoop, calls=%fused_computation.2 | loop fusion | flops 196608 | bytes 786433 | tf_op jit(solution)/shard_map/jit(_where)/select_n | solution.py:477
  1.1 16.0 %collective-permute-start = (bf16[3,256,128]{2,1,0:T(8,128)(2,1)S(1)}, bf16[3,256,128]{2,1,0:T(8,128)(2,1)S(1)}, u32[]{:S(2)}, u32[]{:S(2)}) collective-permute-start(bf16[3,256,128]{2,1,0:T(8,128)(2,1)S(1)} %get-tuple-element.20), channel_id=1, source_target_pairs={{1,2},{2,1},{5,6},{6,5},{9,10},{10,9},{13,14},{14,13},{17,18},{18,... | collective-permute-start | bytes 589832 | tf_op jit(solution)/shard_map/ppermute | solution.py:438
  17.1 1.9 %collective-permute-start.1 = (bf16[3,256,128]{2,1,0:T(8,128)(2,1)S(1)}, bf16[3,256,128]{2,1,0:T(8,128)(2,1)S(1)}, u32[]{:S(2)}, u32[]{:S(2)}) collective-permute-start(bf16[3,256,128]{2,1,0:T(8,128)(2,1)S(1)} %get-tuple-element.19), channel_id=1, source_target_pairs={{0,1},{1,0},{2,3},{3,2},{4,5},{5,4},{6,7},{7,6},{8,9},{9,8},{10,11... | collective-permute-start | bytes 589832 | tf_op jit(solution)/shard_map/ppermute | solution.py:438
  19.6 0.0 copy-start
  19.7 0.0 copy-start.1
  19.7 0.0 copy-start.2
  19.7 2.4 %prepare.1 = (f32[1792,128]{1,0:T(8,128)S(1)}, bf16[8,256,512]{2,1,0:T(8,128)(2,1)S(1)}, f32[8,8,512]{2,1,0:T(8,128)S(1)}) custom-call(f32[1]{0:T(128)S(6)} %copy.29.scale_ref, bf16[4,256,128]{2,1,0:T(8,128)(2,1)} %bitcast.59, bf16[3,384,128]{2,1,0:T(8,128)(2,1)} %bitcast.50, s32[32,128]{1,0:T(8,128)} %bitcast.63, f32[2,32,128]{2,1,0:T(8,128)} %bitcast.62), custom_call_target="tpu_custom_call" | custom-call | flops 10000000000 | bytes 4000000 | tf_op jit(solution)/shard_map/prepare/pallas_call | solution.py:81
  22.0 0.0 collective-permute-done.1.core_ref
  22.1 0.0 copy-done
  22.1 0.0 copy-done.1
  22.1 0.0 copy-done.2
  22.1 0.0 collective-permute-done.far_ref
  22.1 0.0 copy-start.8
  22.1 0.0 copy-start.9
  22.1 3.1 %features.1 = bf16[1024,128]{1,0:T(8,128)(2,1)} custom-call(s32[1]{0:T(128)} %bitcast.1.pos_ref, bf16[3,256,128]{2,1,0:T(8,128)(2,1)S(1)} %collective-permute-done.far_ref, bf16[3,256,128]{2,1,0:T(8,128)(2,1)S(1)} %collective-permute-done.1.core_ref, bf16[3,384,128]{2,1,0:T(8,128)(2,1)S(1)} %bitcast.52, bf16[3,384,128]{2,1,0:T(8,128)(2,1)S(1)} %bitcast.54, ...), custom_call_target="tpu_custom_call" | custom-call | tf_op jit(solution)/shard_map/features/pallas_call | solution.py:225
  25.3 17.5 %all-to-all-start = ((bf16[128,8,128]{2,1,0:T(8,128)(2,1)}), bf16[128,8,128]{2,1,0:T(8,128)(2,1)S(1)}, u32[]{:S(2)}, u32[]{:S(2)}) async-start(bf16[128,8,128]{2,1,0:T(8,128)(2,1)} %bitcast.12), calls=%async_computation | async-start | bytes 524288 | tf_op jit(solution)/shard_map/all_to_all | solution.py:494
  42.8 0.0 copy-done.8
  42.8 0.0 copy-done.9
  42.8 0.1 slice_bitcast_fusion.1
  42.9 0.2 concatenate.42
  43.1 0.8 concatenate.41
  43.9 0.0 copy-start.10
  43.9 0.9 concatenate.37
  44.8 0.8 concatenate.36
  45.6 0.8 concatenate.39
  46.5 0.8 concatenate.34
  47.3 0.0 copy-done.10
  47.3 0.1 copy.14
  47.4 0.2 reshape_squeeze.3.by_row_ref
  47.6 0.2 copy.15
  47.8 0.1 pad.11.clone
  47.9 0.4 slots.1.one_hot
  48.2 14.5 %all-to-all-done = bf16[128,8,128]{2,1,0:T(8,128)(2,1)S(1)} async-done(((bf16[128,8,128]{2,1,0:T(8,128)(2,1)}), bf16[128,8,128]{2,1,0:T(8,128)(2,1)S(1)}, u32[]{:S(2)}, u32[]{:S(2)}) %all-to-all-start) | async-done | bytes 262176 | tf_op jit(solution)/shard_map/all_to_all | solution.py:494
  62.8 1.0 %spread.1 = (bf16[4096,128]{1,0:T(8,128)(2,1)S(1)}, bf16[2,32,128]{2,1,0:T(8,128)(2,1)S(1)}) custom-call(s32[1]{0:T(128)} %bitcast.1.pos_ref, bf16[1024,128]{1,0:T(8,128)(2,1)S(1)} %bitcast.55, bf16[256,4096]{1,0:T(8,128)(2,1)S(1)} %slots.1.one_hot, s32[1024,4]{1,0:T(8,128)S(1)} %reshape_squeeze.3.by_row_ref), custom_call_target="tpu_custom_call" | custom-call | tf_op jit(solution)/shard_map/spread/pallas_call | solution.py:277
  63.8 6.2 %collective-permute-start.2 = (bf16[2,32,128]{2,1,0:T(8,128)(2,1)S(1)}, bf16[2,32,128]{2,1,0:T(8,128)(2,1)S(1)}, u32[]{:S(2)}, u32[]{:S(2)}) collective-permute-start(bf16[2,32,128]{2,1,0:T(8,128)(2,1)S(1)} %get-tuple-element.17), channel_id=1, source_target_pairs={{1,2},{2,1},{5,6},{6,5},{9,10},{10,9},{13,14},{14,13},{17,18},{18,... | collective-permute-start | bytes 49160 | tf_op jit(solution)/shard_map/ppermute | solution.py:438
  70.0 0.0 copy-start.3
  70.0 0.0 copy-start.4
  70.0 0.0 copy-start.5
  70.0 0.0 copy-start.6
  70.0 0.0 copy-start.7
  70.0 0.7 scatter.1
  70.8 1.9 %collective-permute-start.3 = (bf16[2,32,128]{2,1,0:T(8,128)(2,1)S(1)}, bf16[2,32,128]{2,1,0:T(8,128)(2,1)S(1)}, u32[]{:S(2)}, u32[]{:S(2)}) collective-permute-start(bf16[2,32,128]{2,1,0:T(8,128)(2,1)S(1)} %slice_select_fusion), channel_id=1, source_target_pairs={{0,1},{1,0},{2,3},{3,2},{4,5},{5,4},{6,7},{7,6},{8,9},{9,8},{10,11... | collective-permute-start | bytes 49160 | tf_op jit(solution)/shard_map/ppermute | solution.py:438
  72.7 0.0 copy-done.3
  72.7 0.0 copy-done.4
  72.7 0.0 copy-done.5
  72.7 0.0 copy-done.6
  72.7 0.0 copy-done.7
  72.7 0.4 pad_maximum_fusion.1
  73.2 4.4 %collective-permute-done.2 = bf16[2,32,128]{2,1,0:T(8,128)(2,1)S(1)} collective-permute-done((bf16[2,32,128]{2,1,0:T(8,128)(2,1)S(1)}, bf16[2,32,128]{2,1,0:T(8,128)(2,1)S(1)}, u32[]{:S(2)}, u32[]{:S(2)}) %collective-permute-start.2) | collective-permute-done | bytes 16416 | tf_op jit(solution)/shard_map/ppermute | solution.py:438
  77.6 0.0 collective-permute-done.3
  77.6 6.2 %collective-permute-start.4 = (bf16[2,192,128]{2,1,0:T(8,128)(2,1)S(1)}, bf16[2,192,128]{2,1,0:T(8,128)(2,1)S(1)}, u32[]{:S(2)}, u32[]{:S(2)}) collective-permute-start(bf16[2,192,128]{2,1,0:T(8,128)(2,1)S(1)} %pad_maximum_fusion.2.own_ref), channel_id=1, source_target_pairs={{4,8},{5,9},{6,10},{7,11},{8,4},{9,5},{10,6},{11,7},{12,16},{13,17... | collective-permute-start | bytes 294920 | tf_op jit(solution)/shard_map/ppermute | solution.py:438
  83.8 1.9 %collective-permute-start.5 = (bf16[2,192,128]{2,1,0:T(8,128)(2,1)S(1)}, bf16[2,192,128]{2,1,0:T(8,128)(2,1)S(1)}, u32[]{:S(2)}, u32[]{:S(2)}) collective-permute-start(bf16[2,192,128]{2,1,0:T(8,128)(2,1)S(1)} %pad_maximum_fusion.2.own_ref), channel_id=1, source_target_pairs={{0,4},{1,5},{2,6},{3,7},{4,0},{5,1},{6,2},{7,3},{8,12},{9,13},{10,... | collective-permute-start | bytes 294920 | tf_op jit(solution)/shard_map/ppermute | solution.py:438
  85.7 0.1 pad_add_fusion.pos_ref
  85.8 0.6 volume_start.1.part_ref
  86.4 4.2 %collective-permute-done.4.next_ref = bf16[2,192,128]{2,1,0:T(8,128)(2,1)S(1)} collective-permute-done((bf16[2,192,128]{2,1,0:T(8,128)(2,1)S(1)}, bf16[2,192,128]{2,1,0:T(8,128)(2,1)S(1)}, u32[]{:S(2)}, u32[]{:S(2)}) %collective-permute-start.4) | collective-permute-done | bytes 98336 | tf_op jit(solution)/shard_map/ppermute | solution.py:438
  90.6 0.8 collective-permute-done.5.near_ref
  91.3 2.7 %volume.1 = bf16[256,128]{1,0:T(8,128)(2,1)} custom-call(s32[2]{0:T(128)S(1)} %pad_add_fusion.pos_ref, bf16[2,192,128]{2,1,0:T(8,128)(2,1)S(1)} %pad_maximum_fusion.2.own_ref, bf16[2,192,128]{2,1,0:T(8,128)(2,1)S(1)} %collective-permute-done.4.next_ref, bf16[2,192,128]{2,1,0:T(8,128)(2,1)S(1)} %collective-permute-done.5.near_ref, ...), custom_call_target="tpu_custom_call" | custom-call | tf_op jit(solution)/shard_map/volume/pallas_call | solution.py:402
  (9 shorter events, 0.1 us)
Async XLA Ops:
  1.1 21.1 %collective-permute-start = (bf16[3,256,128]{2,1,0:T(8,128)(2,1)S(1)}, bf16[3,256,128]{2,1,0:T(8,128)(2,1)S(1)}, u32[]{:S(2)}, u32[]{:S(2)}) collective-permute-start(bf16[3,256,128]{2,1,0:T(8,128)(2,1)S(1)} %get-tuple-element.20), channel_id=1, source_target_pairs={{1,2},{2,1},{5,6},{6,5},{9,10},{10,9},{13,14},{14,13},{17,18},{18,... | collective-permute-start | bytes 589832 | tf_op jit(solution)/shard_map/ppermute | solution.py:438
  17.1 5.0 %collective-permute-start.1 = (bf16[3,256,128]{2,1,0:T(8,128)(2,1)S(1)}, bf16[3,256,128]{2,1,0:T(8,128)(2,1)S(1)}, u32[]{:S(2)}, u32[]{:S(2)}) collective-permute-start(bf16[3,256,128]{2,1,0:T(8,128)(2,1)S(1)} %get-tuple-element.19), channel_id=1, source_target_pairs={{0,1},{1,0},{2,3},{3,2},{4,5},{5,4},{6,7},{7,6},{8,9},{9,8},{10,11... | collective-permute-start | bytes 589832 | tf_op jit(solution)/shard_map/ppermute | solution.py:438
  19.6 2.4 %copy-start = (bf16[3,3,128,128]{3,2,1,0:T(8,128)(2,1)S(1)}, bf16[3,3,128,128]{3,2,1,0:T(8,128)(2,1)}, u32[]{:S(2)}) copy-start(bf16[3,3,128,128]{3,2,1,0:T(8,128)(2,1)} %param.11) | copy-start | bytes 884740
  19.7 2.4 %copy-start.1 = (bf16[3,3,128,128]{3,2,1,0:T(8,128)(2,1)S(1)}, bf16[3,3,128,128]{3,2,1,0:T(8,128)(2,1)}, u32[]{:S(2)}) copy-start(bf16[3,3,128,128]{3,2,1,0:T(8,128)(2,1)} %param.12) | copy-start | bytes 884740
  19.7 2.4 %copy-start.2 = (bf16[128,32]{0,1:T(8,128)(2,1)S(1)}, bf16[128,32]{0,1:T(8,128)(2,1)}, u32[]{:S(2)}) copy-start(bf16[128,32]{0,1:T(8,128)(2,1)} %param.13) | copy-start | bytes 24580
  22.1 20.7 %copy-start.8 = (bf16[27,32,32]{2,1,0:T(8,128)(2,1)S(1)}, bf16[27,32,32]{2,1,0:T(8,128)(2,1)}, u32[]{:S(2)}) copy-start(bf16[27,32,32]{2,1,0:T(8,128)(2,1)} %param.19) | copy-start | bytes 165892
  22.1 20.7 %copy-start.9 = (bf16[27,32,32]{2,1,0:T(8,128)(2,1)S(1)}, bf16[27,32,32]{2,1,0:T(8,128)(2,1)}, u32[]{:S(2)}) copy-start(bf16[27,32,32]{2,1,0:T(8,128)(2,1)} %param.18) | copy-start | bytes 165892
  25.3 37.5 %all-to-all-start = ((bf16[128,8,128]{2,1,0:T(8,128)(2,1)}), bf16[128,8,128]{2,1,0:T(8,128)(2,1)S(1)}, u32[]{:S(2)}, u32[]{:S(2)}) async-start(bf16[128,8,128]{2,1,0:T(8,128)(2,1)} %bitcast.12), calls=%async_computation | async-start | bytes 524288 | tf_op jit(solution)/shard_map/all_to_all | solution.py:494
  43.9 3.4 %copy-start.10 = (s32[1,128,32]{1,2,0:T(8,128)S(1)}, s32[1,128,32]{1,2,0:T(8,128)}, u32[]{:S(2)}) copy-start(s32[1,128,32]{1,2,0:T(8,128)} %param.17) | copy-start | bytes 49156
  63.8 13.8 %collective-permute-start.2 = (bf16[2,32,128]{2,1,0:T(8,128)(2,1)S(1)}, bf16[2,32,128]{2,1,0:T(8,128)(2,1)S(1)}, u32[]{:S(2)}, u32[]{:S(2)}) collective-permute-start(bf16[2,32,128]{2,1,0:T(8,128)(2,1)S(1)} %get-tuple-element.17), channel_id=1, source_target_pairs={{1,2},{2,1},{5,6},{6,5},{9,10},{10,9},{13,14},{14,13},{17,18},{18,... | collective-permute-start | bytes 49160 | tf_op jit(solution)/shard_map/ppermute | solution.py:438
  70.0 2.7 %copy-start.3 = (bf16[9,32,256]{2,1,0:T(8,128)(2,1)S(1)}, bf16[9,32,256]{2,1,0:T(8,128)(2,1)}, u32[]{:S(2)}) copy-start(bf16[9,32,256]{2,1,0:T(8,128)(2,1)} %concatenate.41) | copy-start | bytes 442372
  70.0 2.7 %copy-start.4 = (bf16[9,32,256]{2,1,0:T(8,128)(2,1)S(1)}, bf16[9,32,256]{2,1,0:T(8,128)(2,1)}, u32[]{:S(2)}) copy-start(bf16[9,32,256]{2,1,0:T(8,128)(2,1)} %concatenate.37) | copy-start | bytes 442372
  70.0 2.7 %copy-start.5 = (bf16[9,32,256]{2,1,0:T(8,128)(2,1)S(1)}, bf16[9,32,256]{2,1,0:T(8,128)(2,1)}, u32[]{:S(2)}) copy-start(bf16[9,32,256]{2,1,0:T(8,128)(2,1)} %concatenate.36) | copy-start | bytes 442372
  70.0 2.7 %copy-start.6 = (bf16[9,32,256]{2,1,0:T(8,128)(2,1)S(1)}, bf16[9,32,256]{2,1,0:T(8,128)(2,1)}, u32[]{:S(2)}) copy-start(bf16[9,32,256]{2,1,0:T(8,128)(2,1)} %concatenate.39) | copy-start | bytes 442372
  70.0 2.7 %copy-start.7 = (bf16[9,32,256]{2,1,0:T(8,128)(2,1)S(1)}, bf16[9,32,256]{2,1,0:T(8,128)(2,1)}, u32[]{:S(2)}) copy-start(bf16[9,32,256]{2,1,0:T(8,128)(2,1)} %concatenate.34) | copy-start | bytes 442372
  70.8 6.8 %collective-permute-start.3 = (bf16[2,32,128]{2,1,0:T(8,128)(2,1)S(1)}, bf16[2,32,128]{2,1,0:T(8,128)(2,1)S(1)}, u32[]{:S(2)}, u32[]{:S(2)}) collective-permute-start(bf16[2,32,128]{2,1,0:T(8,128)(2,1)S(1)} %slice_select_fusion), channel_id=1, source_target_pairs={{0,1},{1,0},{2,3},{3,2},{4,5},{5,4},{6,7},{7,6},{8,9},{9,8},{10,11... | collective-permute-start | bytes 49160 | tf_op jit(solution)/shard_map/ppermute | solution.py:438
  77.6 13.0 %collective-permute-start.4 = (bf16[2,192,128]{2,1,0:T(8,128)(2,1)S(1)}, bf16[2,192,128]{2,1,0:T(8,128)(2,1)S(1)}, u32[]{:S(2)}, u32[]{:S(2)}) collective-permute-start(bf16[2,192,128]{2,1,0:T(8,128)(2,1)S(1)} %pad_maximum_fusion.2.own_ref), channel_id=1, source_target_pairs={{4,8},{5,9},{6,10},{7,11},{8,4},{9,5},{10,6},{11,7},{12,16},{13,17... | collective-permute-start | bytes 294920 | tf_op jit(solution)/shard_map/ppermute | solution.py:438
  83.8 7.6 %collective-permute-start.5 = (bf16[2,192,128]{2,1,0:T(8,128)(2,1)S(1)}, bf16[2,192,128]{2,1,0:T(8,128)(2,1)S(1)}, u32[]{:S(2)}, u32[]{:S(2)}) collective-permute-start(bf16[2,192,128]{2,1,0:T(8,128)(2,1)S(1)} %pad_maximum_fusion.2.own_ref), channel_id=1, source_target_pairs={{0,4},{1,5},{2,6},{3,7},{4,0},{5,1},{6,2},{7,3},{8,12},{9,13},{10,... | collective-permute-start | bytes 294920 | tf_op jit(solution)/shard_map/ppermute | solution.py:438

commit v6 on v5

--- a/solution.py
+++ b/solution.py
@@ -239,68 +239,81 @@
     )(slab, far, core, w1, w2, wr, part, weights, blends, inner, ready)
 
 
-def slots_kernel(by_lane_ref, one_hot):
-    lo_iota = lax.broadcasted_iota(jnp.int32, (256, 1024), 0)
+def slots_kernel(pos_ref, by_lane_ref, one_hot):
+    row = lax.broadcasted_iota(jnp.int32, (256, 1024), 0)
+    start = (pos_ref[0] % 2) * 96
+    voxel = (row // 32 % 2 * 128 + start + row % 32) * 4 + row // 64
     for s in range(4):
-        hit = lo_iota == (by_lane_ref[s : s + 1] >> 2)
+        hit = voxel == by_lane_ref[s : s + 1]
         one_hot[:, 1024 * s : 1024 * s + 1024] = jnp.where(hit, 1.0, 0.0).astype(BF16)
 
 
-def slots(by_lane):
+def slots(slab, by_lane):
     return pl.pallas_call(
         slots_kernel,
         out_shape=jax.ShapeDtypeStruct((256, 4096), BF16),
-        in_specs=[whole(pltpu.VMEM)],
+        in_specs=[whole(pltpu.SMEM), whole(pltpu.VMEM)],
         out_specs=whole(pltpu.VMEM),
         compiler_params=pltpu.CompilerParams(vmem_limit_bytes=16 * 2**20),
         cost_estimate=pl.CostEstimate(flops=10**7, bytes_accessed=2 * 10**6, transcendentals=0),
         name="slots",
-    )(by_lane)
-
-
-def spread_kernel(pos_ref, val_ref, one_hot, by_row_ref, spread, facing):
-    start = pl.multiple_of((pos_ref[0] % 2) * 96, 32)
+    )(slab, by_lane)
+
+
+def facing_kernel(val_ref, one_hot, out_ref):
+    group = lax.broadcasted_iota(jnp.int32, (256, 128), 1) // 32
     val = val_ref[...]
+    total = jnp.zeros((256, 128), F32)
+    for s in range(4):
+        part = dot(one_hot[:, 1024 * s : 1024 * s + 1024], val)
+        total = jnp.where(group == s, part, total)
+    total = total + pltpu.roll(total, 64, 1)
+    total = total + pltpu.roll(total, 32, 1)
+    group = group[0:64]
+    rows = jnp.zeros((64, 128), F32)
+    for z in range(4):
+        rows = jnp.where(group == z, total[64 * z : 64 * z + 64], rows)
+    out_ref[...] = rows.reshape(2, 32, 128).astype(BF16)
+
+
+def facing_rows(val, one_hot):
+    return pl.pallas_call(
+        facing_kernel,
+        out_shape=jax.ShapeDtypeStruct((2, 32, 128), BF16),
+        in_specs=[whole(pltpu.VMEM)] * 2,
+        out_specs=whole(pltpu.VMEM),
+        compiler_params=pltpu.CompilerParams(vmem_limit_bytes=16 * 2**20),
+        name="facing",
+    )(val, one_hot)
+
+
+def scatter_kernel(val_ref, by_lane_ref, by_row_ref, out_ref):
+    val = val_ref[...]
+    lo_iota = lax.broadcasted_iota(jnp.int32, (256, 1024), 0)
     hi_iota = lax.broadcasted_iota(jnp.int32, (1024, 128), 1) // 32
     sel_row = lax.broadcasted_iota(jnp.int32, (128, 128), 0)
     sel_col = lax.broadcasted_iota(jnp.int32, (128, 128), 1) % 32
+    total = jnp.zeros((256, 128), F32)
     for s in range(4):
+        one_hot = jnp.where(lo_iota == (by_lane_ref[s : s + 1] >> 2), 1.0, 0.0).astype(BF16)
         select = jnp.where(sel_row == sel_col + 32 * s, 1.0, 0.0).astype(BF16)
-        block = hi_iota == (by_row_ref[:, s : s + 1] & 3)
-        spread[1024 * s : 1024 * s + 1024] = jnp.where(block, dot(val, select), 0.0).astype(BF16)
-    for i in range(2):
-        rows = one_hot[pl.ds(128 * i + start, 32), :]
-        facing[i] = dot(rows, spread[...]).astype(BF16)
-
-
-def spread_values(slab, val, one_hot, by_row):
-    return pl.pallas_call(
-        spread_kernel,
-        out_shape=(
-            jax.ShapeDtypeStruct((4096, 128), BF16),
-            jax.ShapeDtypeStruct((2, 32, 128), BF16),
-        ),
-        in_specs=[whole(pltpu.SMEM)] + [whole(pltpu.VMEM)] * 3,
-        out_specs=(whole(pltpu.VMEM),) * 2,
-        compiler_params=pltpu.CompilerParams(vmem_limit_bytes=16 * 2**20),
-        name="spread",
-    )(slab, val, one_hot, by_row)
-
-
-def scatter_kernel(one_hot, spread, out_ref):
-    out_ref[...] = dot(one_hot[...], spread[...]).reshape(2, 128, 128).astype(BF16)
-
-
-def scatter(one_hot, spread):
+        spread = dot(val, select)
+        hi = by_row_ref[:, s : s + 1] & 3
+        spread = jnp.where(hi_iota == hi, spread, 0.0).astype(BF16)
+        total = total + dot(one_hot, spread)
+    out_ref[...] = total.reshape(2, 128, 128).astype(BF16)
+
+
+def scatter(val, by_lane, by_row):
     return pl.pallas_call(
         scatter_kernel,
         out_shape=jax.ShapeDtypeStruct((2, 128, 128), BF16),
-        in_specs=[whole(pltpu.VMEM)] * 2,
+        in_specs=[whole(pltpu.VMEM)] * 3,
         out_specs=whole(pltpu.VMEM),
         compiler_params=pltpu.CompilerParams(vmem_limit_bytes=16 * 2**20),
         cost_estimate=pl.CostEstimate(flops=3 * 10**8, bytes_accessed=3 * 10**6, transcendentals=0),
         name="scatter",
-    )(one_hot, spread)
+    )(val, by_lane, by_row)
 
 
 def put_depth(dst, plane, x):
@@ -492,10 +505,10 @@
         slab_pos, far, core, w1, w2, w_reduce.T, part, weights, blends, inner, ready
     )
     got = lax.all_to_all(sent.reshape(128, 8, 128), AXES, 0, 0, tiled=True).reshape(1024, 128)
-    one_hot = slots(by_lane)
-    spread, facing = spread_values(slab_pos, got, one_hot, by_row)
+    facing = facing_rows(got, slots(slab_pos, by_lane))
+    facing, got = lax.optimization_barrier((facing, got))
     far = swap(facing, far_partner, cams, slabs)
-    volume = scatter(one_hot, spread)
+    volume = scatter(got, by_lane, by_row)
 
     pos = jnp.stack([p, s]).astype(jnp.int32)
     top, bottom = volume[:, 0:32], volume[:, 96:128]

time: 94.4 us -> 94.1 us (level)
  the two profiles are of different devices: /device:TPU:3 before, /device:TPU:10 now
where the time goes in v6:
time: 94.1 us; the launch traced here: 93.8 us
  starting transfers between devices  54.3 us (58%)
  waiting for transfers between devices  19.5 us (21%)
  Pallas kernels  11.7 us (12%)
  local copies, waits for them, and re-layouts  5.7 us (6%)
  other arithmetic  1.59 us (2%)
  between operations  0.98 us (1%)
    ppermute x6, starting transfers between devices, swap(): return lax.ppermute(x, AXES, pairs)  37.4 us
    all_to_all x1, starting transfers between devices, local(): lax.all_to_all(sent.reshape(128, 8, 128), AXES, 0, 0, tiled=True)  17 us
    all_to_all x1, waiting for transfers between devices, local(): lax.all_to_all(sent.reshape(128, 8, 128), AXES, 0, 0, tiled=True)  14.1 us
    ppermute x6, waiting for transfers between devices, swap(): return lax.ppermute(x, AXES, pairs)  5.4 us
    concatenate x7, local copies, waits for them, and re-layouts, banded(): rows.append(jnp.concatenate(blocks, axis=2))  5.07 us
    pallas_call x1, Pallas kernels, volume_convs(): pl.pallas_call(volume_kernel, out_shape=jax.ShapeDtypeStruct((256, 128),...  2.71 us
    pallas_call x1, Pallas kernels, prepare(): pl.pallas_call(prepare_kernel, out_shape=(jax.ShapeDtypeStruct((1792, 128...  2.36 us
    pallas_call x1, Pallas kernels, features(): pl.pallas_call(features_kernel, out_shape=jax.ShapeDtypeStruct((1024, 128...  2.32 us
  transfers between devices with their start and end apart: 7, of which 4 were waited for; matrix products, arithmetic and copies ran while one was open for 7% of the time, Pallas kernels for 6%

profile of v6, /device:TPU:10, one launch (start us, length us, event | category | flops | bytes accessed | tf_op | source)
XLA Modules:
  0.0 93.8 jit_solution(740296754515305607)
XLA Ops:
  0.0 1.1 %select_bitcast_fusion = (bf16[3,256,128]{2,1,0:T(8,128)(2,1)S(1)}, bf16[3,256,128]{2,1,0:T(8,128)(2,1)S(1)}) fusion(pred[]{:T(512)S(6)} %eq.5, bf16[1,4,256,128]{3,2,1,0:T(8,128)(2,1)} %param.10), kind=kLoop, calls=%fused_computation.2 | loop fusion | flops 196608 | bytes 786433 | tf_op jit(solution)/shard_map/jit(_where)/select_n | solution.py:490
  1.1 0.7 collective-permute-start
  1.7 17.1 %collective-permute-start.1 = (bf16[3,256,128]{2,1,0:T(8,128)(2,1)S(1)}, bf16[3,256,128]{2,1,0:T(8,128)(2,1)S(1)}, u32[]{:S(2)}, u32[]{:S(2)}) collective-permute-start(bf16[3,256,128]{2,1,0:T(8,128)(2,1)S(1)} %get-tuple-element.19), channel_id=1, source_target_pairs={{0,1},{1,0},{2,3},{3,2},{4,5},{5,4},{6,7},{7,6},{8,9},{9,8},{10,11... | collective-permute-start | bytes 589832 | tf_op jit(solution)/shard_map/ppermute | solution.py:451
  19.5 0.0 copy-start
  19.5 0.0 copy-start.1
  19.5 0.0 copy-start.2
  19.5 2.4 %prepare.1 = (f32[1792,128]{1,0:T(8,128)S(1)}, bf16[8,256,512]{2,1,0:T(8,128)(2,1)S(1)}, f32[8,8,512]{2,1,0:T(8,128)S(1)}) custom-call(f32[1]{0:T(128)S(6)} %copy.30.scale_ref, bf16[4,256,128]{2,1,0:T(8,128)(2,1)} %bitcast.61, bf16[3,384,128]{2,1,0:T(8,128)(2,1)} %bitcast.50, s32[32,128]{1,0:T(8,128)} %bitcast.65, f32[2,32,128]{2,1,0:T(8,128)} %bitcast.64), custom_call_target="tpu_custom_call" | custom-call | flops 10000000000 | bytes 4000000 | tf_op jit(solution)/shard_map/prepare/pallas_call | solution.py:81
  21.9 0.0 collective-permute-done.1.core_ref
  21.9 0.0 copy-done
  21.9 0.0 copy-done.1
  21.9 0.0 copy-done.2
  21.9 1.2 %middle.1 = (bf16[2,256,384]{2,1,0:T(8,128)(2,1)S(1)}, bf16[96,256]{1,0:T(8,128)(2,1)S(1)}) custom-call(s32[1]{0:T(128)} %bitcast.1.pos_ref, bf16[3,256,128]{2,1,0:T(8,128)(2,1)S(1)} %collective-permute-done.1.core_ref, bf16[3,384,128]{2,1,0:T(8,128)(2,1)S(1)} %bitcast.51, bf16[3,384,128]{2,1,0:T(8,128)(2,1)S(1)} %bitcast.53, bf16[32,128]{1,0:T(8,128)(2,1)S(1)} %bitcast.59, ...), custom_call_target="tpu_custom_call" | custom-call | flops 1000000 | bytes 1000 | tf_op jit(solution)/shard_map/middle/pallas_call | solution.py:137
  23.1 0.0 collective-permute-done.far_ref
  23.2 0.0 copy-start.9
  23.2 0.0 copy-start.10
  23.2 2.3 %features.1 = bf16[1024,128]{1,0:T(8,128)(2,1)} custom-call(s32[1]{0:T(128)} %bitcast.1.pos_ref, bf16[3,256,128]{2,1,0:T(8,128)(2,1)S(1)} %collective-permute-done.far_ref, bf16[3,256,128]{2,1,0:T(8,128)(2,1)S(1)} %collective-permute-done.1.core_ref, bf16[3,384,128]{2,1,0:T(8,128)(2,1)S(1)} %bitcast.52, bf16[3,384,128]{2,1,0:T(8,128)(2,1)S(1)} %bitcast.54, ...), custom_call_target="tpu_custom_call" | custom-call | tf_op jit(solution)/shard_map/features/pallas_call | solution.py:225
  25.5 17.0 %all-to-all-start = ((bf16[128,8,128]{2,1,0:T(8,128)(2,1)}), bf16[128,8,128]{2,1,0:T(8,128)(2,1)S(1)}, u32[]{:S(2)}, u32[]{:S(2)}) async-start(bf16[128,8,128]{2,1,0:T(8,128)(2,1)} %bitcast.12), calls=%async_computation | async-start | bytes 524288 | tf_op jit(solution)/shard_map/all_to_all | solution.py:507
  42.5 0.0 copy-done.9
  42.5 0.0 copy-done.10
  42.5 0.1 slice_bitcast_fusion.1
  42.6 0.2 concatenate.42
  42.8 0.8 concatenate.41
  43.6 0.0 copy-start.11
  43.6 0.9 concatenate.37
  44.5 0.8 concatenate.36
  45.3 0.8 concatenate.39
  46.1 0.8 concatenate.34
  47.0 0.0 copy-done.11
  47.0 0.1 copy.15
  47.1 0.2 reshape_squeeze.3.by_row_ref
  47.3 0.2 copy.16
  47.5 0.7 pad.11.clone
  48.2 0.4 slots.1.one_hot
  48.6 14.1 %all-to-all-done = bf16[128,8,128]{2,1,0:T(8,128)(2,1)S(1)} async-done(((bf16[128,8,128]{2,1,0:T(8,128)(2,1)}), bf16[128,8,128]{2,1,0:T(8,128)(2,1)S(1)}, u32[]{:S(2)}, u32[]{:S(2)}) %all-to-all-start) | async-done | bytes 262176 | tf_op jit(solution)/shard_map/all_to_all | solution.py:507
  62.6 0.0 copy-start.3
  62.6 0.0 copy-start.4
  62.6 0.0 copy-start.5
  62.6 0.0 copy-start.6
  62.6 0.0 copy-start.7
  62.7 0.0 copy-start.8
  62.7 0.8 facing.1
  63.5 0.7 collective-permute-start.2
  64.2 1.2 %scatter.1 = bf16[2,128,128]{2,1,0:T(8,128)(2,1)S(1)} custom-call(bf16[1024,128]{1,0:T(8,128)(2,1)S(1)} %bitcast.56, s32[4,1024]{1,0:T(4,128)S(1)} %bitcast.58, s32[1024,4]{1,0:T(8,128)S(1)} %reshape_squeeze.3.by_row_ref), custom_call_target="tpu_custom_call" | custom-call | flops 300000000 | bytes 3000000 | tf_op jit(solution)/shard_map/scatter/pallas_call | solution.py:308
  65.4 7.4 %collective-permute-start.3 = (bf16[2,32,128]{2,1,0:T(8,128)(2,1)S(1)}, bf16[2,32,128]{2,1,0:T(8,128)(2,1)S(1)}, u32[]{:S(2)}, u32[]{:S(2)}) collective-permute-start(bf16[2,32,128]{2,1,0:T(8,128)(2,1)S(1)} %slice_select_fusion), channel_id=1, source_target_pairs={{0,1},{1,0},{2,3},{3,2},{4,5},{5,4},{6,7},{7,6},{8,9},{9,8},{10,11... | collective-permute-start | bytes 49160 | tf_op jit(solution)/shard_map/ppermute | solution.py:451
  72.8 0.0 copy-done.3
  72.8 0.0 copy-done.4
  72.9 0.0 copy-done.5
  72.9 0.0 copy-done.6
  72.9 0.0 copy-done.7
  72.9 0.0 copy-done.8
  72.9 0.4 pad_maximum_fusion.1
  73.3 0.0 collective-permute-done.2
  73.4 0.3 collective-permute-done.3
  73.7 9.7 %collective-permute-start.4 = (bf16[2,192,128]{2,1,0:T(8,128)(2,1)S(1)}, bf16[2,192,128]{2,1,0:T(8,128)(2,1)S(1)}, u32[]{:S(2)}, u32[]{:S(2)}) collective-permute-start(bf16[2,192,128]{2,1,0:T(8,128)(2,1)S(1)} %pad_maximum_fusion.2.own_ref), channel_id=1, source_target_pairs={{4,8},{5,9},{6,10},{7,11},{8,4},{9,5},{10,6},{11,7},{12,16},{13,17... | collective-permute-start | bytes 294920 | tf_op jit(solution)/shard_map/ppermute | solution.py:451
  83.4 1.9 %collective-permute-start.5 = (bf16[2,192,128]{2,1,0:T(8,128)(2,1)S(1)}, bf16[2,192,128]{2,1,0:T(8,128)(2,1)S(1)}, u32[]{:S(2)}, u32[]{:S(2)}) collective-permute-start(bf16[2,192,128]{2,1,0:T(8,128)(2,1)S(1)} %pad_maximum_fusion.2.own_ref), channel_id=1, source_target_pairs={{0,4},{1,5},{2,6},{3,7},{4,0},{5,1},{6,2},{7,3},{8,12},{9,13},{10,... | collective-permute-start | bytes 294920 | tf_op jit(solution)/shard_map/ppermute | solution.py:451
  85.3 0.1 pad_add_fusion.pos_ref
  85.4 0.6 volume_start.1.part_ref
  86.0 2.0 %collective-permute-done.4.next_ref = bf16[2,192,128]{2,1,0:T(8,128)(2,1)S(1)} collective-permute-done((bf16[2,192,128]{2,1,0:T(8,128)(2,1)S(1)}, bf16[2,192,128]{2,1,0:T(8,128)(2,1)S(1)}, u32[]{:S(2)}, u32[]{:S(2)}) %collective-permute-start.4) | collective-permute-done | bytes 98336 | tf_op jit(solution)/shard_map/ppermute | solution.py:451
  88.0 3.1 %collective-permute-done.5.near_ref = bf16[2,192,128]{2,1,0:T(8,128)(2,1)S(1)} collective-permute-done((bf16[2,192,128]{2,1,0:T(8,128)(2,1)S(1)}, bf16[2,192,128]{2,1,0:T(8,128)(2,1)S(1)}, u32[]{:S(2)}, u32[]{:S(2)}) %collective-permute-start.5) | collective-permute-done | bytes 98336 | tf_op jit(solution)/shard_map/ppermute | solution.py:451
  91.1 2.7 %volume.1 = bf16[256,128]{1,0:T(8,128)(2,1)} custom-call(s32[2]{0:T(128)S(1)} %pad_add_fusion.pos_ref, bf16[2,192,128]{2,1,0:T(8,128)(2,1)S(1)} %pad_maximum_fusion.2.own_ref, bf16[2,192,128]{2,1,0:T(8,128)(2,1)S(1)} %collective-permute-done.4.next_ref, bf16[2,192,128]{2,1,0:T(8,128)(2,1)S(1)} %collective-permute-done.5.near_ref, ...), custom_call_target="tpu_custom_call" | custom-call | tf_op jit(solution)/shard_map/volume/pallas_call | solution.py:415
  (8 shorter events, 0.1 us)
Async XLA Ops:
  1.1 22.1 %collective-permute-start = (bf16[3,256,128]{2,1,0:T(8,128)(2,1)S(1)}, bf16[3,256,128]{2,1,0:T(8,128)(2,1)S(1)}, u32[]{:S(2)}, u32[]{:S(2)}) collective-permute-start(bf16[3,256,128]{2,1,0:T(8,128)(2,1)S(1)} %get-tuple-element.20), channel_id=1, source_target_pairs={{1,2},{2,1},{5,6},{6,5},{9,10},{10,9},{13,14},{14,13},{17,18},{18,... | collective-permute-start | bytes 589832 | tf_op jit(solution)/shard_map/ppermute | solution.py:451
  1.7 20.1 %collective-permute-start.1 = (bf16[3,256,128]{2,1,0:T(8,128)(2,1)S(1)}, bf16[3,256,128]{2,1,0:T(8,128)(2,1)S(1)}, u32[]{:S(2)}, u32[]{:S(2)}) collective-permute-start(bf16[3,256,128]{2,1,0:T(8,128)(2,1)S(1)} %get-tuple-element.19), channel_id=1, source_target_pairs={{0,1},{1,0},{2,3},{3,2},{4,5},{5,4},{6,7},{7,6},{8,9},{9,8},{10,11... | collective-permute-start | bytes 589832 | tf_op jit(solution)/shard_map/ppermute | solution.py:451
  19.5 2.4 %copy-start = (bf16[3,3,128,128]{3,2,1,0:T(8,128)(2,1)S(1)}, bf16[3,3,128,128]{3,2,1,0:T(8,128)(2,1)}, u32[]{:S(2)}) copy-start(bf16[3,3,128,128]{3,2,1,0:T(8,128)(2,1)} %param.11) | copy-start | bytes 884740
  19.5 2.4 %copy-start.1 = (bf16[3,3,128,128]{3,2,1,0:T(8,128)(2,1)S(1)}, bf16[3,3,128,128]{3,2,1,0:T(8,128)(2,1)}, u32[]{:S(2)}) copy-start(bf16[3,3,128,128]{3,2,1,0:T(8,128)(2,1)} %param.12) | copy-start | bytes 884740
  19.5 2.4 %copy-start.2 = (bf16[128,32]{0,1:T(8,128)(2,1)S(1)}, bf16[128,32]{0,1:T(8,128)(2,1)}, u32[]{:S(2)}) copy-start(bf16[128,32]{0,1:T(8,128)(2,1)} %param.13) | copy-start | bytes 24580
  23.2 19.3 %copy-start.9 = (bf16[27,32,32]{2,1,0:T(8,128)(2,1)S(1)}, bf16[27,32,32]{2,1,0:T(8,128)(2,1)}, u32[]{:S(2)}) copy-start(bf16[27,32,32]{2,1,0:T(8,128)(2,1)} %param.19) | copy-start | bytes 165892
  23.2 19.3 %copy-start.10 = (bf16[27,32,32]{2,1,0:T(8,128)(2,1)S(1)}, bf16[27,32,32]{2,1,0:T(8,128)(2,1)}, u32[]{:S(2)}) copy-start(bf16[27,32,32]{2,1,0:T(8,128)(2,1)} %param.18) | copy-start | bytes 165892
  25.5 37.1 %all-to-all-start = ((bf16[128,8,128]{2,1,0:T(8,128)(2,1)}), bf16[128,8,128]{2,1,0:T(8,128)(2,1)S(1)}, u32[]{:S(2)}, u32[]{:S(2)}) async-start(bf16[128,8,128]{2,1,0:T(8,128)(2,1)} %bitcast.12), calls=%async_computation | async-start | bytes 524288 | tf_op jit(solution)/shard_map/all_to_all | solution.py:507
  43.6 3.4 %copy-start.11 = (s32[1,128,32]{1,2,0:T(8,128)S(1)}, s32[1,128,32]{1,2,0:T(8,128)}, u32[]{:S(2)}) copy-start(s32[1,128,32]{1,2,0:T(8,128)} %param.17) | copy-start | bytes 49156
  62.6 10.2 %copy-start.3 = (bf16[9,32,256]{2,1,0:T(8,128)(2,1)S(1)}, bf16[9,32,256]{2,1,0:T(8,128)(2,1)}, u32[]{:S(2)}) copy-start(bf16[9,32,256]{2,1,0:T(8,128)(2,1)} %concatenate.41) | copy-start | bytes 442372
  62.6 10.2 %copy-start.4 = (bf16[9,32,256]{2,1,0:T(8,128)(2,1)S(1)}, bf16[9,32,256]{2,1,0:T(8,128)(2,1)}, u32[]{:S(2)}) copy-start(bf16[9,32,256]{2,1,0:T(8,128)(2,1)} %concatenate.37) | copy-start | bytes 442372
  62.6 10.2 %copy-start.5 = (bf16[9,32,256]{2,1,0:T(8,128)(2,1)S(1)}, bf16[9,32,256]{2,1,0:T(8,128)(2,1)}, u32[]{:S(2)}) copy-start(bf16[9,32,256]{2,1,0:T(8,128)(2,1)} %concatenate.36) | copy-start | bytes 442372
  62.6 10.2 %copy-start.6 = (bf16[9,32,256]{2,1,0:T(8,128)(2,1)S(1)}, bf16[9,32,256]{2,1,0:T(8,128)(2,1)}, u32[]{:S(2)}) copy-start(bf16[9,32,256]{2,1,0:T(8,128)(2,1)} %concatenate.39) | copy-start | bytes 442372
  62.6 10.2 %copy-start.7 = (bf16[9,32,256]{2,1,0:T(8,128)(2,1)S(1)}, bf16[9,32,256]{2,1,0:T(8,128)(2,1)}, u32[]{:S(2)}) copy-start(bf16[9,32,256]{2,1,0:T(8,128)(2,1)} %concatenate.34) | copy-start | bytes 442372
  62.7 10.2 %copy-start.8 = (bf16[128,256]{1,0:T(8,128)(2,1)S(1)}, bf16[128,256]{1,0:T(8,128)(2,1)}, u32[]{:S(2)}) copy-start(bf16[128,256]{1,0:T(8,128)(2,1)} %pad.11.clone) | copy-start | bytes 196612
  63.5 9.8 %collective-permute-start.2 = (bf16[2,32,128]{2,1,0:T(8,128)(2,1)S(1)}, bf16[2,32,128]{2,1,0:T(8,128)(2,1)S(1)}, u32[]{:S(2)}, u32[]{:S(2)}) collective-permute-start(bf16[2,32,128]{2,1,0:T(8,128)(2,1)S(1)} %facing.1), channel_id=1, source_target_pairs={{1,2},{2,1},{5,6},{6,5},{9,10},{10,9},{13,14},{14,13},{17,18},{18,... | collective-permute-start | bytes 49160 | tf_op jit(solution)/shard_map/ppermute | solution.py:451
  65.4 8.2 %collective-permute-start.3 = (bf16[2,32,128]{2,1,0:T(8,128)(2,1)S(1)}, bf16[2,32,128]{2,1,0:T(8,128)(2,1)S(1)}, u32[]{:S(2)}, u32[]{:S(2)}) collective-permute-start(bf16[2,32,128]{2,1,0:T(8,128)(2,1)S(1)} %slice_select_fusion), channel_id=1, source_target_pairs={{0,1},{1,0},{2,3},{3,2},{4,5},{5,4},{6,7},{7,6},{8,9},{9,8},{10,11... | collective-permute-start | bytes 49160 | tf_op jit(solution)/shard_map/ppermute | solution.py:451
  73.7 14.3 %collective-permute-start.4 = (bf16[2,192,128]{2,1,0:T(8,128)(2,1)S(1)}, bf16[2,192,128]{2,1,0:T(8,128)(2,1)S(1)}, u32[]{:S(2)}, u32[]{:S(2)}) collective-permute-start(bf16[2,192,128]{2,1,0:T(8,128)(2,1)S(1)} %pad_maximum_fusion.2.own_ref), channel_id=1, source_target_pairs={{4,8},{5,9},{6,10},{7,11},{8,4},{9,5},{10,6},{11,7},{12,16},{13,17... | collective-permute-start | bytes 294920 | tf_op jit(solution)/shard_map/ppermute | solution.py:451
  83.4 7.7 %collective-permute-start.5 = (bf16[2,192,128]{2,1,0:T(8,128)(2,1)S(1)}, bf16[2,192,128]{2,1,0:T(8,128)(2,1)S(1)}, u32[]{:S(2)}, u32[]{:S(2)}) collective-permute-start(bf16[2,192,128]{2,1,0:T(8,128)(2,1)S(1)} %pad_maximum_fusion.2.own_ref), channel_id=1, source_target_pairs={{0,4},{1,5},{2,6},{3,7},{4,0},{5,1},{6,2},{7,3},{8,12},{9,13},{10,... | collective-permute-start | bytes 294920 | tf_op jit(solution)/shard_map/ppermute | solution.py:451

commit v7 on v6

--- a/solution.py
+++ b/solution.py
@@ -486,8 +486,11 @@
     even = s % 2 == 0
     img = image[0]
     top, bottom = img[0:3], img[1:4]
-    far = swap(jnp.where(even, top, bottom), far_partner, cams, slabs)
-    core = swap(jnp.where(even, bottom, top), core_partner, cams, slabs)
+    facing_far = jnp.where(even, top, bottom)
+    far = swap(facing_far, far_partner, cams, slabs)
+    later, _ = lax.optimization_barrier((img, facing_far))
+    facing_core = jnp.where(even, later[1:4], later[0:3])
+    core = swap(facing_core, core_partner, cams, slabs)
 
     pix = sample_pixel[0].T
     frac = jnp.transpose(sample_frac[0], (0, 2, 1))

time: 94.1 us -> 94.2 us (level)
  the two profiles are of different devices: /device:TPU:10 before, /device:TPU:27 now
where the time goes in v7:
time: 94.2 us; the launch traced here: 93.6 us
  starting transfers between devices  50.6 us (54%)
  waiting for transfers between devices  22.4 us (24%)
  Pallas kernels  11.3 us (12%)
  local copies, waits for them, and re-layouts  5.68 us (6%)
  other arithmetic  2.63 us (3%)
  between operations  0.99 us (1%)
    ppermute x6, starting transfers between devices, swap(): return lax.ppermute(x, AXES, pairs)  34.1 us
    all_to_all x1, starting transfers between devices, local(): lax.all_to_all(sent.reshape(128, 8, 128), AXES, 0, 0, tiled=True)  16.5 us
    all_to_all x1, waiting for transfers between devices, local(): lax.all_to_all(sent.reshape(128, 8, 128), AXES, 0, 0, tiled=True)  13.9 us
    ppermute x6, waiting for transfers between devices, swap(): return lax.ppermute(x, AXES, pairs)  8.56 us
    concatenate x7, local copies, waits for them, and re-layouts, banded(): rows.append(jnp.concatenate(blocks, axis=2))  5.05 us
    pallas_call x1, Pallas kernels, features(): pl.pallas_call(features_kernel, out_shape=jax.ShapeDtypeStruct((1024, 128...  3.13 us
    pallas_call x1, Pallas kernels, volume_convs(): pl.pallas_call(volume_kernel, out_shape=jax.ShapeDtypeStruct((256, 128),...  2.71 us
    pallas_call x1, Pallas kernels, prepare(): pl.pallas_call(prepare_kernel, out_shape=(jax.ShapeDtypeStruct((1792, 128...  2.37 us
  transfers between devices with their start and end apart: 7, of which 4 were waited for; matrix products, arithmetic and copies ran while one was open for 8% of the time, Pallas kernels for 5%

profile of v7, /device:TPU:27, one launch (start us, length us, event | category | flops | bytes accessed | tf_op | source)
XLA Modules:
  0.0 93.6 jit_solution(10210541275977002959)
XLA Ops:
  0.0 1.0 %select_bitcast_fusion = bf16[3,256,128]{2,1,0:T(8,128)(2,1)S(1)} fusion(bf16[1,4,256,128]{3,2,1,0:T(8,128)(2,1)} %param.10, pred[]{:T(512)S(6)} %eq.5), kind=kLoop, calls=%fused_computation.3 | loop fusion | flops 98304 | bytes 589825 | tf_op jit(solution)/shard_map/jit(_where)/select_n | solution.py:489
  1.0 16.0 %collective-permute-start = (bf16[3,256,128]{2,1,0:T(8,128)(2,1)S(1)}, bf16[3,256,128]{2,1,0:T(8,128)(2,1)S(1)}, u32[]{:S(2)}, u32[]{:S(2)}) collective-permute-start(bf16[3,256,128]{2,1,0:T(8,128)(2,1)S(1)} %select_bitcast_fusion), channel_id=1, source_target_pairs={{1,2},{2,1},{5,6},{6,5},{9,10},{10,9},{13,14},{14,13},{17,18},{18,... | collective-permute-start | bytes 589832 | tf_op jit(solution)/shard_map/ppermute | solution.py:451
  17.1 1.0 %slice_select_fusion = bf16[3,256,128]{2,1,0:T(8,128)(2,1)S(1)} fusion(bf16[4,256,128]{2,1,0:T(8,128)(2,1)} %bitcast.59, pred[]{:T(512)S(6)} %eq.5), kind=kLoop, calls=%fused_computation.2 | loop fusion | flops 98304 | bytes 589825 | tf_op jit(solution)/shard_map/jit(_where)/select_n | solution.py:492
  18.1 1.9 %collective-permute-start.1 = (bf16[3,256,128]{2,1,0:T(8,128)(2,1)S(1)}, bf16[3,256,128]{2,1,0:T(8,128)(2,1)S(1)}, u32[]{:S(2)}, u32[]{:S(2)}) collective-permute-start(bf16[3,256,128]{2,1,0:T(8,128)(2,1)S(1)} %slice_select_fusion), channel_id=1, source_target_pairs={{0,1},{1,0},{2,3},{3,2},{4,5},{5,4},{6,7},{7,6},{8,9},{9,8},{10,11... | collective-permute-start | bytes 589832 | tf_op jit(solution)/shard_map/ppermute | solution.py:451
  20.7 0.0 copy-start
  20.7 0.0 copy-start.1
  20.7 0.0 copy-start.2
  20.7 2.4 %prepare.1 = (f32[1792,128]{1,0:T(8,128)S(1)}, bf16[8,256,512]{2,1,0:T(8,128)(2,1)S(1)}, f32[8,8,512]{2,1,0:T(8,128)S(1)}) custom-call(f32[1]{0:T(128)S(6)} %copy.30.scale_ref, bf16[4,256,128]{2,1,0:T(8,128)(2,1)} %bitcast.60, bf16[3,384,128]{2,1,0:T(8,128)(2,1)} %bitcast.48, s32[32,128]{1,0:T(8,128)} %bitcast.64, f32[2,32,128]{2,1,0:T(8,128)} %bitcast.63), custom_call_target="tpu_custom_call" | custom-call | flops 10000000000 | bytes 4000000 | tf_op jit(solution)/shard_map/prepare/pallas_call | solution.py:81
  23.1 0.0 collective-permute-done.1.core_ref
  23.1 0.0 copy-done
  23.1 0.0 copy-done.1
  23.1 0.0 copy-done.2
  23.2 0.0 collective-permute-done.far_ref
  23.2 0.0 copy-start.9
  23.2 0.0 copy-start.10
  23.2 3.1 %features.1 = bf16[1024,128]{1,0:T(8,128)(2,1)} custom-call(s32[1]{0:T(128)} %bitcast.1.pos_ref, bf16[3,256,128]{2,1,0:T(8,128)(2,1)S(1)} %collective-permute-done.far_ref, bf16[3,256,128]{2,1,0:T(8,128)(2,1)S(1)} %collective-permute-done.1.core_ref, bf16[3,384,128]{2,1,0:T(8,128)(2,1)S(1)} %bitcast.50, bf16[3,384,128]{2,1,0:T(8,128)(2,1)S(1)} %bitcast.52, ...), custom_call_target="tpu_custom_call" | custom-call | tf_op jit(solution)/shard_map/features/pallas_call | solution.py:225
  26.3 16.5 %all-to-all-start = ((bf16[128,8,128]{2,1,0:T(8,128)(2,1)}), bf16[128,8,128]{2,1,0:T(8,128)(2,1)S(1)}, u32[]{:S(2)}, u32[]{:S(2)}) async-start(bf16[128,8,128]{2,1,0:T(8,128)(2,1)} %bitcast.11), calls=%async_computation | async-start | bytes 524288 | tf_op jit(solution)/shard_map/all_to_all | solution.py:510
  42.8 0.0 copy-done.9
  42.8 0.0 copy-done.10
  42.8 0.1 slice_bitcast_fusion.1
  42.9 0.2 concatenate.42
  43.1 0.8 concatenate.41
  43.9 0.0 copy-start.11
  43.9 0.9 concatenate.37
  44.8 0.8 concatenate.36
  45.6 0.8 concatenate.39
  46.5 0.8 concatenate.34
  47.3 0.0 copy-done.11
  47.3 0.1 copy.15
  47.4 0.2 reshape_squeeze.3.by_row_ref
  47.6 0.2 copy.16
  47.8 0.7 pad.11.clone
  48.5 0.4 slots.1.one_hot
  48.9 13.9 %all-to-all-done = bf16[128,8,128]{2,1,0:T(8,128)(2,1)S(1)} async-done(((bf16[128,8,128]{2,1,0:T(8,128)(2,1)}), bf16[128,8,128]{2,1,0:T(8,128)(2,1)S(1)}, u32[]{:S(2)}, u32[]{:S(2)}) %all-to-all-start) | async-done | bytes 262176 | tf_op jit(solution)/shard_map/all_to_all | solution.py:510
  62.8 0.0 copy-start.3
  62.8 0.0 copy-start.4
  62.8 0.0 copy-start.5
  62.8 0.0 copy-start.6
  62.8 0.0 copy-start.7
  62.8 0.0 copy-start.8
  62.8 0.8 facing.1
  63.6 6.2 %collective-permute-start.2 = (bf16[2,32,128]{2,1,0:T(8,128)(2,1)S(1)}, bf16[2,32,128]{2,1,0:T(8,128)(2,1)S(1)}, u32[]{:S(2)}, u32[]{:S(2)}) collective-permute-start(bf16[2,32,128]{2,1,0:T(8,128)(2,1)S(1)} %facing.1), channel_id=1, source_target_pairs={{1,2},{2,1},{5,6},{6,5},{9,10},{10,9},{13,14},{14,13},{17,18},{18,... | collective-permute-start | bytes 49160 | tf_op jit(solution)/shard_map/ppermute | solution.py:451
  69.8 1.2 %scatter.1 = bf16[2,128,128]{2,1,0:T(8,128)(2,1)S(1)} custom-call(bf16[1024,128]{1,0:T(8,128)(2,1)S(1)} %bitcast.54, s32[4,1024]{1,0:T(4,128)S(1)} %bitcast.56, s32[1024,4]{1,0:T(8,128)S(1)} %reshape_squeeze.3.by_row_ref), custom_call_target="tpu_custom_call" | custom-call | flops 300000000 | bytes 3000000 | tf_op jit(solution)/shard_map/scatter/pallas_call | solution.py:308
  71.1 1.9 %collective-permute-start.3 = (bf16[2,32,128]{2,1,0:T(8,128)(2,1)S(1)}, bf16[2,32,128]{2,1,0:T(8,128)(2,1)S(1)}, u32[]{:S(2)}, u32[]{:S(2)}) collective-permute-start(bf16[2,32,128]{2,1,0:T(8,128)(2,1)S(1)} %slice_select_fusion.1), channel_id=1, source_target_pairs={{0,1},{1,0},{2,3},{3,2},{4,5},{5,4},{6,7},{7,6},{8,9},{9,8},{10,11... | collective-permute-start | bytes 49160 | tf_op jit(solution)/shard_map/ppermute | solution.py:451
  73.0 0.0 copy-done.3
  73.0 0.0 copy-done.4
  73.0 0.0 copy-done.5
  73.0 0.0 copy-done.6
  73.1 0.0 copy-done.7
  73.1 0.0 copy-done.8
  73.1 0.4 pad_maximum_fusion.1
  73.5 3.9 %collective-permute-done.2 = bf16[2,32,128]{2,1,0:T(8,128)(2,1)S(1)} collective-permute-done((bf16[2,32,128]{2,1,0:T(8,128)(2,1)S(1)}, bf16[2,32,128]{2,1,0:T(8,128)(2,1)S(1)}, u32[]{:S(2)}, u32[]{:S(2)}) %collective-permute-start.2) | collective-permute-done | bytes 16416 | tf_op jit(solution)/shard_map/ppermute | solution.py:451
  77.4 0.0 collective-permute-done.3
  77.4 6.2 %collective-permute-start.4 = (bf16[2,192,128]{2,1,0:T(8,128)(2,1)S(1)}, bf16[2,192,128]{2,1,0:T(8,128)(2,1)S(1)}, u32[]{:S(2)}, u32[]{:S(2)}) collective-permute-start(bf16[2,192,128]{2,1,0:T(8,128)(2,1)S(1)} %pad_maximum_fusion.2.own_ref), channel_id=1, source_target_pairs={{4,8},{5,9},{6,10},{7,11},{8,4},{9,5},{10,6},{11,7},{12,16},{13,17... | collective-permute-start | bytes 294920 | tf_op jit(solution)/shard_map/ppermute | solution.py:451
  83.6 1.9 %collective-permute-start.5 = (bf16[2,192,128]{2,1,0:T(8,128)(2,1)S(1)}, bf16[2,192,128]{2,1,0:T(8,128)(2,1)S(1)}, u32[]{:S(2)}, u32[]{:S(2)}) collective-permute-start(bf16[2,192,128]{2,1,0:T(8,128)(2,1)S(1)} %pad_maximum_fusion.2.own_ref), channel_id=1, source_target_pairs={{0,4},{1,5},{2,6},{3,7},{4,0},{5,1},{6,2},{7,3},{8,12},{9,13},{10,... | collective-permute-start | bytes 294920 | tf_op jit(solution)/shard_map/ppermute | solution.py:451
  85.5 0.1 pad_add_fusion.pos_ref
  85.6 0.6 volume_start.1.part_ref
  86.2 4.5 %collective-permute-done.4.next_ref = bf16[2,192,128]{2,1,0:T(8,128)(2,1)S(1)} collective-permute-done((bf16[2,192,128]{2,1,0:T(8,128)(2,1)S(1)}, bf16[2,192,128]{2,1,0:T(8,128)(2,1)S(1)}, u32[]{:S(2)}, u32[]{:S(2)}) %collective-permute-start.4) | collective-permute-done | bytes 98336 | tf_op jit(solution)/shard_map/ppermute | solution.py:451
  90.7 0.2 collective-permute-done.5.near_ref
  90.9 2.7 %volume.1 = bf16[256,128]{1,0:T(8,128)(2,1)} custom-call(s32[2]{0:T(128)S(1)} %pad_add_fusion.pos_ref, bf16[2,192,128]{2,1,0:T(8,128)(2,1)S(1)} %pad_maximum_fusion.2.own_ref, bf16[2,192,128]{2,1,0:T(8,128)(2,1)S(1)} %collective-permute-done.4.next_ref, bf16[2,192,128]{2,1,0:T(8,128)(2,1)S(1)} %collective-permute-done.5.near_ref, ...), custom_call_target="tpu_custom_call" | custom-call | tf_op jit(solution)/shard_map/volume/pallas_call | solution.py:415
  (9 shorter events, 0.1 us)
Async XLA Ops:
  1.0 22.1 %collective-permute-start = (bf16[3,256,128]{2,1,0:T(8,128)(2,1)S(1)}, bf16[3,256,128]{2,1,0:T(8,128)(2,1)S(1)}, u32[]{:S(2)}, u32[]{:S(2)}) collective-permute-start(bf16[3,256,128]{2,1,0:T(8,128)(2,1)S(1)} %select_bitcast_fusion), channel_id=1, source_target_pairs={{1,2},{2,1},{5,6},{6,5},{9,10},{10,9},{13,14},{14,13},{17,18},{18,... | collective-permute-start | bytes 589832 | tf_op jit(solution)/shard_map/ppermute | solution.py:451
  18.1 5.0 %collective-permute-start.1 = (bf16[3,256,128]{2,1,0:T(8,128)(2,1)S(1)}, bf16[3,256,128]{2,1,0:T(8,128)(2,1)S(1)}, u32[]{:S(2)}, u32[]{:S(2)}) collective-permute-start(bf16[3,256,128]{2,1,0:T(8,128)(2,1)S(1)} %slice_select_fusion), channel_id=1, source_target_pairs={{0,1},{1,0},{2,3},{3,2},{4,5},{5,4},{6,7},{7,6},{8,9},{9,8},{10,11... | collective-permute-start | bytes 589832 | tf_op jit(solution)/shard_map/ppermute | solution.py:451
  20.7 2.4 %copy-start = (bf16[3,3,128,128]{3,2,1,0:T(8,128)(2,1)S(1)}, bf16[3,3,128,128]{3,2,1,0:T(8,128)(2,1)}, u32[]{:S(2)}) copy-start(bf16[3,3,128,128]{3,2,1,0:T(8,128)(2,1)} %param.11) | copy-start | bytes 884740
  20.7 2.4 %copy-start.1 = (bf16[3,3,128,128]{3,2,1,0:T(8,128)(2,1)S(1)}, bf16[3,3,128,128]{3,2,1,0:T(8,128)(2,1)}, u32[]{:S(2)}) copy-start(bf16[3,3,128,128]{3,2,1,0:T(8,128)(2,1)} %param.12) | copy-start | bytes 884740
  20.7 2.4 %copy-start.2 = (bf16[128,32]{0,1:T(8,128)(2,1)S(1)}, bf16[128,32]{0,1:T(8,128)(2,1)}, u32[]{:S(2)}) copy-start(bf16[128,32]{0,1:T(8,128)(2,1)} %param.13) | copy-start | bytes 24580
  23.2 19.6 %copy-start.9 = (bf16[27,32,32]{2,1,0:T(8,128)(2,1)S(1)}, bf16[27,32,32]{2,1,0:T(8,128)(2,1)}, u32[]{:S(2)}) copy-start(bf16[27,32,32]{2,1,0:T(8,128)(2,1)} %param.19) | copy-start | bytes 165892
  23.2 19.6 %copy-start.10 = (bf16[27,32,32]{2,1,0:T(8,128)(2,1)S(1)}, bf16[27,32,32]{2,1,0:T(8,128)(2,1)}, u32[]{:S(2)}) copy-start(bf16[27,32,32]{2,1,0:T(8,128)(2,1)} %param.18) | copy-start | bytes 165892
  26.3 36.4 %all-to-all-start = ((bf16[128,8,128]{2,1,0:T(8,128)(2,1)}), bf16[128,8,128]{2,1,0:T(8,128)(2,1)S(1)}, u32[]{:S(2)}, u32[]{:S(2)}) async-start(bf16[128,8,128]{2,1,0:T(8,128)(2,1)} %bitcast.11), calls=%async_computation | async-start | bytes 524288 | tf_op jit(solution)/shard_map/all_to_all | solution.py:510
  43.9 3.3 %copy-start.11 = (s32[1,128,32]{1,2,0:T(8,128)S(1)}, s32[1,128,32]{1,2,0:T(8,128)}, u32[]{:S(2)}) copy-start(s32[1,128,32]{1,2,0:T(8,128)} %param.17) | copy-start | bytes 49156
  62.8 10.3 %copy-start.3 = (bf16[9,32,256]{2,1,0:T(8,128)(2,1)S(1)}, bf16[9,32,256]{2,1,0:T(8,128)(2,1)}, u32[]{:S(2)}) copy-start(bf16[9,32,256]{2,1,0:T(8,128)(2,1)} %concatenate.41) | copy-start | bytes 442372
  62.8 10.3 %copy-start.4 = (bf16[9,32,256]{2,1,0:T(8,128)(2,1)S(1)}, bf16[9,32,256]{2,1,0:T(8,128)(2,1)}, u32[]{:S(2)}) copy-start(bf16[9,32,256]{2,1,0:T(8,128)(2,1)} %concatenate.37) | copy-start | bytes 442372
  62.8 10.3 %copy-start.5 = (bf16[9,32,256]{2,1,0:T(8,128)(2,1)S(1)}, bf16[9,32,256]{2,1,0:T(8,128)(2,1)}, u32[]{:S(2)}) copy-start(bf16[9,32,256]{2,1,0:T(8,128)(2,1)} %concatenate.36) | copy-start | bytes 442372
  62.8 10.3 %copy-start.6 = (bf16[9,32,256]{2,1,0:T(8,128)(2,1)S(1)}, bf16[9,32,256]{2,1,0:T(8,128)(2,1)}, u32[]{:S(2)}) copy-start(bf16[9,32,256]{2,1,0:T(8,128)(2,1)} %concatenate.39) | copy-start | bytes 442372
  62.8 10.3 %copy-start.7 = (bf16[9,32,256]{2,1,0:T(8,128)(2,1)S(1)}, bf16[9,32,256]{2,1,0:T(8,128)(2,1)}, u32[]{:S(2)}) copy-start(bf16[9,32,256]{2,1,0:T(8,128)(2,1)} %concatenate.34) | copy-start | bytes 442372
  62.8 10.3 %copy-start.8 = (bf16[128,256]{1,0:T(8,128)(2,1)S(1)}, bf16[128,256]{1,0:T(8,128)(2,1)}, u32[]{:S(2)}) copy-start(bf16[128,256]{1,0:T(8,128)(2,1)} %pad.11.clone) | copy-start | bytes 196612
  63.6 13.8 %collective-permute-start.2 = (bf16[2,32,128]{2,1,0:T(8,128)(2,1)S(1)}, bf16[2,32,128]{2,1,0:T(8,128)(2,1)S(1)}, u32[]{:S(2)}, u32[]{:S(2)}) collective-permute-start(bf16[2,32,128]{2,1,0:T(8,128)(2,1)S(1)} %facing.1), channel_id=1, source_target_pairs={{1,2},{2,1},{5,6},{6,5},{9,10},{10,9},{13,14},{14,13},{17,18},{18,... | collective-permute-start | bytes 49160 | tf_op jit(solution)/shard_map/ppermute | solution.py:451
  71.1 6.3 %collective-permute-start.3 = (bf16[2,32,128]{2,1,0:T(8,128)(2,1)S(1)}, bf16[2,32,128]{2,1,0:T(8,128)(2,1)S(1)}, u32[]{:S(2)}, u32[]{:S(2)}) collective-permute-start(bf16[2,32,128]{2,1,0:T(8,128)(2,1)S(1)} %slice_select_fusion.1), channel_id=1, source_target_pairs={{0,1},{1,0},{2,3},{3,2},{4,5},{5,4},{6,7},{7,6},{8,9},{9,8},{10,11... | collective-permute-start | bytes 49160 | tf_op jit(solution)/shard_map/ppermute | solution.py:451
  77.4 13.3 %collective-permute-start.4 = (bf16[2,192,128]{2,1,0:T(8,128)(2,1)S(1)}, bf16[2,192,128]{2,1,0:T(8,128)(2,1)S(1)}, u32[]{:S(2)}, u32[]{:S(2)}) collective-permute-start(bf16[2,192,128]{2,1,0:T(8,128)(2,1)S(1)} %pad_maximum_fusion.2.own_ref), channel_id=1, source_target_pairs={{4,8},{5,9},{6,10},{7,11},{8,4},{9,5},{10,6},{11,7},{12,16},{13,17... | collective-permute-start | bytes 294920 | tf_op jit(solution)/shard_map/ppermute | solution.py:451
  83.6 7.3 %collective-permute-start.5 = (bf16[2,192,128]{2,1,0:T(8,128)(2,1)S(1)}, bf16[2,192,128]{2,1,0:T(8,128)(2,1)S(1)}, u32[]{:S(2)}, u32[]{:S(2)}) collective-permute-start(bf16[2,192,128]{2,1,0:T(8,128)(2,1)S(1)} %pad_maximum_fusion.2.own_ref), channel_id=1, source_target_pairs={{0,4},{1,5},{2,6},{3,7},{4,0},{5,1},{6,2},{7,3},{8,12},{9,13},{10,... | collective-permute-start | bytes 294920 | tf_op jit(solution)/shard_map/ppermute | solution.py:451

commit v8 on v6

--- a/solution.py
+++ b/solution.py
@@ -109,7 +109,17 @@
     return rows
 
 
-def middle_kernel(pos_ref, core_ref, w1_ref, w2_ref, wr_ref, part_ref, inner, table, x1, x2, acc):
+def blended(table, first, weights, blend):
+    got = dot(table, weights)
+    total = got[0:32] * blend[first : first + 1]
+    for r in range(1, got.shape[0] // 32):
+        total = total + got[32 * r : 32 * r + 32] * blend[first + r : first + r + 1]
+    return total
+
+
+def middle_kernel(
+    pos_ref, core_ref, w1_ref, w2_ref, wr_ref, part_ref, weights, blends, inner, rest, x1, x2, acc
+):
     @pl.when(pos_ref[0] % 2 == 0)
     def _():
         for i in range(3):
@@ -130,17 +140,19 @@
         acc[...] = dot(x2[0:3].reshape(768, 384), w2_ref[0])
         acc[...] += dot(x2[1:4].reshape(768, 384), w2_ref[1])
         acc[...] += dot(x2[2:5].reshape(768, 384), w2_ref[2])
-        table[...] = jnp.concatenate(table_rows(acc, 0, 3, wr_ref[...]), axis=0).astype(BF16)
-
-
-def middle(slab, core, w1, w2, wr, part):
+        table = jnp.concatenate(table_rows(acc, 0, 3, wr_ref[...]), axis=0).astype(BF16)
+        for k in range(8):
+            rest[k] = blended(table, 2, weights[k], blends[k])
+
+
+def middle(slab, core, w1, w2, wr, part, weights, blends):
     return pl.pallas_call(
         middle_kernel,
         out_shape=(
             jax.ShapeDtypeStruct((2, 256, 384), BF16),
-            jax.ShapeDtypeStruct((96, 256), BF16),
+            jax.ShapeDtypeStruct((8, 32, 512), F32),
         ),
-        in_specs=[whole(pltpu.SMEM)] + [whole(pltpu.VMEM)] * 5,
+        in_specs=[whole(pltpu.SMEM)] + [whole(pltpu.VMEM)] * 7,
         out_specs=(whole(pltpu.VMEM),) * 2,
         scratch_shapes=[
             pltpu.VMEM((3, 256, 384), BF16),
@@ -150,12 +162,12 @@
         compiler_params=pltpu.CompilerParams(vmem_limit_bytes=24 * 2**20),
         cost_estimate=pl.CostEstimate(flops=1000000, bytes_accessed=10**3, transcendentals=0),
         name="middle",
-    )(slab, core, w1, w2, wr, part)
+    )(slab, core, w1, w2, wr, part, weights, blends)
 
 
 def features_kernel(
     pos_ref, far_ref, core_ref, w1_ref, w2_ref, wr_ref, part_ref, weights, blends,
-    inner, ready, out_ref, x1, x2, acc, table, packed,
+    inner, rest, out_ref, x1, x2, acc, packed,
 ):
     slab = pos_ref[0]
     not_first = jnp.where(slab == 0, 0.0, 1.0)
@@ -166,6 +178,10 @@
             put_columns(x1, i, above[1 + i].astype(F32))
         head = dot(x1[0:2].reshape(512, 384), w1_ref[0])
         return head[0:256] + dot(x1[1], w1_ref[1]), head[256:512]
+
+    def pack(k, total):
+        block = jnp.concatenate([total[:, 128 * i : 128 * i + 128] for i in range(4)], axis=0)
+        packed[pl.ds(k, 128, stride=8), :] = block.T
 
     @pl.when(slab % 2 == 0)
     def _():
@@ -176,8 +192,9 @@
         acc[0:512] = dot(x2[0:2].reshape(512, 384), w2_ref[0])
         acc[0:512] += dot(x2[1:3].reshape(512, 384), w2_ref[1])
         acc[0:512] += dot(x2[2:4].reshape(512, 384), w2_ref[2])
-        table[0:64] = jnp.concatenate(table_rows(acc, 0, 2, wr_ref[...]), axis=0).astype(BF16)
-        table[64:160] = ready[...]
+        table = jnp.concatenate(table_rows(acc, 0, 2, wr_ref[...]), axis=0).astype(BF16)
+        for k in range(8):
+            pack(k, blended(table, 0, weights[k], blends[k]) + rest[k])
 
     @pl.when(slab % 2 == 1)
     def _():
@@ -208,20 +225,14 @@
         acc[...] += dot(x2[2:7].reshape(1280, 384), w2_ref[2])
         rows = table_rows(acc, 0, 5, wr_ref[...])
         rows[4] = rows[4] * not_last
-        table[...] = jnp.concatenate(rows, axis=0).astype(BF16)
-
-    for k in range(8):
-        got = dot(table[...], weights[k])
-        blend = blends[k]
-        total = got[0:32] * blend[0:1]
-        for r in range(1, 5):
-            total = total + got[32 * r : 32 * r + 32] * blend[r : r + 1]
-        block = jnp.concatenate([total[:, 128 * i : 128 * i + 128] for i in range(4)], axis=0)
-        packed[pl.ds(k, 128, stride=8), :] = block.T
+        table = jnp.concatenate(rows, axis=0).astype(BF16)
+        for k in range(8):
+            pack(k, blended(table, 0, weights[k], blends[k]))
+
     out_ref[...] = packed[...].astype(BF16)
 
 
-def features(slab, far, core, w1, w2, wr, part, weights, blends, inner, ready):
+def features(slab, far, core, w1, w2, wr, part, weights, blends, inner, rest):
     return pl.pallas_call(
         features_kernel,
         out_shape=jax.ShapeDtypeStruct((1024, 128), BF16),
@@ -231,12 +242,11 @@
             pltpu.VMEM((5, 256, 384), BF16),
             pltpu.VMEM((7, 256, 384), BF16),
             pltpu.VMEM((1280, 128), F32),
-            pltpu.VMEM((160, 256), BF16),
             pltpu.VMEM((1024, 128), F32),
         ],
         compiler_params=pltpu.CompilerParams(vmem_limit_bytes=32 * 2**20),
         name="features",
-    )(slab, far, core, w1, w2, wr, part, weights, blends, inner, ready)
+    )(slab, far, core, w1, w2, wr, part, weights, blends, inner, rest)
 
 
 def slots_kernel(pos_ref, by_lane_ref, one_hot):
@@ -500,9 +510,9 @@
     slab_pos = s.astype(jnp.int32).reshape(1)
 
     part, weights, blends = prepare(cam_weight, img, w1, pix, frac)
-    inner, ready = middle(slab_pos, core, w1, w2, w_reduce.T, part)
+    inner, rest = middle(slab_pos, core, w1, w2, w_reduce.T, part, weights, blends)
     sent = features(
-        slab_pos, far, core, w1, w2, w_reduce.T, part, weights, blends, inner, ready
+        slab_pos, far, core, w1, w2, w_reduce.T, part, weights, blends, inner, rest
     )
     got = lax.all_to_all(sent.reshape(128, 8, 128), AXES, 0, 0, tiled=True).reshape(1024, 128)
     facing = facing_rows(got, slots(slab_pos, by_lane))

time: 94.1 us -> 94.1 us (level)
  the two profiles are of different devices: /device:TPU:10 before, /device:TPU:27 now
where the time goes in v8:
time: 94.1 us; the launch traced here: 93.6 us
  starting transfers between devices  51.9 us (55%)
  waiting for transfers between devices  22.2 us (24%)
  Pallas kernels  11.2 us (12%)
  local copies, waits for them, and re-layouts  5.7 us (6%)
  other arithmetic  1.59 us (2%)
  between operations  0.98 us (1%)
    ppermute x6, starting transfers between devices, swap(): return lax.ppermute(x, AXES, pairs)  34.4 us
    all_to_all x1, starting transfers between devices, local(): lax.all_to_all(sent.reshape(128, 8, 128), AXES, 0, 0, tiled=True)  17.5 us
    all_to_all x1, waiting for transfers between devices, local(): lax.all_to_all(sent.reshape(128, 8, 128), AXES, 0, 0, tiled=True)  13.9 us
    ppermute x6, waiting for transfers between devices, swap(): return lax.ppermute(x, AXES, pairs)  8.35 us
    concatenate x7, local copies, waits for them, and re-layouts, banded(): rows.append(jnp.concatenate(blocks, axis=2))  5.07 us
    pallas_call x1, Pallas kernels, features(): pl.pallas_call(features_kernel, out_shape=jax.ShapeDtypeStruct((1024, 128...  3.06 us
    pallas_call x1, Pallas kernels, volume_convs(): pl.pallas_call(volume_kernel, out_shape=jax.ShapeDtypeStruct((256, 128),...  2.72 us
    pallas_call x1, Pallas kernels, prepare(): pl.pallas_call(prepare_kernel, out_shape=(jax.ShapeDtypeStruct((1792, 128...  2.35 us
  transfers between devices with their start and end apart: 7, of which 3 were waited for; matrix products, arithmetic and copies ran while one was open for 7% of the time, Pallas kernels for 5%

profile of v8, /device:TPU:27, one launch (start us, length us, event | category | flops | bytes accessed | tf_op | source)
XLA Modules:
  0.0 93.6 jit_solution(16877441139335910111)
XLA Ops:
  0.0 1.1 %select_bitcast_fusion = (bf16[3,256,128]{2,1,0:T(8,128)(2,1)S(1)}, bf16[3,256,128]{2,1,0:T(8,128)(2,1)S(1)}) fusion(pred[]{:T(512)S(6)} %eq.5, bf16[1,4,256,128]{3,2,1,0:T(8,128)(2,1)} %param.10), kind=kLoop, calls=%fused_computation.2 | loop fusion | flops 196608 | bytes 786433 | tf_op jit(solution)/shard_map/jit(_where)/select_n | solution.py:500
  1.1 16.0 %collective-permute-start = (bf16[3,256,128]{2,1,0:T(8,128)(2,1)S(1)}, bf16[3,256,128]{2,1,0:T(8,128)(2,1)S(1)}, u32[]{:S(2)}, u32[]{:S(2)}) collective-permute-start(bf16[3,256,128]{2,1,0:T(8,128)(2,1)S(1)} %get-tuple-element.20), channel_id=1, source_target_pairs={{1,2},{2,1},{5,6},{6,5},{9,10},{10,9},{13,14},{14,13},{17,18},{18,... | collective-permute-start | bytes 589832 | tf_op jit(solution)/shard_map/ppermute | solution.py:461
  17.1 1.9 %collective-permute-start.1 = (bf16[3,256,128]{2,1,0:T(8,128)(2,1)S(1)}, bf16[3,256,128]{2,1,0:T(8,128)(2,1)S(1)}, u32[]{:S(2)}, u32[]{:S(2)}) collective-permute-start(bf16[3,256,128]{2,1,0:T(8,128)(2,1)S(1)} %get-tuple-element.19), channel_id=1, source_target_pairs={{0,1},{1,0},{2,3},{3,2},{4,5},{5,4},{6,7},{7,6},{8,9},{9,8},{10,11... | collective-permute-start | bytes 589832 | tf_op jit(solution)/shard_map/ppermute | solution.py:461
  19.6 0.0 copy-start
  19.7 0.0 copy-start.1
  19.7 0.0 copy-start.2
  19.7 2.4 %prepare.1 = (f32[1792,128]{1,0:T(8,128)S(1)}, bf16[8,256,512]{2,1,0:T(8,128)(2,1)S(1)}, f32[8,8,512]{2,1,0:T(8,128)S(1)}) custom-call(f32[1]{0:T(128)S(6)} %copy.30.scale_ref, bf16[4,256,128]{2,1,0:T(8,128)(2,1)} %bitcast.61, bf16[3,384,128]{2,1,0:T(8,128)(2,1)} %bitcast.50, s32[32,128]{1,0:T(8,128)} %bitcast.65, f32[2,32,128]{2,1,0:T(8,128)} %bitcast.64), custom_call_target="tpu_custom_call" | custom-call | flops 10000000000 | bytes 4000000 | tf_op jit(solution)/shard_map/prepare/pallas_call | solution.py:81
  22.0 0.0 collective-permute-done.1.core_ref
  22.0 0.0 copy-done
  22.1 0.0 copy-done.1
  22.1 0.0 copy-done.2
  22.1 0.0 collective-permute-done.far_ref
  22.1 0.0 copy-start.9
  22.1 0.0 copy-start.10
  22.1 3.1 %features.1 = bf16[1024,128]{1,0:T(8,128)(2,1)} custom-call(s32[1]{0:T(128)} %bitcast.1.pos_ref, bf16[3,256,128]{2,1,0:T(8,128)(2,1)S(1)} %collective-permute-done.far_ref, bf16[3,256,128]{2,1,0:T(8,128)(2,1)S(1)} %collective-permute-done.1.core_ref, bf16[3,384,128]{2,1,0:T(8,128)(2,1)S(1)} %bitcast.52, bf16[3,384,128]{2,1,0:T(8,128)(2,1)S(1)} %bitcast.54, ...), custom_call_target="tpu_custom_call" | custom-call | tf_op jit(solution)/shard_map/features/pallas_call | solution.py:236
  25.2 17.5 %all-to-all-start = ((bf16[128,8,128]{2,1,0:T(8,128)(2,1)}), bf16[128,8,128]{2,1,0:T(8,128)(2,1)S(1)}, u32[]{:S(2)}, u32[]{:S(2)}) async-start(bf16[128,8,128]{2,1,0:T(8,128)(2,1)} %bitcast.12), calls=%async_computation | async-start | bytes 524288 | tf_op jit(solution)/shard_map/all_to_all | solution.py:517
  42.7 0.0 copy-done.9
  42.7 0.0 copy-done.10
  42.7 0.1 slice_bitcast_fusion.1
  42.8 0.2 concatenate.42
  43.0 0.8 concatenate.41
  43.8 0.0 copy-start.11
  43.8 0.9 concatenate.37
  44.7 0.8 concatenate.36
  45.5 0.8 concatenate.39
  46.4 0.8 concatenate.34
  47.2 0.0 copy-done.11
  47.2 0.1 copy.15
  47.3 0.2 reshape_squeeze.3.by_row_ref
  47.5 0.2 copy.16
  47.7 0.7 pad.11.clone
  48.4 0.4 slots.1.one_hot
  48.8 13.9 %all-to-all-done = bf16[128,8,128]{2,1,0:T(8,128)(2,1)S(1)} async-done(((bf16[128,8,128]{2,1,0:T(8,128)(2,1)}), bf16[128,8,128]{2,1,0:T(8,128)(2,1)S(1)}, u32[]{:S(2)}, u32[]{:S(2)}) %all-to-all-start) | async-done | bytes 262176 | tf_op jit(solution)/shard_map/all_to_all | solution.py:517
  62.7 0.0 copy-start.3
  62.7 0.0 copy-start.4
  62.7 0.0 copy-start.5
  62.7 0.0 copy-start.6
  62.7 0.0 copy-start.7
  62.7 0.0 copy-start.8
  62.7 0.8 facing.1
  63.5 6.4 %collective-permute-start.2 = (bf16[2,32,128]{2,1,0:T(8,128)(2,1)S(1)}, bf16[2,32,128]{2,1,0:T(8,128)(2,1)S(1)}, u32[]{:S(2)}, u32[]{:S(2)}) collective-permute-start(bf16[2,32,128]{2,1,0:T(8,128)(2,1)S(1)} %facing.1), channel_id=1, source_target_pairs={{1,2},{2,1},{5,6},{6,5},{9,10},{10,9},{13,14},{14,13},{17,18},{18,... | collective-permute-start | bytes 49160 | tf_op jit(solution)/shard_map/ppermute | solution.py:461
  69.9 1.2 %scatter.1 = bf16[2,128,128]{2,1,0:T(8,128)(2,1)S(1)} custom-call(bf16[1024,128]{1,0:T(8,128)(2,1)S(1)} %bitcast.56, s32[4,1024]{1,0:T(4,128)S(1)} %bitcast.58, s32[1024,4]{1,0:T(8,128)S(1)} %reshape_squeeze.3.by_row_ref), custom_call_target="tpu_custom_call" | custom-call | flops 300000000 | bytes 3000000 | tf_op jit(solution)/shard_map/scatter/pallas_call | solution.py:318
  71.2 1.9 %collective-permute-start.3 = (bf16[2,32,128]{2,1,0:T(8,128)(2,1)S(1)}, bf16[2,32,128]{2,1,0:T(8,128)(2,1)S(1)}, u32[]{:S(2)}, u32[]{:S(2)}) collective-permute-start(bf16[2,32,128]{2,1,0:T(8,128)(2,1)S(1)} %slice_select_fusion), channel_id=1, source_target_pairs={{0,1},{1,0},{2,3},{3,2},{4,5},{5,4},{6,7},{7,6},{8,9},{9,8},{10,11... | collective-permute-start | bytes 49160 | tf_op jit(solution)/shard_map/ppermute | solution.py:461
  73.1 0.0 copy-done.3
  73.1 0.0 copy-done.4
  73.1 0.0 copy-done.5
  73.1 0.0 copy-done.6
  73.1 0.0 copy-done.7
  73.1 0.0 copy-done.8
  73.2 0.4 pad_maximum_fusion.1
  73.6 3.7 %collective-permute-done.2 = bf16[2,32,128]{2,1,0:T(8,128)(2,1)S(1)} collective-permute-done((bf16[2,32,128]{2,1,0:T(8,128)(2,1)S(1)}, bf16[2,32,128]{2,1,0:T(8,128)(2,1)S(1)}, u32[]{:S(2)}, u32[]{:S(2)}) %collective-permute-start.2) | collective-permute-done | bytes 16416 | tf_op jit(solution)/shard_map/ppermute | solution.py:461
  77.3 0.0 collective-permute-done.3
  77.3 6.3 %collective-permute-start.4 = (bf16[2,192,128]{2,1,0:T(8,128)(2,1)S(1)}, bf16[2,192,128]{2,1,0:T(8,128)(2,1)S(1)}, u32[]{:S(2)}, u32[]{:S(2)}) collective-permute-start(bf16[2,192,128]{2,1,0:T(8,128)(2,1)S(1)} %pad_maximum_fusion.2.own_ref), channel_id=1, source_target_pairs={{4,8},{5,9},{6,10},{7,11},{8,4},{9,5},{10,6},{11,7},{12,16},{13,17... | collective-permute-start | bytes 294920 | tf_op jit(solution)/shard_map/ppermute | solution.py:461
  83.7 1.9 %collective-permute-start.5 = (bf16[2,192,128]{2,1,0:T(8,128)(2,1)S(1)}, bf16[2,192,128]{2,1,0:T(8,128)(2,1)S(1)}, u32[]{:S(2)}, u32[]{:S(2)}) collective-permute-start(bf16[2,192,128]{2,1,0:T(8,128)(2,1)S(1)} %pad_maximum_fusion.2.own_ref), channel_id=1, source_target_pairs={{0,4},{1,5},{2,6},{3,7},{4,0},{5,1},{6,2},{7,3},{8,12},{9,13},{10,... | collective-permute-start | bytes 294920 | tf_op jit(solution)/shard_map/ppermute | solution.py:461
  85.6 0.1 pad_add_fusion.pos_ref
  85.7 0.6 volume_start.1.part_ref
  86.3 4.6 %collective-permute-done.4.next_ref = bf16[2,192,128]{2,1,0:T(8,128)(2,1)S(1)} collective-permute-done((bf16[2,192,128]{2,1,0:T(8,128)(2,1)S(1)}, bf16[2,192,128]{2,1,0:T(8,128)(2,1)S(1)}, u32[]{:S(2)}, u32[]{:S(2)}) %collective-permute-start.4) | collective-permute-done | bytes 98336 | tf_op jit(solution)/shard_map/ppermute | solution.py:461
  90.9 0.0 collective-permute-done.5.near_ref
  90.9 2.7 %volume.1 = bf16[256,128]{1,0:T(8,128)(2,1)} custom-call(s32[2]{0:T(128)S(1)} %pad_add_fusion.pos_ref, bf16[2,192,128]{2,1,0:T(8,128)(2,1)S(1)} %pad_maximum_fusion.2.own_ref, bf16[2,192,128]{2,1,0:T(8,128)(2,1)S(1)} %collective-permute-done.4.next_ref, bf16[2,192,128]{2,1,0:T(8,128)(2,1)S(1)} %collective-permute-done.5.near_ref, ...), custom_call_target="tpu_custom_call" | custom-call | tf_op jit(solution)/shard_map/volume/pallas_call | solution.py:425
  (9 shorter events, 0.1 us)
Async XLA Ops:
  1.1 21.0 %collective-permute-start = (bf16[3,256,128]{2,1,0:T(8,128)(2,1)S(1)}, bf16[3,256,128]{2,1,0:T(8,128)(2,1)S(1)}, u32[]{:S(2)}, u32[]{:S(2)}) collective-permute-start(bf16[3,256,128]{2,1,0:T(8,128)(2,1)S(1)} %get-tuple-element.20), channel_id=1, source_target_pairs={{1,2},{2,1},{5,6},{6,5},{9,10},{10,9},{13,14},{14,13},{17,18},{18,... | collective-permute-start | bytes 589832 | tf_op jit(solution)/shard_map/ppermute | solution.py:461
  17.1 5.0 %collective-permute-start.1 = (bf16[3,256,128]{2,1,0:T(8,128)(2,1)S(1)}, bf16[3,256,128]{2,1,0:T(8,128)(2,1)S(1)}, u32[]{:S(2)}, u32[]{:S(2)}) collective-permute-start(bf16[3,256,128]{2,1,0:T(8,128)(2,1)S(1)} %get-tuple-element.19), channel_id=1, source_target_pairs={{0,1},{1,0},{2,3},{3,2},{4,5},{5,4},{6,7},{7,6},{8,9},{9,8},{10,11... | collective-permute-start | bytes 589832 | tf_op jit(solution)/shard_map/ppermute | solution.py:461
  19.6 2.4 %copy-start = (bf16[3,3,128,128]{3,2,1,0:T(8,128)(2,1)S(1)}, bf16[3,3,128,128]{3,2,1,0:T(8,128)(2,1)}, u32[]{:S(2)}) copy-start(bf16[3,3,128,128]{3,2,1,0:T(8,128)(2,1)} %param.11) | copy-start | bytes 884740
  19.7 2.4 %copy-start.1 = (bf16[3,3,128,128]{3,2,1,0:T(8,128)(2,1)S(1)}, bf16[3,3,128,128]{3,2,1,0:T(8,128)(2,1)}, u32[]{:S(2)}) copy-start(bf16[3,3,128,128]{3,2,1,0:T(8,128)(2,1)} %param.12) | copy-start | bytes 884740
  19.7 2.4 %copy-start.2 = (bf16[128,32]{0,1:T(8,128)(2,1)S(1)}, bf16[128,32]{0,1:T(8,128)(2,1)}, u32[]{:S(2)}) copy-start(bf16[128,32]{0,1:T(8,128)(2,1)} %param.13) | copy-start | bytes 24580
  22.1 20.6 %copy-start.9 = (bf16[27,32,32]{2,1,0:T(8,128)(2,1)S(1)}, bf16[27,32,32]{2,1,0:T(8,128)(2,1)}, u32[]{:S(2)}) copy-start(bf16[27,32,32]{2,1,0:T(8,128)(2,1)} %param.19) | copy-start | bytes 165892
  22.1 20.6 %copy-start.10 = (bf16[27,32,32]{2,1,0:T(8,128)(2,1)S(1)}, bf16[27,32,32]{2,1,0:T(8,128)(2,1)}, u32[]{:S(2)}) copy-start(bf16[27,32,32]{2,1,0:T(8,128)(2,1)} %param.18) | copy-start | bytes 165892
  25.2 37.5 %all-to-all-start = ((bf16[128,8,128]{2,1,0:T(8,128)(2,1)}), bf16[128,8,128]{2,1,0:T(8,128)(2,1)S(1)}, u32[]{:S(2)}, u32[]{:S(2)}) async-start(bf16[128,8,128]{2,1,0:T(8,128)(2,1)} %bitcast.12), calls=%async_computation | async-start | bytes 524288 | tf_op jit(solution)/shard_map/all_to_all | solution.py:517
  43.8 3.4 %copy-start.11 = (s32[1,128,32]{1,2,0:T(8,128)S(1)}, s32[1,128,32]{1,2,0:T(8,128)}, u32[]{:S(2)}) copy-start(s32[1,128,32]{1,2,0:T(8,128)} %param.17) | copy-start | bytes 49156
  62.7 10.4 %copy-start.3 = (bf16[9,32,256]{2,1,0:T(8,128)(2,1)S(1)}, bf16[9,32,256]{2,1,0:T(8,128)(2,1)}, u32[]{:S(2)}) copy-start(bf16[9,32,256]{2,1,0:T(8,128)(2,1)} %concatenate.41) | copy-start | bytes 442372
  62.7 10.4 %copy-start.4 = (bf16[9,32,256]{2,1,0:T(8,128)(2,1)S(1)}, bf16[9,32,256]{2,1,0:T(8,128)(2,1)}, u32[]{:S(2)}) copy-start(bf16[9,32,256]{2,1,0:T(8,128)(2,1)} %concatenate.37) | copy-start | bytes 442372
  62.7 10.5 %copy-start.5 = (bf16[9,32,256]{2,1,0:T(8,128)(2,1)S(1)}, bf16[9,32,256]{2,1,0:T(8,128)(2,1)}, u32[]{:S(2)}) copy-start(bf16[9,32,256]{2,1,0:T(8,128)(2,1)} %concatenate.36) | copy-start | bytes 442372
  62.7 10.5 %copy-start.6 = (bf16[9,32,256]{2,1,0:T(8,128)(2,1)S(1)}, bf16[9,32,256]{2,1,0:T(8,128)(2,1)}, u32[]{:S(2)}) copy-start(bf16[9,32,256]{2,1,0:T(8,128)(2,1)} %concatenate.39) | copy-start | bytes 442372
  62.7 10.5 %copy-start.7 = (bf16[9,32,256]{2,1,0:T(8,128)(2,1)S(1)}, bf16[9,32,256]{2,1,0:T(8,128)(2,1)}, u32[]{:S(2)}) copy-start(bf16[9,32,256]{2,1,0:T(8,128)(2,1)} %concatenate.34) | copy-start | bytes 442372
  62.7 10.5 %copy-start.8 = (bf16[128,256]{1,0:T(8,128)(2,1)S(1)}, bf16[128,256]{1,0:T(8,128)(2,1)}, u32[]{:S(2)}) copy-start(bf16[128,256]{1,0:T(8,128)(2,1)} %pad.11.clone) | copy-start | bytes 196612
  63.5 13.8 %collective-permute-start.2 = (bf16[2,32,128]{2,1,0:T(8,128)(2,1)S(1)}, bf16[2,32,128]{2,1,0:T(8,128)(2,1)S(1)}, u32[]{:S(2)}, u32[]{:S(2)}) collective-permute-start(bf16[2,32,128]{2,1,0:T(8,128)(2,1)S(1)} %facing.1), channel_id=1, source_target_pairs={{1,2},{2,1},{5,6},{6,5},{9,10},{10,9},{13,14},{14,13},{17,18},{18,... | collective-permute-start | bytes 49160 | tf_op jit(solution)/shard_map/ppermute | solution.py:461
  71.2 6.1 %collective-permute-start.3 = (bf16[2,32,128]{2,1,0:T(8,128)(2,1)S(1)}, bf16[2,32,128]{2,1,0:T(8,128)(2,1)S(1)}, u32[]{:S(2)}, u32[]{:S(2)}) collective-permute-start(bf16[2,32,128]{2,1,0:T(8,128)(2,1)S(1)} %slice_select_fusion), channel_id=1, source_target_pairs={{0,1},{1,0},{2,3},{3,2},{4,5},{5,4},{6,7},{7,6},{8,9},{9,8},{10,11... | collective-permute-start | bytes 49160 | tf_op jit(solution)/shard_map/ppermute | solution.py:461
  77.3 13.5 %collective-permute-start.4 = (bf16[2,192,128]{2,1,0:T(8,128)(2,1)S(1)}, bf16[2,192,128]{2,1,0:T(8,128)(2,1)S(1)}, u32[]{:S(2)}, u32[]{:S(2)}) collective-permute-start(bf16[2,192,128]{2,1,0:T(8,128)(2,1)S(1)} %pad_maximum_fusion.2.own_ref), channel_id=1, source_target_pairs={{4,8},{5,9},{6,10},{7,11},{8,4},{9,5},{10,6},{11,7},{12,16},{13,17... | collective-permute-start | bytes 294920 | tf_op jit(solution)/shard_map/ppermute | solution.py:461
  83.7 7.3 %collective-permute-start.5 = (bf16[2,192,128]{2,1,0:T(8,128)(2,1)S(1)}, bf16[2,192,128]{2,1,0:T(8,128)(2,1)S(1)}, u32[]{:S(2)}, u32[]{:S(2)}) collective-permute-start(bf16[2,192,128]{2,1,0:T(8,128)(2,1)S(1)} %pad_maximum_fusion.2.own_ref), channel_id=1, source_target_pairs={{0,4},{1,5},{2,6},{3,7},{4,0},{5,1},{6,2},{7,3},{8,12},{9,13},{10,... | collective-permute-start | bytes 294920 | tf_op jit(solution)/shard_map/ppermute | solution.py:461
